TPU v7x, 32 devices: a whole 2x2x4 slice. The times are simulated.
32 devices in a mesh: group: 2 (over y), tm: 4 (over x, core), row: 4 (over z).
Axes of the slice: x: 2, y: 2, z: 4, core: 2. Of those that a mesh axis runs over, the one named last changes fastest.
Arguments:
- traces: bfloat16 [4096, 1024], P('row', ('group', 'tm')), parts along dimension 1, may hold values from -6 to 6
- weights: bfloat16 [4, 4096, 4096], P(None, 'row'), may hold values from -0.09375 to 0.09375
- pattern: int32 [4, 32, 32], replicated, may hold values 0 or 1
- cluster: int32 [4096], replicated, may hold values from 0 to 31
- element_damping_rate: float32 [4096], replicated, may hold values from 0 to 0.034, as said below
- local_step_length: float32 [512], P('tm'), may hold values from 0.4 to 1.9, as said below
- housing_keep_share: float32 [512], P('tm'), may hold values from 0.2 to 1, as said below
- admittance: float32 [4096], replicated, may hold values from 0.5 to 2
Outputs:
- adjoint_state: float32 [4096, 1024], P('row', ('group', 'tm')), parts along dimension 1
- pressure: bfloat16 [4096, 1024], P('row', ('group', 'tm')), parts along dimension 1
There are 2 independent parts, one for each index of `group`. A program takes and returns all parts, laid end to end along the dimension named above; an argument that names none is the same for every part. Nothing has to cross between parts.
Inputs may be any that keep to these rules, and one draw needn't show every extreme that they name: `element_damping_rate`: damping rates, positive. `local_step_length`: positive step lengths. `housing_keep_share`: kept shares, positive.
All inputs are finite; a program needn't handle non-finite values.
Results may differ from a plain program's by a relative error of at most 0.012.
Values may be sent and summed in bfloat16 or wider, within the bound.
No kernel may reach another device: no remote copies, remote signals or barrier semaphores. Data moves between devices by JAX's collectives and lax.ppermute only.
A program may use at most 192 MiB of HBM per device.

v0:
```python
import jax
import jax.numpy as jnp
from jax import lax
from jax.sharding import PartitionSpec as P


def carried_in(array, axis, join, neutral):
    count = lax.axis_size(axis)
    place = lax.axis_index(axis)
    ahead = count - 1 - place
    gathered = jax.tree.map(
        lambda a, kind: lax.all_gather(a.astype(kind), axis),
        array,
        jax.tree.map(lambda a: jnp.bfloat16 if a.dtype == jnp.float32 else a.dtype, array),
    )
    state = jax.tree.map(lambda a, e: jnp.zeros_like(a) + jnp.asarray(e, a.dtype), array, neutral)

    def one(hop, state):
        source = count - 1 - hop
        return join(
            state,
            jax.tree.map(
                lambda a, own: lax.dynamic_index_in_dim(a, source, 0, False).astype(own.dtype),
                gathered,
                array,
            ),
        )

    return lax.fori_loop(0, ahead, one, state)


def from_behind(array, axis, by):
    count = lax.axis_size(axis)
    pairs = [(i, i + by) for i in range(count) if 0 <= i + by < count]
    return lax.ppermute(array, axis, pairs)


def lag_kernels(weights, pattern, cluster, first_row):
    local_rows = weights.shape[1]
    own_labels = lax.dynamic_slice_in_dim(cluster, first_row, local_rows, 0)
    labels = jnp.arange(pattern.shape[1], dtype=jnp.int32)
    row_onehot = (own_labels[:, None] == labels[None, :]).astype(jnp.bfloat16)
    column_onehot = (labels[:, None] == cluster[None, :]).astype(jnp.bfloat16)
    kernels = []
    for lag_index in range(weights.shape[0]):
        picked = jnp.dot(
            row_onehot, pattern[lag_index].astype(jnp.bfloat16), preferred_element_type=jnp.float32
        )
        table = jnp.dot(
            picked.astype(jnp.bfloat16), column_onehot, preferred_element_type=jnp.float32
        )
        kernels.append(weights[lag_index] * table.astype(jnp.bfloat16))
    return kernels


def correlate(kernels, extended):
    length = extended.shape[1] - len(kernels) + 1
    running = None
    for lag_index in range(len(kernels)):
        columns = kernels[lag_index]
        product_term = lax.dot_general(
            columns,
            extended[:, lag_index : lag_index + length],
            (((0,), (0,)), ((), ())),
            preferred_element_type=jnp.float32,
        )
        running = product_term if running is None else running + product_term
    return running


def reconstruct(kernels, extended, running):
    number_of_lags = len(kernels)
    length = extended.shape[1] - number_of_lags + 1
    col_count = extended.shape[0]
    for lag_index in range(number_of_lags):
        columns = lax.slice_in_dim(kernels[lag_index], 0, col_count, axis=1)
        offset = number_of_lags - 1 - lag_index
        running = running + jnp.dot(
            columns, extended[:, offset : offset + length], preferred_element_type=jnp.float32
        )
    return running


def chain_step(earlier, later):
    return (later[0] * earlier[0], later[1] + later[0] * earlier[1])


def block_recurrence(keep_fraction, inflow):
    elements = keep_fraction.shape[0]
    length = keep_fraction.shape[1]
    span = 8
    keep_rows = keep_fraction.T.reshape(length // span, span, elements)
    inflow_rows = inflow.T.reshape(length // span, span, elements)

    def advance(carry, pieces):
        kept_now, state_now = carry
        keep_block, inflow_block = pieces
        kept_list = [None] * span
        state_list = [None] * span
        for inner in range(span - 1, -1, -1):
            state_now = keep_block[inner] * state_now + inflow_block[inner]
            kept_now = keep_block[inner] * kept_now
            kept_list[inner] = kept_now
            state_list[inner] = state_now
        return ((kept_now, state_now), (jnp.stack(kept_list, 0), jnp.stack(state_list, 0)))

    start = (jnp.ones((elements,), jnp.float32), jnp.zeros((elements,), jnp.float32))
    _, outputs = lax.scan(advance, start, (keep_rows, inflow_rows), reverse=True)
    retained = outputs[0].reshape(length, elements).T
    partial_state = outputs[1].reshape(length, elements).T
    return (retained, partial_state)


def forward_step(
    adjoint_total_sum,
    element_damping_rate,
    local_step_length,
    housing_keep_share,
    admittance,
    number_of_lags,
):
    length = adjoint_total_sum.shape[1]
    distribute_rows = element_damping_rate[:, None] * local_step_length[None, :]
    keep_fraction = jnp.exp(-distribute_rows) * housing_keep_share[None, :]
    inflow = jnp.sqrt(-jnp.expm1(-2.0 * distribute_rows)) * adjoint_total_sum
    retained, partial_state = block_recurrence(keep_fraction, inflow)
    neutral = (jnp.ones_like(retained[:, 0]), jnp.zeros_like(partial_state[:, 0]))
    incoming = carried_in((retained[:, 0], partial_state[:, 0]), "tm", chain_step, neutral)
    adj_state = partial_state + retained * incoming[1][:, None]
    driving = (admittance[:, None] * adj_state).astype(jnp.bfloat16)
    leading = from_behind(driving[:, length - number_of_lags + 1 :], "tm", 1)
    return (adj_state, jnp.concatenate([leading, driving], 1))


def local(
    traces,
    weights,
    pattern,
    cluster,
    element_damping_rate,
    local_step_length,
    housing_keep_share,
    admittance,
):
    local_rows = traces.shape[0]
    length = traces.shape[1]
    number_of_lags = weights.shape[0]
    first_row = lax.axis_index("row") * local_rows
    kernels = lag_kernels(weights, pattern, cluster, first_row)
    trailing = from_behind(traces[:, : number_of_lags - 1], "tm", -1)
    extended = jnp.concatenate([traces, trailing], 1)
    empty = jnp.zeros((local_rows, length), jnp.float32)
    adjoint_total_sum = lax.psum(correlate(kernels, extended).astype(jnp.bfloat16), "row").astype(
        jnp.float32
    )
    adj_state, driving = forward_step(
        adjoint_total_sum,
        element_damping_rate,
        local_step_length,
        housing_keep_share,
        admittance,
        number_of_lags,
    )
    pressure = reconstruct(kernels, driving, empty)
    adj_state = lax.dynamic_slice_in_dim(adj_state, first_row, local_rows, 0)
    return (adj_state, pressure.astype(jnp.bfloat16))


def solution(mesh):
    placed = (P("row", ("group", "tm")), P(None, "row", None), P(), P(), P(), P("tm"), P("tm"), P())
    return jax.shard_map(
        local,
        mesh=mesh,
        in_specs=placed,
        out_specs=(P("row", ("group", "tm")), P("row", ("group", "tm"))),
        check_vma=False,
    )
```

profile of v0, /device:TPU:0, one launch (start us, length us, event | category | flops | bytes accessed | tf_op | source)
XLA Modules:
  0.0 234.8 jit_solution(9270569396340060062)
XLA Ops:
  7.2 1.3 collective-permute-start
  8.5 0.8 convert.14
  9.4 0.7 dynamic_slice.40
  10.1 8.1 %bitcast_multiply_fusion.3 = bf16[1024,4096]{1,0:T(8,128)(2,1)} fusion(bf16[4,1024,4096]{2,1,0:T(8,128)(2,1)} %param.13, s32[4096]{0:T(1024)} %param.15, s32[1024]{0:T(1024)S(1)} %dynamic_slice.40, bf16[4,32,32]{2,1,0:T(8,128)(2,1)S(1)} %convert.14), kind=kOutput, calls=%fused_computation.34 | convolution fusion | flops 291700736 | bytes 16805888 | tf_op jit(solution)/shard_map/dot_general | solution.py:49
  18.1 7.2 %bitcast_multiply_fusion.2 = bf16[1024,4096]{1,0:T(8,128)(2,1)} fusion(bf16[4,1024,4096]{2,1,0:T(8,128)(2,1)} %param.13, s32[4096]{0:T(1024)S(1)} %copy-done.2, s32[1024]{0:T(1024)S(1)} %dynamic_slice.40, bf16[4,32,32]{2,1,0:T(8,128)(2,1)S(1)} %convert.14), kind=kOutput, calls=%fused_computation.33 | convolution fusion | flops 291700736 | bytes 16805888 | tf_op jit(solution)/shard_map/dot_general | solution.py:49
  25.3 7.1 %bitcast_multiply_fusion = bf16[1024,4096]{1,0:T(8,128)(2,1)} fusion(bf16[4,1024,4096]{2,1,0:T(8,128)(2,1)} %param.13, s32[4096]{0:T(1024)S(1)} %copy-done.2, s32[1024]{0:T(1024)S(1)} %dynamic_slice.40, bf16[4,32,32]{2,1,0:T(8,128)(2,1)S(1)} %convert.14), kind=kOutput, calls=%fused_computation.31 | convolution fusion | flops 291700736 | bytes 16805888 | tf_op jit(solution)/shard_map/dot_general | solution.py:49
  32.4 7.2 %bitcast_multiply_fusion.1 = bf16[1024,4096]{1,0:T(8,128)(2,1)} fusion(bf16[4,1024,4096]{2,1,0:T(8,128)(2,1)} %param.13, s32[4096]{0:T(1024)S(1)} %copy-done.2, s32[1024]{0:T(1024)S(1)} %dynamic_slice.40, bf16[4,32,32]{2,1,0:T(8,128)(2,1)S(1)} %convert.14), kind=kOutput, calls=%fused_computation.32 | convolution fusion | flops 291700736 | bytes 16805888 | tf_op jit(solution)/shard_map/dot_general | solution.py:49
  39.6 6.0 %fusion.42 = f32[4096,128]{1,0:T(8,128)S(1)} fusion(bf16[1024,4096]{1,0:T(8,128)(2,1)} %bitcast_multiply_fusion.3, bf16[1024,128]{1,0:T(8,128)(2,1)S(1)} %copy-done.1), kind=kOutput, calls=%fused_computation.94 | convolution fusion | flops 1073741824 | bytes 10747904 | tf_op jit(solution)/shard_map/dot_general | solution.py:61
  45.8 2.6 %fusion.20 = f32[4096,128]{1,0:T(8,128)S(1)} fusion(bf16[1024,4096]{1,0:T(8,128)(2,1)S(1)} %copy-done, bf16[1024,131]{1,0:T(8,128)(2,1)S(1)} %constant_dynamic-update-slice_fusion), kind=kOutput, calls=%fused_computation.72 | convolution fusion | flops 1073741824 | bytes 10747904 | tf_op jit(solution)/shard_map/dot_general | solution.py:61
  48.4 2.5 %convolution_add_fusion.1 = f32[4096,128]{1,0:T(8,128)S(1)} fusion(f32[4096,128]{1,0:T(8,128)S(1)} %fusion.42, bf16[1024,4096]{1,0:T(8,128)(2,1)S(1)} %bitcast.168, bf16[1024,131]{1,0:T(8,128)(2,1)S(1)} %constant_dynamic-update-slice_fusion), kind=kOutput, calls=%fused_computation.37 | convolution fusion | flops 1074266112 | bytes 12845056 | tf_op jit(solution)/shard_map/dot_general | solution.py:61
  51.0 3.6 %fusion.2 = bf16[4096,128]{1,0:T(8,128)(2,1)} fusion(f32[4096,128]{1,0:T(8,128)S(1)} %fusion.20, f32[4096,128]{1,0:T(8,128)S(1)} %convolution_add_fusion.1, bf16[1024,4096]{1,0:T(8,128)(2,1)S(1)} %bitcast.170, bf16[1024,131]{1,0:T(8,128)(2,1)S(1)} %constant_dynamic-update-slice_fusion), kind=kOutput, calls=%fused_computation.38 | convolution fusion | flops 1075314688 | bytes 13893632 | tf_op jit(solution)/shard_map/dot_general | solution.py:61
  54.8 1.6 exponential_multiply_fusion
  56.4 53.6 %all-reduce.2.cloned.1.call-done = bf16[4096,128]{1,0:T(8,128)(2,1)} async-done(((bf16[4096,128]{1,0:T(8,128)(2,1)}), bf16[4096,128]{1,0:T(8,128)(2,1)}) %all-reduce.2.cloned.1.call-update) | async-done | bytes 1048592 | tf_op jit(solution)/shard_map/psum | solution.py:153
  110.0 2.6 %multiply_bitcast_fusion = f32[128,4096]{0,1:T(8,128)S(1)} fusion(bf16[4096,128]{1,0:T(8,128)(2,1)} %all-reduce.2.cloned.1.call-done, f32[128]{0:T(128)S(1)} %copy-done.5, f32[4096]{0:T(1024)S(1)} %copy-done.3), kind=kLoop, calls=%fused_computation.44 | loop fusion | flops 2621440 | bytes 3162624 | tf_op jit(solution)/shard_map/transpose | solution.py:93
  112.6 1.9 copy.13
  114.7 1.5 broadcast.27.clone
  116.2 72.6 %while.36 = (s32[]{:T(128)}, f32[4096]{0:T(1024)S(1)}, f32[4096]{0:T(1024)S(1)}, f32[16,8,4096]{2,1,0:T(8,128)S(1)}, f32[16,8,4096]{2,1,0:T(8,128)}, /*index=5*/...) while((s32[]{:T(128)}, f32[4096]{0:T(1024)S(1)}, ...), condition=%wide.region_2.3_spmd.clone, body=%wide.region_1.2_spmd.clone.sunk | while | flops 106507 | bytes 2130251 | solution.py:108
  116.2 1.6 constant_dynamic-slice_fusion.18
  117.8 1.9 constant_dynamic-slice_fusion.19
  120.2 0.7 bitcast_dynamic-update-slice_fusion.3
  120.9 1.6 constant_dynamic-slice_fusion.18
  122.5 1.6 constant_dynamic-slice_fusion.19
  125.3 1.6 constant_dynamic-slice_fusion.18
  126.9 1.6 constant_dynamic-slice_fusion.19
  129.7 1.8 constant_dynamic-slice_fusion.18
  131.6 1.9 constant_dynamic-slice_fusion.19
  134.0 0.7 bitcast_dynamic-update-slice_fusion.3
  134.6 1.6 constant_dynamic-slice_fusion.18
  136.2 1.6 constant_dynamic-slice_fusion.19
  139.0 1.6 constant_dynamic-slice_fusion.18
  140.6 1.7 constant_dynamic-slice_fusion.19
  143.4 1.6 constant_dynamic-slice_fusion.18
  145.0 1.6 constant_dynamic-slice_fusion.19
  147.8 1.6 constant_dynamic-slice_fusion.18
  149.4 1.6 constant_dynamic-slice_fusion.19
  151.6 0.7 bitcast_dynamic-update-slice_fusion.3
  152.2 1.9 constant_dynamic-slice_fusion.18
  154.1 1.6 constant_dynamic-slice_fusion.19
  156.9 1.6 constant_dynamic-slice_fusion.18
  158.5 1.9 constant_dynamic-slice_fusion.19
  161.5 1.6 constant_dynamic-slice_fusion.18
  163.1 1.6 constant_dynamic-slice_fusion.19
  165.9 1.8 constant_dynamic-slice_fusion.18
  167.7 1.6 constant_dynamic-slice_fusion.19
  169.8 0.7 bitcast_dynamic-update-slice_fusion.3
  170.5 1.6 constant_dynamic-slice_fusion.18
  172.1 1.9 constant_dynamic-slice_fusion.19
  174.5 0.7 bitcast_dynamic-update-slice_fusion.3
  175.2 1.6 constant_dynamic-slice_fusion.18
  176.8 1.6 constant_dynamic-slice_fusion.19
  179.6 1.8 constant_dynamic-slice_fusion.18
  181.4 1.6 constant_dynamic-slice_fusion.19
  184.2 1.6 constant_dynamic-slice_fusion.18
  185.8 1.9 constant_dynamic-slice_fusion.19
  188.9 1.7 fusion.10
  190.6 5.2 %all-gather = bf16[16384,1]{0,1:T(2,128)(2,1)S(1)} all-gather(bf16[4096,1]{0,1:T(2,128)(2,1)S(1)} %slice.269), channel_id=2, replica_groups=mesh['group'=2,'tm'=4,'row'=4] {'tm'}, dimensions={0}, use_global_device_ids=true | all-gather | bytes 40960 | tf_op jit(solution)/shard_map/all_gather | solution.py:12
  196.2 5.2 %all-gather.1 = bf16[16384,1]{0,1:T(2,128)(2,1)S(1)} all-gather(bf16[4096,1]{0,1:T(2,128)(2,1)S(1)} %slice.270), channel_id=3, replica_groups=mesh['group'=2,'tm'=4,'row'=4] {'tm'}, dimensions={0}, use_global_device_ids=true | all-gather | bytes 40960 | tf_op jit(solution)/shard_map/all_gather | solution.py:12
  201.9 1.9 fusion.19
  203.9 5.7 %fusion.18 = f32[1024,128]{1,0:T(8,128)S(1)} fusion(bf16[1024,4096]{1,0:T(8,128)(2,1)} %bitcast_multiply_fusion.3, f32[128,4096]{1,0:T(8,128)S(1)} %get-tuple-element.305, f32[4096]{0:T(1024)S(1)} %copy-done.4), kind=kOutput, calls=%fused_computation.70 | convolution fusion | flops 1074790400 | bytes 11026432 | tf_op jit(solution)/shard_map/dot_general | solution.py:78
  209.7 2.2 collective-permute-start.1
  211.9 1.0 copy.14
  212.9 5.9 %fusion.12 = f32[1024,128]{1,0:T(8,128)S(1)} fusion(bf16[1024,4096]{1,0:T(8,128)(2,1)} %bitcast_multiply_fusion, bf16[4096,128]{0,1:T(8,128)(2,1)S(1)} %get-tuple-element.304, bf16[4096,3]{0,1:T(4,128)(2,1)S(1)} %collective-permute-done.1), kind=kOutput, calls=%fused_computation.61 | convolution fusion | flops 1075838976 | bytes 9986048 | tf_op jit(solution)/shard_map/dot_general | solution.py:78
  218.8 6.0 %convolution_add_fusion.3 = f32[1024,128]{1,0:T(8,128)S(1)} fusion(f32[1024,128]{1,0:T(8,128)S(1)} %fusion.18, bf16[1024,4096]{1,0:T(8,128)(2,1)} %bitcast_multiply_fusion.2, bf16[4096,3]{0,1:T(4,128)(2,1)S(1)} %collective-permute-done.1, bf16[4096,128]{0,1:T(8,128)(2,1)S(1)} %get-tuple-element.304), kind=kOutput, calls=%fused_computation.50 | convolution fusion | flops 1075970048 | bytes 10510336 | tf_op jit(solution)/shard_map/dot_general | solution.py:78
  224.8 3.1 %fusion.5 = bf16[1024,128]{1,0:T(8,128)(2,1)} fusion(f32[1024,128]{1,0:T(8,128)S(1)} %fusion.12, f32[1024,128]{1,0:T(8,128)S(1)} %convolution_add_fusion.3, bf16[1024,4096]{1,0:T(8,128)(2,1)S(1)} %bitcast.172, bf16[4096,3]{0,1:T(4,128)(2,1)S(1)} %collective-permute-done.1, bf16[4096,128]{0,1:T(8,128)(2,1)S(1)} %get-tuple-element.304), kind=kOutput, calls=%fused_computation.51 | convolution fusion | flops 1076232192 | bytes 10772480 | tf_op jit(solution)/shard_map/dot_general | solution.py:78
  (116 shorter events, 16.2 us)
Async XLA Ops:
  7.2 102.9 %all-reduce.2.cloned.1.call-start = ((), (), s32[]{:S(2)}) async-start(), calls=%async_computation | async-start | bytes 2097152 | tf_op jit(solution)/shard_map/psum | solution.py:153
  7.2 38.4 %collective-permute-start = (bf16[1024,3]{1,0:T(8,128)(2,1)}, bf16[1024,3]{1,0:T(8,128)(2,1)S(1)}, u32[]{:S(2)}, u32[]{:S(2)}) collective-permute-start(bf16[1024,3]{1,0:T(8,128)(2,1)} %bitcast.208), channel_id=1, source_target_pairs={{4,0},{8,4},{12,8},{5,1},{9,5},{13,9},{6,2},{10,6},{14,10},{7,3},{... | collective-permute-start | bytes 18440 | tf_op jit(solution)/shard_map/ppermute | solution.py:35
  10.1 8.1 %copy-start.2 = (s32[4096]{0:T(1024)S(1)}, s32[4096]{0:T(1024)}, u32[]{:S(2)}) copy-start(s32[4096]{0:T(1024)} %param.15) | copy-start | bytes 49156
  32.4 7.2 %copy-start.1 = (bf16[1024,128]{1,0:T(8,128)(2,1)S(1)}, bf16[1024,128]{1,0:T(8,128)(2,1)}, u32[]{:S(2)}) copy-start(bf16[1024,128]{1,0:T(8,128)(2,1)} %param.12) | copy-start | bytes 786436
  39.6 6.1 %copy-start = (bf16[1024,4096]{1,0:T(8,128)(2,1)S(1)}, bf16[1024,4096]{1,0:T(8,128)(2,1)}, u32[]{:S(2)}) copy-start(bf16[1024,4096]{1,0:T(8,128)(2,1)} %bitcast_multiply_fusion) | copy-start | bytes 25165828
  39.6 8.7 %slice-start = ((s8[8388608]{0:T(1024)(128)(4,1)}), s8[4194304]{0:T(1024)(128)(4,1)S(1)}, s32[]{:S(2)}) async-start(s8[8388608]{0:T(1024)(128)(4,1)} %bitcast.167), calls=%async_computation.1 | async-start | bytes 8388608
  45.6 2.7 %slice-start.1 = ((s8[8388608]{0:T(1024)(128)(4,1)}), s8[4194304]{0:T(1024)(128)(4,1)S(1)}, s32[]{:S(2)}) async-start(s8[8388608]{0:T(1024)(128)(4,1)} %bitcast.167), calls=%async_computation.2 | async-start | bytes 8388608
  45.7 5.2 %slice-start.2 = ((s8[8388608]{0:T(1024)(128)(4,1)}), s8[4194304]{0:T(1024)(128)(4,1)S(1)}, s32[]{:S(2)}) async-start(s8[8388608]{0:T(1024)(128)(4,1)} %bitcast.169), calls=%async_computation.3 | async-start | bytes 8388608
  48.4 2.6 %slice-start.3 = ((s8[8388608]{0:T(1024)(128)(4,1)}), s8[4194304]{0:T(1024)(128)(4,1)S(1)}, s32[]{:S(2)}) async-start(s8[8388608]{0:T(1024)(128)(4,1)} %bitcast.169), calls=%async_computation.4 | async-start | bytes 8388608
  50.9 3.6 %copy-start.5 = (f32[128]{0:T(128)S(1)}, f32[128]{0:T(128)}, u32[]{:S(2)}) copy-start(f32[128]{0:T(128)} %param.17) | copy-start | bytes 1540
  51.0 3.7 %copy-start.6 = (f32[128]{0:T(128)S(1)}, f32[128]{0:T(128)}, u32[]{:S(2)}) copy-start(f32[128]{0:T(128)} %param.18) | copy-start | bytes 1540
  51.0 3.8 %copy-start.3 = (f32[4096]{0:T(1024)S(1)}, f32[4096]{0:T(1024)}, u32[]{:S(2)}) copy-start(f32[4096]{0:T(1024)} %param.16) | copy-start | bytes 49156
  196.1 5.9 %copy-start.4 = (f32[4096]{0:T(1024)S(1)}, f32[4096]{0:T(1024)}, u32[]{:S(2)}) copy-start(f32[4096]{0:T(1024)} %param.19) | copy-start | bytes 49156
  209.7 3.2 %collective-permute-start.1 = (bf16[4096,3]{0,1:T(4,128)(2,1)S(1)}, bf16[4096,3]{0,1:T(4,128)(2,1)S(1)}, u32[]{:S(2)}, u32[]{:S(2)}) collective-permute-start(bf16[4096,3]{0,1:T(4,128)(2,1)S(1)} %slice.271), channel_id=1, source_target_pairs={{0,4},{4,8},{8,12},{1,5},{5,9},{9,13},{2,6},{6,10},{10,14},{3,7},{... | collective-permute-start | bytes 73736 | tf_op jit(solution)/shard_map/ppermute | solution.py:35
  212.9 11.9 %slice-start.4 = ((s8[8388608]{0:T(1024)(128)(4,1)}), s8[4194304]{0:T(1024)(128)(4,1)S(1)}, s32[]{:S(2)}) async-start(s8[8388608]{0:T(1024)(128)(4,1)} %bitcast.171), calls=%async_computation.5 | async-start | bytes 8388608
  218.8 6.0 %slice-start.5 = ((s8[8388608]{0:T(1024)(128)(4,1)}), s8[4194304]{0:T(1024)(128)(4,1)S(1)}, s32[]{:S(2)}) async-start(s8[8388608]{0:T(1024)(128)(4,1)} %bitcast.171), calls=%async_computation.6 | async-start | bytes 8388608
Sparse Core Ops, SparseCore 0:
  54.7 55.2 all-reduce.1
where the time goes:
time: 237 us; the launch traced here: 235 us
  local copies, waits for them, and re-layouts  77 us (32%)
  matrix products  64.9 us (27%)
  waiting for transfers between devices  53.6 us (23%)
  between operations  14.4 us (6%)
  blocking collectives  10.5 us (4%)
  other arithmetic  10.3 us (4%)
  starting transfers between devices  3.49 us (1%)
    psum x1, waiting for transfers between devices, local(): lax.psum(correlate(kernels, extended).astype(jnp.bfloat16), 'row')  53.6 us
    dot_general x4, matrix products, lag_kernels(): jnp.dot(picked.astype(jnp.bfloat16), column_onehot, preferred_element_typ...  29.6 us
    slice x16, local copies, waits for them, and re-layouts, advance(): kept_now = keep_block[inner] * kept_now  27.4 us
    slice x16, local copies, waits for them, and re-layouts, advance(): state_now = keep_block[inner] * state_now + inflow_block[inner]  26.7 us
    dot_general x4, matrix products, reconstruct(): jnp.dot(columns, extended[:, offset:offset + length], preferred_element_t...  20.7 us
    dot_general x4, matrix products, correlate(): lax.dot_general(columns, extended[:, lag_index:lag_index + length], (((0,...  14.6 us
    dynamic_update_slice x16, local copies, waits for them, and re-layouts, block_recurrence(): lax.scan(advance, start, (keep_rows, inflow_rows), reverse=True)  10.7 us
    all_gather x2, blocking collectives, carried_in(): lax.all_gather(a.astype(kind), axis)  10.5 us
  transfers between devices with their start and end apart: 3, of which 1 were waited for; matrix products, arithmetic and copies ran while one was open for 17% of the time, Pallas kernels for 0%

commit v1 on v0

v1 whole, which is shorter than its diff:
```python
import functools

import jax
import jax.numpy as jnp
from jax import lax
from jax.experimental import pallas as pl
from jax.experimental.pallas import tpu as pltpu
from jax.sharding import PartitionSpec as P

HALO = 16
CHUNKS = 2
VMEM_BYTES = 56 << 20


def carried_in(array, axis, join, neutral):
    count = lax.axis_size(axis)
    place = lax.axis_index(axis)
    ahead = count - 1 - place
    gathered = jax.tree.map(
        lambda a, kind: lax.all_gather(a.astype(kind), axis),
        array,
        jax.tree.map(lambda a: jnp.bfloat16 if a.dtype == jnp.float32 else a.dtype, array),
    )
    state = jax.tree.map(lambda a, e: jnp.zeros_like(a) + jnp.asarray(e, a.dtype), array, neutral)

    def one(hop, state):
        source = count - 1 - hop
        return join(
            state,
            jax.tree.map(
                lambda a, own: lax.dynamic_index_in_dim(a, source, 0, False).astype(own.dtype),
                gathered,
                array,
            ),
        )

    return lax.fori_loop(0, ahead, one, state)


def from_behind(array, axis, by):
    count = lax.axis_size(axis)
    pairs = [(i, i + by) for i in range(count) if 0 <= i + by < count]
    return lax.ppermute(array, axis, pairs)


def lag_kernels(weights, pattern, cluster, first_row):
    local_rows = weights.shape[1]
    own_labels = lax.dynamic_slice_in_dim(cluster, first_row, local_rows, 0)
    labels = jnp.arange(pattern.shape[1], dtype=jnp.int32)
    row_onehot = (own_labels[:, None] == labels[None, :]).astype(jnp.bfloat16)
    column_onehot = (labels[:, None] == cluster[None, :]).astype(jnp.bfloat16)
    kernels = []
    for lag_index in range(weights.shape[0]):
        picked = jnp.dot(
            row_onehot, pattern[lag_index].astype(jnp.bfloat16), preferred_element_type=jnp.float32
        )
        table = jnp.dot(
            picked.astype(jnp.bfloat16), column_onehot, preferred_element_type=jnp.float32
        )
        kernels.append(weights[lag_index] * table.astype(jnp.bfloat16))
    return kernels


def correlate(kernels, extended):
    length = extended.shape[1] - len(kernels) + 1
    running = None
    for lag_index in range(len(kernels)):
        product_term = lax.dot_general(
            kernels[lag_index],
            extended[:, lag_index : lag_index + length],
            (((0,), (0,)), ((), ())),
            preferred_element_type=jnp.float32,
        )
        running = product_term if running is None else running + product_term
    return running


def reconstruct(kernels, extended):
    number_of_lags = len(kernels)
    length = extended.shape[1] - number_of_lags + 1
    running = None
    for lag_index in range(number_of_lags):
        offset = number_of_lags - 1 - lag_index
        product_term = jnp.dot(
            kernels[lag_index],
            extended[:, offset : offset + length],
            preferred_element_type=jnp.float32,
        )
        running = product_term if running is None else running + product_term
    return running


def chain_step(earlier, later):
    return (later[0] * earlier[0], later[1] + later[0] * earlier[1])


def block_recurrence(keep_fraction, inflow):
    def advance(carry, pieces):
        kept_now, state_now = carry
        keep, more = pieces
        state_now = keep * state_now + more
        kept_now = keep * kept_now
        return ((kept_now, state_now), (kept_now, state_now))

    elements = keep_fraction.shape[0]
    start = (jnp.ones((elements,), jnp.float32), jnp.zeros((elements,), jnp.float32))
    _, outputs = lax.scan(advance, start, (keep_fraction.T, inflow.T), reverse=True)
    return (outputs[0].T, outputs[1].T)


def general(
    traces,
    weights,
    pattern,
    cluster,
    element_damping_rate,
    local_step_length,
    housing_keep_share,
    admittance,
):
    local_rows = traces.shape[0]
    length = traces.shape[1]
    number_of_lags = weights.shape[0]
    first_row = lax.axis_index("row") * local_rows
    kernels = lag_kernels(weights, pattern, cluster, first_row)
    trailing = from_behind(traces[:, : number_of_lags - 1], "tm", -1)
    extended = jnp.concatenate([traces, trailing], 1)
    adjoint_sum = lax.psum(correlate(kernels, extended).astype(jnp.bfloat16), "row").astype(
        jnp.float32
    )
    spent = element_damping_rate[:, None] * local_step_length[None, :]
    keep_fraction = jnp.exp(-spent) * housing_keep_share[None, :]
    inflow = jnp.sqrt(-jnp.expm1(-2.0 * spent)) * adjoint_sum
    retained, partial_state = block_recurrence(keep_fraction, inflow)
    neutral = (jnp.ones_like(retained[:, 0]), jnp.zeros_like(partial_state[:, 0]))
    incoming = carried_in((retained[:, 0], partial_state[:, 0]), "tm", chain_step, neutral)
    state = partial_state + retained * incoming[1][:, None]
    driving = (admittance[:, None] * state).astype(jnp.bfloat16)
    leading = from_behind(driving[:, length - number_of_lags + 1 :], "tm", 1)
    pressure = reconstruct(kernels, jnp.concatenate([leading, driving], 1))
    state = lax.dynamic_slice_in_dim(state, first_row, local_rows, 0)
    return (state, pressure.astype(jnp.bfloat16))


def masked(weight, words, bit):
    return jnp.where((words & bit) != 0, weight, jnp.zeros_like(weight))


def correlate_kernel(
    place, traces, partner, ahead, behind, words, bit, weight, o0, o1, o2, o3, steps, lagged, columns
):
    slot = pl.program_id(0)
    lags, rows, _ = weight.shape
    length = traces.shape[1]
    window = lagged.shape[1]
    half = place[1]

    @pl.when(slot == 0)
    def _():
        first = pl.multiple_of(HALO + half * length, HALO)
        second = pl.multiple_of(HALO + (1 - half) * length, HALO)
        steps[0:HALO, :] = ahead[:, 0:rows]
        steps[window : window + HALO, :] = behind[:, 0:rows]
        steps[pl.ds(first, length), :] = traces[...].astype(jnp.float32).T
        steps[pl.ds(second, length), :] = partner[...].astype(jnp.float32).T
        for lag in range(lags):
            lagged[lag] = steps[lag : lag + window, :].astype(jnp.bfloat16)
        columns[...] = words[...].T

    total = None
    for lag in range(lags):
        kernel = masked(weight[lag], columns[:, lag : lag + 1], bit[...])
        term = jnp.dot(lagged[lag], kernel, preferred_element_type=jnp.float32)
        total = term if total is None else total + term
    total = total.astype(jnp.bfloat16)
    for index, out in enumerate((o0, o1, o2, o3)):

        @pl.when(slot == index)
        def _(out=out):
            out[...] = total


def one_less_exp(y):
    series = jnp.ones_like(y)
    for k in range(9, 1, -1):
        series = 1.0 - series * y * (1.0 / k)
    return jnp.where(y < 0.5, y * series, 1.0 - jnp.exp(-y))


def recurrence_kernel(place, own, direct, paired, rate, aux, partial, first):
    window, unit = own.shape
    columns = aux[...].T
    spent = columns[0:window, 0:1] * rate[...]
    total = (
        own[...].astype(jnp.float32)
        + direct[...].astype(jnp.float32)
        + paired[...].astype(jnp.float32)
    )
    kept = jnp.exp(-spent) * columns[0:window, 1:2]
    state = jnp.sqrt(one_less_exp(2.0 * spent)) * total
    index = lax.broadcasted_iota(jnp.int32, (window, unit), 0) & 7
    for shift in (1, 2, 4):
        inside = index < 8 - shift
        later_state = pltpu.roll(state, window - shift, 0)
        later_kept = pltpu.roll(kept, window - shift, 0)
        state = jnp.where(inside, state + kept * later_state, state)
        kept = jnp.where(inside, kept * later_kept, kept)
    carry = jnp.zeros((1, unit), jnp.float32)
    for group in range(window // 8 - 1, -1, -1):
        rows = slice(group * 8, group * 8 + 8)
        block = state[rows] + kept[rows] * carry
        partial[rows, :] = block
        carry = block[0:1]
        if group * 8 == HALO:
            first[...] = jnp.broadcast_to(carry, first.shape)


def finish_kernel(place, partial, incoming, rate, admittance, aux, drive, mine, theirs, states):
    window, unit = partial.shape
    length = mine.shape[1]
    half = place[1]
    columns = aux[...].T
    reach = jnp.exp(-(columns[0:window, 2:3] * rate[...])) * columns[0:window, 3:4]
    state = partial[...] + reach * incoming[0:1, :]
    drive[...] = (admittance[...] * state).astype(jnp.bfloat16)
    states[...] = state
    first = pl.multiple_of(HALO + half * length, HALO)
    second = pl.multiple_of(HALO + (1 - half) * length, HALO)
    mine[...] = states[pl.ds(first, length), :].T
    theirs[...] = states[pl.ds(second, length), :].T


def reconstruct_kernel(last, place, d0, d1, d2, d3, words, bit, weight, *refs):
    if last:
        before, keep, send, total, steps, lagged, columns = refs
    else:
        keep, steps, lagged, columns = refs
        before, total = None, keep
    slot = pl.program_id(0)
    lags, rows, unit = weight.shape
    width = total.shape[1]
    window = d0.shape[0]

    @pl.when(slot == 0)
    def _():
        columns[...] = words[...].T
        total[...] = jnp.zeros_like(total) if before is None else before[...]

    for index, drive in enumerate((d0, d1, d2, d3)):

        @pl.when(slot == index)
        def _(drive=drive):
            steps[...] = drive[...].astype(jnp.float32)

    for lag in range(lags):
        lagged[lag] = steps[HALO - lag : HALO - lag + width, :].astype(jnp.bfloat16)
    added = None
    for lag in range(lags):
        kernel = masked(weight[lag], columns[:, lag : lag + 1], bit[...])
        term = lax.dot_general(
            kernel, lagged[lag], (((1,), (1,)), ((), ())), preferred_element_type=jnp.float32
        )
        added = term if added is None else added + term
    total[...] += added
    if last:
        length = width // 2

        @pl.when(slot == 3)
        def _():
            first = pl.multiple_of(place[1] * length, length)
            second = pl.multiple_of((1 - place[1]) * length, length)
            keep[...] = total[:, pl.ds(first, length)]
            send[...] = total[:, pl.ds(second, length)].astype(send.dtype)


def whole(shape):
    return pl.BlockSpec(shape, lambda slot, place: (0,) * len(shape))


def call(kernel, name, grid, in_specs, out_specs, out_shape, scratch, flops, moved):
    return pl.pallas_call(
        kernel,
        out_shape=out_shape,
        grid_spec=pltpu.PrefetchScalarGridSpec(
            num_scalar_prefetch=1,
            grid=(grid,),
            in_specs=in_specs,
            out_specs=out_specs,
            scratch_shapes=scratch,
        ),
        cost_estimate=pl.CostEstimate(flops=flops, bytes_accessed=moved, transcendentals=0),
        compiler_params=pltpu.CompilerParams(vmem_limit_bytes=VMEM_BYTES),
        name=name,
    )


def paired(
    traces,
    weights,
    pattern,
    cluster,
    element_damping_rate,
    local_step_length,
    housing_keep_share,
    admittance,
):
    rows, length = traces.shape
    lags, _, elements = weights.shape
    window = HALO + 2 * length
    unit = rows // (2 * CHUNKS)
    row = lax.axis_index("row")
    slab = lax.axis_index("tm")
    half = slab % 2
    place = jnp.stack([row, half]).astype(jnp.int32)
    f32, bf16 = jnp.float32, jnp.bfloat16
    tm_count = lax.axis_size("tm")
    swap = [(i, i ^ 1) for i in range(tm_count)]
    near = [(i, i + 1 if i % 2 else i - 1) for i in range(tm_count)]
    near = [(i, j) for i, j in near if 0 <= j < tm_count]
    far = [(i, i + 2 if i % 2 else i - 2) for i in range(tm_count)]
    far = [(i, j) for i, j in far if 0 <= j < tm_count]

    partner = lax.ppermute(traces, "tm", swap)
    clocks = jnp.stack([local_step_length, housing_keep_share])
    partner_clocks = lax.ppermute(clocks, "tm", swap)
    odd = half == 1
    edge = jnp.where(odd, traces[:, length - HALO :], traces[:, :HALO]).astype(f32).T
    edge_clocks = jnp.where(odd, clocks[:, length - HALO :], clocks[:, :HALO]).T
    edge = jnp.concatenate([edge, edge_clocks, jnp.zeros((HALO, 126), f32)], 1)
    got_near = lax.ppermute(edge, "tm", near)
    got_far = lax.ppermute(edge, "tm", far)
    ahead = jnp.where(odd, got_far, got_near)
    behind = jnp.where(odd, got_near, got_far)

    words_by_row = (pattern << jnp.arange(pattern.shape[2], dtype=jnp.int32)).sum(2)
    own_labels = lax.dynamic_slice_in_dim(cluster, row * rows, rows, 0)
    hit = own_labels[None, :] == jnp.arange(pattern.shape[1], dtype=jnp.int32)[:, None]
    words = jnp.where(hit[None], words_by_row[:, :, None], 0).sum(1)
    words = jnp.concatenate([words, jnp.zeros((8 - lags, rows), jnp.int32)], 0)
    bit = (jnp.int32(1) << cluster)[None, :]
    rate = element_damping_rate[None, :]
    gain = admittance[None, :]

    first_clocks = jnp.where(odd, partner_clocks, clocks)
    second_clocks = jnp.where(odd, clocks, partner_clocks)
    clock = jnp.concatenate([ahead[:, rows : rows + 2].T, first_clocks, second_clocks], 1)
    at = jnp.arange(window, dtype=jnp.int32)
    from_here = at[:, None] <= at[None, :]
    spans = jnp.where(from_here, clock[0][None, :], 0.0).sum(1)
    shares = jnp.where(from_here, clock[1][None, :], 1.0).prod(1)
    aux = jnp.concatenate([clock, spans[None], shares[None], jnp.zeros((4, window), f32)], 0)
    aux = jnp.concatenate([aux, jnp.zeros((8, -window % 128), f32)], 1)

    def slot_block(chunk):
        return lambda slot, place: (
            (jnp.bitwise_xor(place[0], slot) * 2 + place[1]) * CHUNKS + chunk
        )

    def weight_spec(chunk):
        block = slot_block(chunk)
        return pl.BlockSpec((lags, rows, unit), lambda slot, place: (0, 0, block(slot, place)))

    def row_spec(chunk, own=False):
        block = slot_block(chunk)
        return pl.BlockSpec(
            (1, unit), lambda slot, place: (0, block(0 if own else slot, place))
        )

    strip = jax.ShapeDtypeStruct((window, unit), bf16)
    share_bytes = 4 * lags * rows * unit * 2
    share_flops = 2 * 4 * lags * rows * unit * window

    def correlated(chunk):
        return call(
            correlate_kernel,
            "correlate",
            4,
            [
                whole((rows, length)),
                whole((rows, length)),
                whole((HALO, rows + 128)),
                whole((HALO, rows + 128)),
                whole((8, rows)),
                row_spec(chunk),
                weight_spec(chunk),
            ],
            [whole((window, unit))] * 4,
            [strip] * 4,
            [
                pltpu.VMEM((window + HALO, rows), f32),
                pltpu.VMEM((lags, window, rows), bf16),
                pltpu.VMEM((rows, 8), jnp.int32),
            ],
            share_flops,
            share_bytes,
        )(place, traces, partner, ahead, behind, words, bit, weights)

    def over_row(array, by):
        return lax.ppermute(array, "row", [(i, i ^ by) for i in range(4)])

    def summed(parts):
        o0, o1, o2, o3 = parts
        s3 = over_row(o3, 1)
        s1 = over_row(o1, 1)
        pair = (o2.astype(f32) + s3.astype(f32)).astype(bf16)
        return o0, s1, over_row(pair, 2)

    def recurrence(chunk, terms):
        return call(
            recurrence_kernel,
            "recurrence",
            1,
            [whole((window, unit))] * 3 + [row_spec(chunk, True), whole(aux.shape)],
            [whole((window, unit)), whole((8, unit))],
            [jax.ShapeDtypeStruct((window, unit), f32), jax.ShapeDtypeStruct((8, unit), f32)],
            [],
            window * unit * 40,
            window * unit * 10,
        )(place, *terms, rate, aux)

    def finished(chunk, partial, incoming):
        piece = jax.ShapeDtypeStruct((unit, length), f32)
        return call(
            finish_kernel,
            "finish",
            1,
            [whole((window, unit)), whole((8, unit))]
            + [row_spec(chunk, True)] * 2
            + [whole(aux.shape)],
            [whole((window, unit)), whole((unit, length)), whole((unit, length))],
            [strip, piece, piece],
            [pltpu.VMEM((window, unit), f32)],
            window * unit * 20,
            window * unit * 12,
        )(place, partial, incoming, rate, gain, aux)

    def reconstructed(chunk, drives, before):
        last = before is not None
        wide = whole((rows, 2 * length))
        scratch = [
            pltpu.VMEM((window, unit), f32),
            pltpu.VMEM((lags, 2 * length, unit), bf16),
            pltpu.VMEM((rows, 8), jnp.int32),
        ]
        if last:
            out_specs = [whole((rows, length))] * 2
            out_shape = [jax.ShapeDtypeStruct((rows, length), f32)] * 2
            out_shape[1] = jax.ShapeDtypeStruct((rows, length), bf16)
            scratch = [pltpu.VMEM((rows, 2 * length), f32)] + scratch
        else:
            out_specs = wide
            out_shape = jax.ShapeDtypeStruct((rows, 2 * length), f32)
        return call(
            functools.partial(reconstruct_kernel, last),
            "reconstruct",
            4,
            [whole((window, unit))] * 4
            + [whole((8, rows)), row_spec(chunk), weight_spec(chunk)]
            + ([wide] if last else []),
            out_specs,
            out_shape,
            scratch,
            share_flops,
            share_bytes,
        )(place, *drives, words, bit, weights, *([before] if last else []))

    parts = [correlated(chunk) for chunk in range(CHUNKS)]
    states, drives = [], []
    for chunk in range(CHUNKS):
        partial, first = recurrence(chunk, summed(parts[chunk]))
        incoming = lax.ppermute(first, "tm", [(i, i - 2) for i in range(2, tm_count)])
        drive, mine, theirs = finished(chunk, partial, incoming)
        d1 = over_row(drive, 1)
        d2 = over_row(drive, 2)
        d3 = over_row(d2, 1)
        drives.append((drive, d1, d2, d3))
        states.append((mine, lax.ppermute(theirs, "tm", swap)))
    held = None
    for chunk in range(CHUNKS):
        held = reconstructed(chunk, drives[chunk], held)
    keep, send = held
    pressure = keep + lax.ppermute(send, "tm", swap).astype(f32)
    mine = jnp.concatenate([s[0] for s in states], 0)
    other = jnp.concatenate([s[1] for s in states], 0)
    state = jnp.where(
        odd, jnp.concatenate([other, mine], 0), jnp.concatenate([mine, other], 0)
    )
    return (state, pressure.astype(bf16))


def local(traces, weights, pattern, *rest):
    rows, length = traces.shape
    fits = (
        lax.axis_size("row") == 4
        and lax.axis_size("tm") == 4
        and length == 128
        and rows % (256 * CHUNKS) == 0
        and weights.shape[0] <= 8
        and pattern.shape[1] <= 32
    )
    return (paired if fits else general)(traces, weights, pattern, *rest)


def solution(mesh):
    placed = (P("row", ("group", "tm")), P(None, "row", None), P(), P(), P(), P("tm"), P("tm"), P())
    return jax.shard_map(
        local,
        mesh=mesh,
        in_specs=placed,
        out_specs=(P("row", ("group", "tm")), P("row", ("group", "tm"))),
        check_vma=False,
    )
```

time: 237 us -> 116 us (0.49)
  local copies, waits for them, and re-layouts: 77 us -> 10.9 us
  matrix products: 64.9 us -> 0 us
  Pallas kernels: 0 us -> 48.1 us
  waiting for transfers between devices: 53.6 us -> 23.1 us
  starting transfers between devices: 3.49 us -> 23.7 us
  between operations: 14.4 us -> 0.86 us
  blocking collectives: 10.5 us -> 0 us
    dot_general x12 -> x0, matrix products: 64.9 us -> none  [the longest x4 29.6 us: lag_kernels(): jnp.dot(picked.astype(jnp.bfloat16), column_onehot, preferred_element_typ...]
    psum x1 -> x0, waiting for transfers between devices: 53.6 us -> none  [local(): lax.psum(correlate(kernels, extended).astype(jnp.bfloat16), 'row')]
    slice x35 -> x2, local copies, waits for them, and re-layouts: 54.2 us -> 1.19 us  [the longest x1 1.16 us: paired(): traces[:, :HALO]]
    pallas_call x0 -> x8, Pallas kernels: none -> 48.1 us  [the longest x2 18.7 us: correlated(): call(correlate_kernel, 'correlate', 4, [whole((rows, length)), whole((row...]
    ppermute x2 -> x21, waiting for transfers between devices: 0.01 us -> 23.1 us  [the longest x12 11.6 us: over_row(): return lax.ppermute(array, 'row', [(i, i ^ by) for i in range(4)])]
    ppermute x2 -> x21, starting transfers between devices: 3.45 us -> 23.7 us  [the longest x12 17.9 us: over_row(): return lax.ppermute(array, 'row', [(i, i ^ by) for i in range(4)])]
    dynamic_update_slice x16 -> x0, local copies, waits for them, and re-layouts: 10.7 us -> none  [block_recurrence(): lax.scan(advance, start, (keep_rows, inflow_rows), reverse=True)]
    all_gather x2 -> x0, blocking collectives: 10.5 us -> none  [carried_in(): lax.all_gather(a.astype(kind), axis)]
  transfers between devices with their start and end apart: 3 -> 21, of which waited for: 1 -> 9; matrix products, arithmetic and copies ran while one was open for 17% -> 10% of each run, Pallas kernels for 0% -> 26%
where the time goes in v1:
time: 116 us; the launch traced here: 115 us
  Pallas kernels  48.1 us (41%)
  starting transfers between devices  23.7 us (20%)
  waiting for transfers between devices  23.1 us (20%)
  local copies, waits for them, and re-layouts  10.9 us (9%)
  other arithmetic  8.51 us (7%)
    pallas_call x2, Pallas kernels, correlated(): call(correlate_kernel, 'correlate', 4, [whole((rows, length)), whole((row...  18.7 us
    ppermute x12, starting transfers between devices, over_row(): return lax.ppermute(array, 'row', [(i, i ^ by) for i in range(4)])  17.9 us
    pallas_call x2, Pallas kernels, reconstructed(): call(functools.partial(reconstruct_kernel, last), 'reconstruct', 4, [whol...  16.9 us
    ppermute x12, waiting for transfers between devices, over_row(): return lax.ppermute(array, 'row', [(i, i ^ by) for i in range(4)])  11.6 us
    ppermute x2, waiting for transfers between devices, paired(): lax.ppermute(first, 'tm', [(i, i - 2) for i in range(2, tm_count)])  8.73 us
    pallas_call x2, Pallas kernels, recurrence(): call(recurrence_kernel, 'recurrence', 1, [whole((window, unit))] * 3 + [r...  6.97 us
    pallas_call x2, Pallas kernels, finished(): call(finish_kernel, 'finish', 1, [whole((window, unit)), whole((8, unit))...  5.48 us
    unnamed x38, local copies, waits for them, and re-layouts  5.46 us
  transfers between devices with their start and end apart: 21, of which 9 were waited for; matrix products, arithmetic and copies ran while one was open for 10% of the time, Pallas kernels for 26%

profile of v1, /device:TPU:0, one launch (start us, length us, event | category | flops | bytes accessed | tf_op | source)
XLA Modules:
  0.0 115.1 jit_solution(12895262776027008371)
XLA Ops:
  0.6 0.7 pad_maximum_fusion.1
  1.3 0.5 collective-permute-start.6
  1.8 1.2 %fusion = (bf16[1024,16]{1,0:T(8,128)(2,1)S(1)}, bf16[1024,16]{1,0:T(8,128)(2,1)S(1)}) fusion(bf16[1024,128]{1,0:T(8,128)(2,1)} %traces.3), kind=kLoop, calls=%fused_computation.24 | loop fusion | bytes 131072 | tf_op jit(solution)/shard_map/slice | solution.py:327
  3.1 0.1 copy.27
  3.2 0.1 copy.37
  3.3 0.1 copy.36
  3.5 0.7 collective-permute-start.2
  4.2 1.3 %collective-permute-start.1 = (f32[16,1152]{1,0:T(8,128)S(1)}, f32[16,1152]{1,0:T(8,128)S(1)}, u32[]{:S(2)}, u32[]{:S(2)}) collective-permute-start(f32[16,1152]{1,0:T(8,128)S(1)} %concatenate.25), channel_id=1, source_target_pairs={{4,12},{8,0},{5,13},{9,1},{6,14},{10,2},{7,15},{11,3},{20,28},{24,... | collective-permute-start | bytes 221192 | tf_op jit(solution)/shard_map/ppermute | solution.py:331
  5.5 1.0 shift-left_reduce_fusion
  6.5 1.3 %broadcast_shift-left_fusion = s32[4096]{0:T(1024)} fusion(s32[4096]{0:T(1024)} %param.11), kind=kLoop, calls=%fused_computation.14 | loop fusion | flops 4096 | bytes 32768 | tf_op jit(solution)/shard_map/shift_left | solution.py:340
  7.8 0.7 dynamic_slice.3
  8.5 0.1 select_reduce_fusion
  8.7 0.6 pad_add_fusion.place
  9.2 0.6 concatenate.26.words
  9.9 0.7 broadcast_select_fusion.3
  10.6 1.4 %collective-permute-done.1 = f32[16,1152]{1,0:T(8,128)S(1)} collective-permute-done((f32[16,1152]{1,0:T(8,128)S(1)}, f32[16,1152]{1,0:T(8,128)S(1)}, u32[]{:S(2)}, u32[]{:S(2)}) %collective-permute-start.1) | collective-permute-done | bytes 73760 | tf_op jit(solution)/shard_map/ppermute | solution.py:331
  12.0 0.2 copy.28
  12.2 0.2 copy.29
  12.5 0.1 broadcast_select_fusion
  12.6 0.2 select_reduce_fusion.1
  12.8 0.8 copy.32.ahead
  13.7 0.8 copy.33.behind
  14.6 0.6 concatenate.29.aux
  15.2 0.7 copy-done
  15.9 9.4 %correlate.2 = (bf16[272,256]{1,0:T(8,128)(2,1)}, bf16[272,256]{1,0:T(8,128)(2,1)}, bf16[272,256]{1,0:T(8,128)(2,1)}, bf16[272,256]{1,0:T(8,128)(2,1)}) custom-call(s32[2]{0:T(128)} %pad_add_fusion.place, bf16[1024,128]{1,0:T(8,128)(2,1)} %traces.3, bf16[1024,128]{1,0:T(8,128)(2,1)} %copy-done, f32[16,1152]{1,0:T(8,128)} %copy.32.ahead, ...), custom_call_target="tpu_custom_call" | custom-call | flops 2281701376 | bytes 8388608 | tf_op jit(solution)/shard_map/correlate/pallas_call | solution.py:374
  25.3 1.8 %collective-permute-start.3 = (bf16[272,256]{1,0:T(8,128)(2,1)}, bf16[272,256]{1,0:T(8,128)(2,1)S(1)}, u32[]{:S(2)}, u32[]{:S(2)}) collective-permute-start(bf16[272,256]{1,0:T(8,128)(2,1)} %get-tuple-element.23), channel_id=1, source_target_pairs={{0,1},{1,0},{2,3},{3,2},{4,5},{5,4},{6,7},{7,6},{8,9},{9,8},{10,11... | collective-permute-start | bytes 417800 | tf_op jit(solution)/shard_map/ppermute | solution.py:399
  27.1 0.3 collective-permute-start.4
  27.3 9.4 %correlate.3 = (bf16[272,256]{1,0:T(8,128)(2,1)}, bf16[272,256]{1,0:T(8,128)(2,1)}, bf16[272,256]{1,0:T(8,128)(2,1)}, bf16[272,256]{1,0:T(8,128)(2,1)}) custom-call(s32[2]{0:T(128)} %pad_add_fusion.place, bf16[1024,128]{1,0:T(8,128)(2,1)} %traces.3, bf16[1024,128]{1,0:T(8,128)(2,1)} %copy-done, f32[16,1152]{1,0:T(8,128)} %copy.32.ahead, ...), custom_call_target="tpu_custom_call" | custom-call | flops 2281701376 | bytes 8388608 | tf_op jit(solution)/shard_map/correlate/pallas_call | solution.py:374
  36.7 1.8 %collective-permute-start.9 = (bf16[272,256]{1,0:T(8,128)(2,1)}, bf16[272,256]{1,0:T(8,128)(2,1)S(1)}, u32[]{:S(2)}, u32[]{:S(2)}) collective-permute-start(bf16[272,256]{1,0:T(8,128)(2,1)} %get-tuple-element.30), channel_id=1, source_target_pairs={{0,1},{1,0},{2,3},{3,2},{4,5},{5,4},{6,7},{7,6},{8,9},{9,8},{10,11... | collective-permute-start | bytes 417800 | tf_op jit(solution)/shard_map/ppermute | solution.py:399
  38.5 0.3 collective-permute-start.10
  38.8 2.8 %collective-permute-start.5 = (bf16[272,256]{1,0:T(8,128)(2,1)S(1)}, bf16[272,256]{1,0:T(8,128)(2,1)S(1)}, u32[]{:S(2)}, u32[]{:S(2)}) collective-permute-start(bf16[272,256]{1,0:T(8,128)(2,1)S(1)} %add_convert_fusion.2), channel_id=1, source_target_pairs={{0,2},{1,3},{2,0},{3,1},{4,6},{5,7},{6,4},{7,5},{8,10},{9,11},{10,... | collective-permute-start | bytes 417800 | tf_op jit(solution)/shard_map/ppermute | solution.py:399
  41.6 6.6 %collective-permute-done.10 = bf16[272,256]{1,0:T(8,128)(2,1)S(1)} collective-permute-done((bf16[272,256]{1,0:T(8,128)(2,1)}, bf16[272,256]{1,0:T(8,128)(2,1)S(1)}, u32[]{:S(2)}, u32[]{:S(2)}) %collective-permute-start.10) | collective-permute-done | bytes 139296 | tf_op jit(solution)/shard_map/ppermute | solution.py:399
  48.2 0.9 add_convert_fusion.1
  49.2 1.9 %collective-permute-start.11 = (bf16[272,256]{1,0:T(8,128)(2,1)S(1)}, bf16[272,256]{1,0:T(8,128)(2,1)S(1)}, u32[]{:S(2)}, u32[]{:S(2)}) collective-permute-start(bf16[272,256]{1,0:T(8,128)(2,1)S(1)} %add_convert_fusion.1), channel_id=1, source_target_pairs={{0,2},{1,3},{2,0},{3,1},{4,6},{5,7},{6,4},{7,5},{8,10},{9,11},{10,... | collective-permute-start | bytes 417800 | tf_op jit(solution)/shard_map/ppermute | solution.py:399
  51.1 0.6 copy-done.8
  51.8 3.5 %recurrence.2 = (f32[272,256]{1,0:T(8,128)}, f32[8,256]{1,0:T(8,128)}) custom-call(s32[2]{0:T(128)} %pad_add_fusion.place, bf16[272,256]{1,0:T(8,128)(2,1)} %get-tuple-element.22.own, bf16[272,256]{1,0:T(8,128)(2,1)} %copy-done.8, bf16[272,256]{1,0:T(8,128)(2,1)} %copy-done.11, f32[1,4096]{1,0:T(1,128)} %bitcast.17, f32[8,384]{1,0:T(8,128)} %concatenate.29.aux), custom_call_target="tpu_custom_call" | custom-call | flops 2785280 | bytes 696320 | tf_op jit(solution)/shard_map/recurrence/pallas_call | solution.py:409
  55.3 1.3 %collective-permute-start.7 = (f32[8,256]{1,0:T(8,128)}, f32[8,256]{1,0:T(8,128)S(1)}, u32[]{:S(2)}, u32[]{:S(2)}) collective-permute-start(f32[8,256]{1,0:T(8,128)} %get-tuple-element.27), channel_id=1, source_target_pairs={{8,0},{12,4},{9,1},{13,5},{10,2},{14,6},{11,3},{15,7},{24,16},{28,... | collective-permute-start | bytes 24584 | tf_op jit(solution)/shard_map/ppermute | solution.py:471
  56.5 4.5 %collective-permute-done.7.incoming = f32[8,256]{1,0:T(8,128)S(1)} collective-permute-done((f32[8,256]{1,0:T(8,128)}, f32[8,256]{1,0:T(8,128)S(1)}, u32[]{:S(2)}, u32[]{:S(2)}) %collective-permute-start.7) | collective-permute-done | bytes 8224 | tf_op jit(solution)/shard_map/ppermute | solution.py:471
  61.0 0.6 copy-done.15
  61.6 2.7 %finish.2 = (bf16[272,256]{1,0:T(8,128)(2,1)}, f32[256,128]{1,0:T(8,128)}, f32[256,128]{1,0:T(8,128)}) custom-call(s32[2]{0:T(128)} %pad_add_fusion.place, f32[272,256]{1,0:T(8,128)} %get-tuple-element.26.partial, f32[8,256]{1,0:T(8,128)} %copy-done.15, f32[1,4096]{1,0:T(1,128)} %bitcast.18, f32[1,4096]{1,0:T(1,128)} %bitcast.21, f32[8,384]{1,0:T(8,128)} %concatenate.29.aux), custom_call_target="tpu_custom_call" | custom-call | flops 1392640 | bytes 835584 | tf_op jit(solution)/shard_map/finish/pallas_call | solution.py:423
  64.3 1.1 collective-permute-start.18
  65.4 0.6 copy-done.7
  66.1 3.5 %recurrence.3 = (f32[272,256]{1,0:T(8,128)}, f32[8,256]{1,0:T(8,128)}) custom-call(s32[2]{0:T(128)} %pad_add_fusion.place, bf16[272,256]{1,0:T(8,128)(2,1)} %get-tuple-element.29.own, bf16[272,256]{1,0:T(8,128)(2,1)} %copy-done.7, bf16[272,256]{1,0:T(8,128)(2,1)} %copy-done.9, f32[1,4096]{1,0:T(1,128)} %bitcast.19, f32[8,384]{1,0:T(8,128)} %concatenate.29.aux), custom_call_target="tpu_custom_call" | custom-call | flops 2785280 | bytes 696320 | tf_op jit(solution)/shard_map/recurrence/pallas_call | solution.py:409
  69.6 1.5 %collective-permute-start.12 = (f32[8,256]{1,0:T(8,128)}, f32[8,256]{1,0:T(8,128)S(1)}, u32[]{:S(2)}, u32[]{:S(2)}) collective-permute-start(f32[8,256]{1,0:T(8,128)} %get-tuple-element.34), channel_id=1, source_target_pairs={{8,0},{12,4},{9,1},{13,5},{10,2},{14,6},{11,3},{15,7},{24,16},{28,... | collective-permute-start | bytes 24584 | tf_op jit(solution)/shard_map/ppermute | solution.py:471
  71.1 4.3 %collective-permute-done.12.incoming = f32[8,256]{1,0:T(8,128)S(1)} collective-permute-done((f32[8,256]{1,0:T(8,128)}, f32[8,256]{1,0:T(8,128)S(1)}, u32[]{:S(2)}, u32[]{:S(2)}) %collective-permute-start.12) | collective-permute-done | bytes 8224 | tf_op jit(solution)/shard_map/ppermute | solution.py:471
  75.4 0.6 copy-done.14
  76.0 2.7 %finish.3 = (bf16[272,256]{1,0:T(8,128)(2,1)}, f32[256,128]{1,0:T(8,128)}, f32[256,128]{1,0:T(8,128)}) custom-call(s32[2]{0:T(128)} %pad_add_fusion.place, f32[272,256]{1,0:T(8,128)} %get-tuple-element.33.partial, f32[8,256]{1,0:T(8,128)} %copy-done.14, f32[1,4096]{1,0:T(1,128)} %bitcast.20, f32[1,4096]{1,0:T(1,128)} %bitcast.22, f32[8,384]{1,0:T(8,128)} %concatenate.29.aux), custom_call_target="tpu_custom_call" | custom-call | flops 1392640 | bytes 835584 | tf_op jit(solution)/shard_map/finish/pallas_call | solution.py:423
  78.7 1.9 %collective-permute-start.15 = (bf16[272,256]{1,0:T(8,128)(2,1)}, bf16[272,256]{1,0:T(8,128)(2,1)S(1)}, u32[]{:S(2)}, u32[]{:S(2)}) collective-permute-start(bf16[272,256]{1,0:T(8,128)(2,1)} %get-tuple-element.38.d0), channel_id=1, source_target_pairs={{0,2},{1,3},{2,0},{3,1},{4,6},{5,7},{6,4},{7,5},{8,10},{9,11},{10,... | collective-permute-start | bytes 417800 | tf_op jit(solution)/shard_map/ppermute | solution.py:399
  80.6 2.5 %collective-permute-start.17 = (bf16[272,256]{1,0:T(8,128)(2,1)}, bf16[272,256]{1,0:T(8,128)(2,1)S(1)}, u32[]{:S(2)}, u32[]{:S(2)}) collective-permute-start(bf16[272,256]{1,0:T(8,128)(2,1)} %get-tuple-element.39.d0), channel_id=1, source_target_pairs={{0,1},{1,0},{2,3},{3,2},{4,5},{5,4},{6,7},{7,6},{8,9},{9,8},{10,11... | collective-permute-start | bytes 417800 | tf_op jit(solution)/shard_map/ppermute | solution.py:399
  83.2 2.0 %collective-permute-start.14 = (bf16[272,256]{1,0:T(8,128)(2,1)}, bf16[272,256]{1,0:T(8,128)(2,1)S(1)}, u32[]{:S(2)}, u32[]{:S(2)}) collective-permute-start(bf16[272,256]{1,0:T(8,128)(2,1)} %get-tuple-element.38.d0), channel_id=1, source_target_pairs={{0,1},{1,0},{2,3},{3,2},{4,5},{5,4},{6,7},{7,6},{8,9},{9,8},{10,11... | collective-permute-start | bytes 417800 | tf_op jit(solution)/shard_map/ppermute | solution.py:399
  85.2 1.3 %collective-permute-done.15.d2 = bf16[272,256]{1,0:T(8,128)(2,1)S(1)} collective-permute-done((bf16[272,256]{1,0:T(8,128)(2,1)}, bf16[272,256]{1,0:T(8,128)(2,1)S(1)}, u32[]{:S(2)}, u32[]{:S(2)}) %collective-permute-start.15) | collective-permute-done | bytes 139296 | tf_op jit(solution)/shard_map/ppermute | solution.py:399
  86.5 1.5 %collective-permute-start.16 = (bf16[272,256]{1,0:T(8,128)(2,1)S(1)}, bf16[272,256]{1,0:T(8,128)(2,1)S(1)}, u32[]{:S(2)}, u32[]{:S(2)}) collective-permute-start(bf16[272,256]{1,0:T(8,128)(2,1)S(1)} %collective-permute-done.15.d2), channel_id=1, source_target_pairs={{0,1},{1,0},{2,3},{3,2},{4,5},{5,4},{6,7},{7,6},{8,9},{9,8},{10,11... | collective-permute-start | bytes 417800 | tf_op jit(solution)/shard_map/ppermute | solution.py:399
  88.0 0.8 collective-permute-done.17.d1
  88.7 3.0 %collective-permute-done.19.d3 = bf16[272,256]{1,0:T(8,128)(2,1)S(1)} collective-permute-done((bf16[272,256]{1,0:T(8,128)(2,1)S(1)}, bf16[272,256]{1,0:T(8,128)(2,1)S(1)}, u32[]{:S(2)}, u32[]{:S(2)}) %collective-permute-start.19) | collective-permute-done | bytes 139296 | tf_op jit(solution)/shard_map/ppermute | solution.py:399
  91.7 0.7 copy-done.6
  92.4 8.3 %reconstruct.2.refs_0_ = f32[1024,256]{1,0:T(8,128)} custom-call(s32[2]{0:T(128)} %pad_add_fusion.place, bf16[272,256]{1,0:T(8,128)(2,1)} %get-tuple-element.39.d0, bf16[272,256]{1,0:T(8,128)(2,1)} %copy-done.4, bf16[272,256]{1,0:T(8,128)(2,1)} %copy-done.1, bf16[272,256]{1,0:T(8,128)(2,1)} %copy-done.6, s32[8,1024]{1,0:T(8,128)} %concatenate.26.words, ...), custom_call_target="tpu_custom_call" | custom-call | flops 2281701376 | bytes 8388608 | tf_op jit(solution)/shard_map/reconstruct/pallas_call | solution.py:453
  100.7 0.6 copy-done.3
  101.3 0.6 copy-done.5
  102.0 8.6 %reconstruct.3 = (f32[1024,128]{1,0:T(8,128)}, bf16[1024,128]{1,0:T(8,128)(2,1)}) custom-call(s32[2]{0:T(128)} %pad_add_fusion.place, bf16[272,256]{1,0:T(8,128)(2,1)} %get-tuple-element.38.d0, bf16[272,256]{1,0:T(8,128)(2,1)} %copy-done.3, bf16[272,256]{1,0:T(8,128)(2,1)} %copy-done.2, bf16[272,256]{1,0:T(8,128)(2,1)} %copy-done.5, ...), custom_call_target="tpu_custom_call" | custom-call | flops 2281701376 | bytes 8388608 | tf_op jit(solution)/shard_map/reconstruct/pallas_call | solution.py:453
  110.6 0.5 collective-permute-start.8
  111.2 1.1 collective-permute-done.8
  112.3 0.2 collective-permute-done.13
  112.5 0.8 maximum_select_fusion
  113.3 1.8 %add_convert_fusion = bf16[1024,128]{1,0:T(8,128)(2,1)} fusion(f32[1024,128]{1,0:T(8,128)} %get-tuple-element.40, bf16[1024,128]{1,0:T(8,128)(2,1)S(1)} %collective-permute-done.20), kind=kLoop, calls=%fused_computation.1 | loop fusion | flops 393216 | bytes 1048576 | tf_op jit(solution)/shard_map/convert_element_type | solution.py:488
  (58 shorter events, 0.9 us)
Async XLA Ops:
  1.3 8.6 %collective-permute-start.6 = (f32[2,128]{1,0:T(2,128)S(1)}, f32[2,128]{1,0:T(2,128)S(1)}, u32[]{:S(2)}, u32[]{:S(2)}) collective-permute-start(f32[2,128]{1,0:T(2,128)S(1)} %pad_maximum_fusion.1), channel_id=1, source_target_pairs={{0,4},{4,0},{8,12},{12,8},{1,5},{5,1},{9,13},{13,9},{2,6},{6,2},{1... | collective-permute-start | bytes 3080 | tf_op jit(solution)/shard_map/ppermute | solution.py:325
  1.8 13.4 %collective-permute-start = (bf16[1024,128]{1,0:T(8,128)(2,1)}, bf16[1024,128]{1,0:T(8,128)(2,1)S(1)}, u32[]{:S(2)}, u32[]{:S(2)}) collective-permute-start(bf16[1024,128]{1,0:T(8,128)(2,1)} %traces.3), channel_id=1, source_target_pairs={{0,4},{4,0},{8,12},{12,8},{1,5},{5,1},{9,13},{13,9},{2,6},{6,2},{1... | collective-permute-start | bytes 786440 | tf_op jit(solution)/shard_map/ppermute | solution.py:323
  3.5 8.7 %collective-permute-start.2 = (f32[16,1152]{1,0:T(8,128)S(1)}, f32[16,1152]{1,0:T(8,128)S(1)}, u32[]{:S(2)}, u32[]{:S(2)}) collective-permute-start(f32[16,1152]{1,0:T(8,128)S(1)} %concatenate.25), channel_id=1, source_target_pairs={{4,8},{8,4},{5,9},{9,5},{6,10},{10,6},{7,11},{11,7},{20,24},{24,20... | collective-permute-start | bytes 221192 | tf_op jit(solution)/shard_map/ppermute | solution.py:330
  4.2 7.8 %collective-permute-start.1 = (f32[16,1152]{1,0:T(8,128)S(1)}, f32[16,1152]{1,0:T(8,128)S(1)}, u32[]{:S(2)}, u32[]{:S(2)}) collective-permute-start(f32[16,1152]{1,0:T(8,128)S(1)} %concatenate.25), channel_id=1, source_target_pairs={{4,12},{8,0},{5,13},{9,1},{6,14},{10,2},{7,15},{11,3},{20,28},{24,... | collective-permute-start | bytes 221192 | tf_op jit(solution)/shard_map/ppermute | solution.py:331
  15.2 0.7 copy-start
  25.3 13.5 %copy-start.10 = (bf16[272,256]{1,0:T(8,128)(2,1)S(1)}, bf16[272,256]{1,0:T(8,128)(2,1)}, u32[]{:S(2)}) copy-start(bf16[272,256]{1,0:T(8,128)(2,1)} %get-tuple-element.24) | copy-start | bytes 417796
  25.3 25.8 %collective-permute-start.3 = (bf16[272,256]{1,0:T(8,128)(2,1)}, bf16[272,256]{1,0:T(8,128)(2,1)S(1)}, u32[]{:S(2)}, u32[]{:S(2)}) collective-permute-start(bf16[272,256]{1,0:T(8,128)(2,1)} %get-tuple-element.23), channel_id=1, source_target_pairs={{0,1},{1,0},{2,3},{3,2},{4,5},{5,4},{6,7},{7,6},{8,9},{9,8},{10,11... | collective-permute-start | bytes 417800 | tf_op jit(solution)/shard_map/ppermute | solution.py:399
  27.1 11.7 %collective-permute-start.4 = (bf16[272,256]{1,0:T(8,128)(2,1)}, bf16[272,256]{1,0:T(8,128)(2,1)S(1)}, u32[]{:S(2)}, u32[]{:S(2)}) collective-permute-start(bf16[272,256]{1,0:T(8,128)(2,1)} %get-tuple-element.25), channel_id=1, source_target_pairs={{0,1},{1,0},{2,3},{3,2},{4,5},{5,4},{6,7},{7,6},{8,9},{9,8},{10,11... | collective-permute-start | bytes 417800 | tf_op jit(solution)/shard_map/ppermute | solution.py:399
  36.7 28.7 %collective-permute-start.9 = (bf16[272,256]{1,0:T(8,128)(2,1)}, bf16[272,256]{1,0:T(8,128)(2,1)S(1)}, u32[]{:S(2)}, u32[]{:S(2)}) collective-permute-start(bf16[272,256]{1,0:T(8,128)(2,1)} %get-tuple-element.30), channel_id=1, source_target_pairs={{0,1},{1,0},{2,3},{3,2},{4,5},{5,4},{6,7},{7,6},{8,9},{9,8},{10,11... | collective-permute-start | bytes 417800 | tf_op jit(solution)/shard_map/ppermute | solution.py:399
  38.5 9.7 %collective-permute-start.10 = (bf16[272,256]{1,0:T(8,128)(2,1)}, bf16[272,256]{1,0:T(8,128)(2,1)S(1)}, u32[]{:S(2)}, u32[]{:S(2)}) collective-permute-start(bf16[272,256]{1,0:T(8,128)(2,1)} %get-tuple-element.32), channel_id=1, source_target_pairs={{0,1},{1,0},{2,3},{3,2},{4,5},{5,4},{6,7},{7,6},{8,9},{9,8},{10,11... | collective-permute-start | bytes 417800 | tf_op jit(solution)/shard_map/ppermute | solution.py:399
  38.8 12.3 %collective-permute-start.5 = (bf16[272,256]{1,0:T(8,128)(2,1)S(1)}, bf16[272,256]{1,0:T(8,128)(2,1)S(1)}, u32[]{:S(2)}, u32[]{:S(2)}) collective-permute-start(bf16[272,256]{1,0:T(8,128)(2,1)S(1)} %add_convert_fusion.2), channel_id=1, source_target_pairs={{0,2},{1,3},{2,0},{3,1},{4,6},{5,7},{6,4},{7,5},{8,10},{9,11},{10,... | collective-permute-start | bytes 417800 | tf_op jit(solution)/shard_map/ppermute | solution.py:399
  49.2 16.3 %collective-permute-start.11 = (bf16[272,256]{1,0:T(8,128)(2,1)S(1)}, bf16[272,256]{1,0:T(8,128)(2,1)S(1)}, u32[]{:S(2)}, u32[]{:S(2)}) collective-permute-start(bf16[272,256]{1,0:T(8,128)(2,1)S(1)} %add_convert_fusion.1), channel_id=1, source_target_pairs={{0,2},{1,3},{2,0},{3,1},{4,6},{5,7},{6,4},{7,5},{8,10},{9,11},{10,... | collective-permute-start | bytes 417800 | tf_op jit(solution)/shard_map/ppermute | solution.py:399
  51.1 0.7 copy-start.8
  51.1 0.7 copy-start.11
  55.3 5.7 %collective-permute-start.7 = (f32[8,256]{1,0:T(8,128)}, f32[8,256]{1,0:T(8,128)S(1)}, u32[]{:S(2)}, u32[]{:S(2)}) collective-permute-start(f32[8,256]{1,0:T(8,128)} %get-tuple-element.27), channel_id=1, source_target_pairs={{8,0},{12,4},{9,1},{13,5},{10,2},{14,6},{11,3},{15,7},{24,16},{28,... | collective-permute-start | bytes 24584 | tf_op jit(solution)/shard_map/ppermute | solution.py:471
  61.0 0.6 copy-start.15
  64.3 18.8 %collective-permute-start.18 = (bf16[272,256]{1,0:T(8,128)(2,1)}, bf16[272,256]{1,0:T(8,128)(2,1)S(1)}, u32[]{:S(2)}, u32[]{:S(2)}) collective-permute-start(bf16[272,256]{1,0:T(8,128)(2,1)} %get-tuple-element.39.d0), channel_id=1, source_target_pairs={{0,2},{1,3},{2,0},{3,1},{4,6},{5,7},{6,4},{7,5},{8,10},{9,11},{10,... | collective-permute-start | bytes 417800 | tf_op jit(solution)/shard_map/ppermute | solution.py:399
  65.4 0.7 copy-start.7
  65.4 0.7 copy-start.9
  69.6 5.7 %collective-permute-start.12 = (f32[8,256]{1,0:T(8,128)}, f32[8,256]{1,0:T(8,128)S(1)}, u32[]{:S(2)}, u32[]{:S(2)}) collective-permute-start(f32[8,256]{1,0:T(8,128)} %get-tuple-element.34), channel_id=1, source_target_pairs={{8,0},{12,4},{9,1},{13,5},{10,2},{14,6},{11,3},{15,7},{24,16},{28,... | collective-permute-start | bytes 24584 | tf_op jit(solution)/shard_map/ppermute | solution.py:471
  75.4 0.6 copy-start.14
  78.7 31.9 %copy-start.16 = (f32[256,128]{1,0:T(8,128)S(1)}, f32[256,128]{1,0:T(8,128)}, u32[]{:S(2)}) copy-start(f32[256,128]{1,0:T(8,128)} %get-tuple-element.28) | copy-start | bytes 393220
  78.7 32.4 %copy-start.17 = (f32[256,128]{1,0:T(8,128)S(1)}, f32[256,128]{1,0:T(8,128)}, u32[]{:S(2)}) copy-start(f32[256,128]{1,0:T(8,128)} %get-tuple-element.35) | copy-start | bytes 393220
  78.7 33.8 %copy-start.12 = (f32[256,128]{1,0:T(8,128)S(1)}, f32[256,128]{1,0:T(8,128)}, u32[]{:S(2)}) copy-start(f32[256,128]{1,0:T(8,128)} %get-tuple-element.36) | copy-start | bytes 393220
  78.7 33.8 %copy-start.13 = (f32[256,128]{1,0:T(8,128)S(1)}, f32[256,128]{1,0:T(8,128)}, u32[]{:S(2)}) copy-start(f32[256,128]{1,0:T(8,128)} %get-tuple-element.37) | copy-start | bytes 393220
  78.7 7.7 %collective-permute-start.15 = (bf16[272,256]{1,0:T(8,128)(2,1)}, bf16[272,256]{1,0:T(8,128)(2,1)S(1)}, u32[]{:S(2)}, u32[]{:S(2)}) collective-permute-start(bf16[272,256]{1,0:T(8,128)(2,1)} %get-tuple-element.38.d0), channel_id=1, source_target_pairs={{0,2},{1,3},{2,0},{3,1},{4,6},{5,7},{6,4},{7,5},{8,10},{9,11},{10,... | collective-permute-start | bytes 417800 | tf_op jit(solution)/shard_map/ppermute | solution.py:399
  80.6 8.1 %collective-permute-start.17 = (bf16[272,256]{1,0:T(8,128)(2,1)}, bf16[272,256]{1,0:T(8,128)(2,1)S(1)}, u32[]{:S(2)}, u32[]{:S(2)}) collective-permute-start(bf16[272,256]{1,0:T(8,128)(2,1)} %get-tuple-element.39.d0), channel_id=1, source_target_pairs={{0,1},{1,0},{2,3},{3,2},{4,5},{5,4},{6,7},{7,6},{8,9},{9,8},{10,11... | collective-permute-start | bytes 417800 | tf_op jit(solution)/shard_map/ppermute | solution.py:399
  83.1 8.6 %copy-start.1 = (bf16[272,256]{1,0:T(8,128)(2,1)}, bf16[272,256]{1,0:T(8,128)(2,1)S(1)}, u32[]{:S(2)}) copy-start(bf16[272,256]{1,0:T(8,128)(2,1)S(1)} %collective-permute-done.18.d2) | copy-start | bytes 417796
  83.2 8.6 %collective-permute-start.19 = (bf16[272,256]{1,0:T(8,128)(2,1)S(1)}, bf16[272,256]{1,0:T(8,128)(2,1)S(1)}, u32[]{:S(2)}, u32[]{:S(2)}) collective-permute-start(bf16[272,256]{1,0:T(8,128)(2,1)S(1)} %collective-permute-done.18.d2), channel_id=1, source_target_pairs={{0,1},{1,0},{2,3},{3,2},{4,5},{5,4},{6,7},{7,6},{8,9},{9,8},{10,11... | collective-permute-start | bytes 417800 | tf_op jit(solution)/shard_map/ppermute | solution.py:399
  83.2 17.4 %collective-permute-start.14 = (bf16[272,256]{1,0:T(8,128)(2,1)}, bf16[272,256]{1,0:T(8,128)(2,1)S(1)}, u32[]{:S(2)}, u32[]{:S(2)}) collective-permute-start(bf16[272,256]{1,0:T(8,128)(2,1)} %get-tuple-element.38.d0), channel_id=1, source_target_pairs={{0,1},{1,0},{2,3},{3,2},{4,5},{5,4},{6,7},{7,6},{8,9},{9,8},{10,11... | collective-permute-start | bytes 417800 | tf_op jit(solution)/shard_map/ppermute | solution.py:399
  86.5 14.2 %copy-start.2 = (bf16[272,256]{1,0:T(8,128)(2,1)}, bf16[272,256]{1,0:T(8,128)(2,1)S(1)}, u32[]{:S(2)}) copy-start(bf16[272,256]{1,0:T(8,128)(2,1)S(1)} %collective-permute-done.15.d2) | copy-start | bytes 417796
  86.5 14.2 %collective-permute-start.16 = (bf16[272,256]{1,0:T(8,128)(2,1)S(1)}, bf16[272,256]{1,0:T(8,128)(2,1)S(1)}, u32[]{:S(2)}, u32[]{:S(2)}) collective-permute-start(bf16[272,256]{1,0:T(8,128)(2,1)S(1)} %collective-permute-done.15.d2), channel_id=1, source_target_pairs={{0,1},{1,0},{2,3},{3,2},{4,5},{5,4},{6,7},{7,6},{8,9},{9,8},{10,11... | collective-permute-start | bytes 417800 | tf_op jit(solution)/shard_map/ppermute | solution.py:399
  88.7 3.0 %copy-start.4 = (bf16[272,256]{1,0:T(8,128)(2,1)}, bf16[272,256]{1,0:T(8,128)(2,1)S(1)}, u32[]{:S(2)}) copy-start(bf16[272,256]{1,0:T(8,128)(2,1)S(1)} %collective-permute-done.17.d1) | copy-start | bytes 417796
  91.7 0.7 copy-start.6
  100.7 0.7 copy-start.3
  101.3 0.6 copy-start.5
  110.6 2.7 %collective-permute-start.20 = (bf16[1024,128]{1,0:T(8,128)(2,1)}, bf16[1024,128]{1,0:T(8,128)(2,1)S(1)}, u32[]{:S(2)}, u32[]{:S(2)}) collective-permute-start(bf16[1024,128]{1,0:T(8,128)(2,1)} %get-tuple-element.41), channel_id=1, source_target_pairs={{0,4},{4,0},{8,12},{12,8},{1,5},{5,1},{9,13},{13,9},{2,6},{6,2},{1... | collective-permute-start | bytes 786440 | tf_op jit(solution)/shard_map/ppermute | solution.py:482
  110.6 1.7 %collective-permute-start.8 = (f32[256,128]{1,0:T(8,128)S(1)}, f32[256,128]{1,0:T(8,128)S(1)}, u32[]{:S(2)}, u32[]{:S(2)}) collective-permute-start(f32[256,128]{1,0:T(8,128)S(1)} %copy-done.16), channel_id=1, source_target_pairs={{0,4},{4,0},{8,12},{12,8},{1,5},{5,1},{9,13},{13,9},{2,6},{6,2},{1... | collective-permute-start | bytes 393224 | tf_op jit(solution)/shard_map/ppermute | solution.py:477
  111.1 1.4 %collective-permute-start.13 = (f32[256,128]{1,0:T(8,128)S(1)}, f32[256,128]{1,0:T(8,128)S(1)}, u32[]{:S(2)}, u32[]{:S(2)}) collective-permute-start(f32[256,128]{1,0:T(8,128)S(1)} %copy-done.17), channel_id=1, source_target_pairs={{0,4},{4,0},{8,12},{12,8},{1,5},{5,1},{9,13},{13,9},{2,6},{6,2},{1... | collective-permute-start | bytes 393224 | tf_op jit(solution)/shard_map/ppermute | solution.py:477

commit v2 on v0

v2 whole, which is shorter than its diff:
```python
import functools

import jax
import jax.numpy as jnp
from jax import lax
from jax.experimental import pallas as pl
from jax.experimental.pallas import tpu as pltpu
from jax.sharding import PartitionSpec as P

HALO = 16
CHUNKS = 2
VMEM_BYTES = 20 << 20


def carried_in(array, axis, join, neutral):
    count = lax.axis_size(axis)
    place = lax.axis_index(axis)
    ahead = count - 1 - place
    gathered = jax.tree.map(
        lambda a, kind: lax.all_gather(a.astype(kind), axis),
        array,
        jax.tree.map(lambda a: jnp.bfloat16 if a.dtype == jnp.float32 else a.dtype, array),
    )
    state = jax.tree.map(lambda a, e: jnp.zeros_like(a) + jnp.asarray(e, a.dtype), array, neutral)

    def one(hop, state):
        source = count - 1 - hop
        return join(
            state,
            jax.tree.map(
                lambda a, own: lax.dynamic_index_in_dim(a, source, 0, False).astype(own.dtype),
                gathered,
                array,
            ),
        )

    return lax.fori_loop(0, ahead, one, state)


def from_behind(array, axis, by):
    count = lax.axis_size(axis)
    pairs = [(i, i + by) for i in range(count) if 0 <= i + by < count]
    return lax.ppermute(array, axis, pairs)


def lag_kernels(weights, pattern, cluster, first_row):
    local_rows = weights.shape[1]
    own_labels = lax.dynamic_slice_in_dim(cluster, first_row, local_rows, 0)
    labels = jnp.arange(pattern.shape[1], dtype=jnp.int32)
    row_onehot = (own_labels[:, None] == labels[None, :]).astype(jnp.bfloat16)
    column_onehot = (labels[:, None] == cluster[None, :]).astype(jnp.bfloat16)
    kernels = []
    for lag_index in range(weights.shape[0]):
        picked = jnp.dot(
            row_onehot, pattern[lag_index].astype(jnp.bfloat16), preferred_element_type=jnp.float32
        )
        table = jnp.dot(
            picked.astype(jnp.bfloat16), column_onehot, preferred_element_type=jnp.float32
        )
        kernels.append(weights[lag_index] * table.astype(jnp.bfloat16))
    return kernels


def correlate(kernels, extended):
    length = extended.shape[1] - len(kernels) + 1
    running = None
    for lag_index in range(len(kernels)):
        product_term = lax.dot_general(
            kernels[lag_index],
            extended[:, lag_index : lag_index + length],
            (((0,), (0,)), ((), ())),
            preferred_element_type=jnp.float32,
        )
        running = product_term if running is None else running + product_term
    return running


def reconstruct(kernels, extended):
    number_of_lags = len(kernels)
    length = extended.shape[1] - number_of_lags + 1
    running = None
    for lag_index in range(number_of_lags):
        offset = number_of_lags - 1 - lag_index
        product_term = jnp.dot(
            kernels[lag_index],
            extended[:, offset : offset + length],
            preferred_element_type=jnp.float32,
        )
        running = product_term if running is None else running + product_term
    return running


def chain_step(earlier, later):
    return (later[0] * earlier[0], later[1] + later[0] * earlier[1])


def block_recurrence(keep_fraction, inflow):
    def advance(carry, pieces):
        kept_now, state_now = carry
        keep, more = pieces
        state_now = keep * state_now + more
        kept_now = keep * kept_now
        return ((kept_now, state_now), (kept_now, state_now))

    elements = keep_fraction.shape[0]
    start = (jnp.ones((elements,), jnp.float32), jnp.zeros((elements,), jnp.float32))
    _, outputs = lax.scan(advance, start, (keep_fraction.T, inflow.T), reverse=True)
    return (outputs[0].T, outputs[1].T)


def general(
    traces,
    weights,
    pattern,
    cluster,
    element_damping_rate,
    local_step_length,
    housing_keep_share,
    admittance,
):
    local_rows = traces.shape[0]
    length = traces.shape[1]
    number_of_lags = weights.shape[0]
    first_row = lax.axis_index("row") * local_rows
    kernels = lag_kernels(weights, pattern, cluster, first_row)
    trailing = from_behind(traces[:, : number_of_lags - 1], "tm", -1)
    extended = jnp.concatenate([traces, trailing], 1)
    adjoint_sum = lax.psum(correlate(kernels, extended).astype(jnp.bfloat16), "row").astype(
        jnp.float32
    )
    spent = element_damping_rate[:, None] * local_step_length[None, :]
    keep_fraction = jnp.exp(-spent) * housing_keep_share[None, :]
    inflow = jnp.sqrt(-jnp.expm1(-2.0 * spent)) * adjoint_sum
    retained, partial_state = block_recurrence(keep_fraction, inflow)
    neutral = (jnp.ones_like(retained[:, 0]), jnp.zeros_like(partial_state[:, 0]))
    incoming = carried_in((retained[:, 0], partial_state[:, 0]), "tm", chain_step, neutral)
    state = partial_state + retained * incoming[1][:, None]
    driving = (admittance[:, None] * state).astype(jnp.bfloat16)
    leading = from_behind(driving[:, length - number_of_lags + 1 :], "tm", 1)
    pressure = reconstruct(kernels, jnp.concatenate([leading, driving], 1))
    state = lax.dynamic_slice_in_dim(state, first_row, local_rows, 0)
    return (state, pressure.astype(jnp.bfloat16))


def setup_kernel(
    traces_in,
    length_in,
    share_in,
    pattern_in,
    cluster_in,
    edge,
    clocks,
    columns,
    bits,
    traces,
    turned,
    pattern,
    cluster,
    ready,
):
    rows, length = traces.shape
    lags, kinds, _ = pattern.shape
    row, odd = lax.axis_index("row"), lax.axis_index("tm") % 2
    moves = (
        (traces_in, traces),
        (length_in, clocks.at[0:1, :]),
        (share_in, clocks.at[1:2, :]),
        (pattern_in, pattern),
        (cluster_in, cluster),
    )
    clocks[...] = jnp.zeros_like(clocks)
    copies = [
        pltpu.make_async_copy(source, target, ready.at[index])
        for index, (source, target) in enumerate(moves)
    ]
    for copy in copies:
        copy.start()
    for copy in copies:
        copy.wait()
    turned[:, 0:rows] = traces[...].astype(jnp.float32).T
    turned[:, rows:] = jnp.zeros((length, 128), jnp.float32)
    turned[:, rows : rows + 8] = clocks[...].T
    edge[...] = turned[pl.ds(pl.multiple_of(odd * (length - HALO), HALO), HALO), :]

    bits[...] = jnp.int32(1) << cluster[...]
    labels = cluster[:, pl.ds(pl.multiple_of(row * rows, rows), rows)]
    hit = lax.broadcasted_iota(jnp.int32, (kinds, rows), 0) == labels
    places = lax.broadcasted_iota(jnp.int32, (kinds, pattern.shape[2]), 1)
    found = []
    for lag in range(lags):
        word = (pattern[lag] << places).sum(1, keepdims=True)
        found.append(jnp.where(hit, word, 0).sum(0, keepdims=True))
    found = jnp.concatenate(found + [jnp.zeros((8 - lags, rows), jnp.int32)], 0)
    columns[...] = found.T


def mask_kernel(chunk, columns, bits, weights, kernels, spread, arrived):
    lags, rows, _ = weights.shape
    unit = kernels.shape[1] // 4
    row, half = lax.axis_index("row"), lax.axis_index("tm") % 2

    def start_of(slot):
        owner = jnp.bitwise_xor(row, slot)
        return pl.multiple_of(((owner * 2 + half) * CHUNKS + chunk) * unit, unit)

    def fetch(lag, slot):
        return pltpu.make_async_copy(
            weights.at[lag, :, pl.ds(start_of(slot), unit)],
            kernels.at[pl.ds(lag * rows, rows), pl.ds(slot * unit, unit)],
            arrived.at[slot, lag],
        )

    blocks = [(lag, slot) for lag in range(lags) for slot in range(4)]
    for block in blocks:
        fetch(*block).start()
    picked = [bits[:, pl.ds(start_of(slot), unit)] for slot in range(4)]
    for lag, slot in blocks:
        if slot == 0:
            spread[...] = jnp.broadcast_to(columns[:, lag : lag + 1], (rows, 128))
        fetch(lag, slot).wait()
        for at in range(0, unit, 128):
            place = slice(lag * rows, lag * rows + rows)
            part = slice(slot * unit + at, slot * unit + at + 128)
            weight = kernels[place, part]
            keep = (spread[...] & picked[slot][:, at : at + 128]) != 0
            kernels[place, part] = jnp.where(keep, weight, jnp.zeros_like(weight))


def correlate_kernel(own, partner_in, near, far, kernels, *refs):
    *outs, lagged, steps, traces, partner, ready = refs
    rows, length = traces.shape
    window = lagged.shape[0]
    lags = lagged.shape[1] // rows
    unit = outs[0].shape[1]
    half = lax.axis_index("tm") % 2
    copies = [
        pltpu.make_async_copy(own, traces, ready.at[0]),
        pltpu.make_async_copy(partner_in, partner, ready.at[1]),
    ]
    for copy in copies:
        copy.start()
    odd = half == 1
    first = pl.multiple_of(HALO + half * length, HALO)
    second = pl.multiple_of(HALO + (1 - half) * length, HALO)
    steps[0:HALO, :] = jnp.where(odd, far[:, 0:rows], near[:, 0:rows])
    steps[window : window + HALO, :] = jnp.where(odd, near[:, 0:rows], far[:, 0:rows])
    copies[0].wait()
    steps[pl.ds(first, length), :] = traces[...].astype(jnp.float32).T
    copies[1].wait()
    steps[pl.ds(second, length), :] = partner[...].astype(jnp.float32).T
    for lag in range(lags):
        part = slice(lag * rows, lag * rows + rows)
        lagged[:, part] = steps[lag : lag + window, :].astype(jnp.bfloat16)
    multiply(lagged, kernels, outs)


def correlate_again_kernel(lagged, kernels, after, *outs):
    multiply(lagged, kernels, outs)


def pair_kernel(mine, theirs, out):
    out[...] = (mine[...].astype(jnp.float32) + theirs[...].astype(jnp.float32)).astype(out.dtype)


def multiply(lagged, kernels, outs):
    unit = outs[0].shape[1]
    for low in (0, 2):
        product = jnp.dot(
            lagged[...],
            kernels[:, low * unit : low * unit + 2 * unit],
            preferred_element_type=jnp.float32,
        ).astype(jnp.bfloat16)
        outs[low][...] = product[:, :unit]
        outs[low + 1][...] = product[:, unit:]


def one_less_exp(y):
    series = jnp.ones_like(y)
    for k in range(9, 1, -1):
        series = 1.0 - series * y * (1.0 / k)
    return jnp.where(y < 0.5, y * series, 1.0 - jnp.exp(-y))


def factors_kernel(clocks, partner_clocks, near, far, rate, *refs):
    *outs, columns = refs
    chunks = len(outs)
    _, window, unit = outs[0].shape
    length = clocks.shape[1]
    rows = near.shape[1] - 128
    row, half = lax.axis_index("row"), lax.axis_index("tm") % 2
    first = pl.multiple_of(HALO + half * length, HALO)
    second = pl.multiple_of(HALO + (1 - half) * length, HALO)
    columns[0:HALO, :] = jnp.where(half == 1, far[:, rows : rows + 8], near[:, rows : rows + 8])
    columns[pl.ds(first, length), :] = clocks[...].T
    columns[pl.ds(second, length), :] = partner_clocks[...].T
    index = lax.broadcasted_iota(jnp.int32, (window, unit), 0) & 7
    for chunk, out in enumerate(outs):
        start = pl.multiple_of(((row * 2 + half) * chunks + chunk) * unit, unit)
        spent = columns[:, 0:1] * rate[:, pl.ds(start, unit)]
        out[0] = jnp.sqrt(one_less_exp(2.0 * spent))
        kept = jnp.exp(-spent) * columns[:, 1:2]
        for slot, shift in ((1, 1), (2, 2), (3, 4)):
            inside = index < 8 - shift
            out[slot] = jnp.where(inside, kept, 0.0)
            kept = jnp.where(inside, kept * pltpu.roll(kept, window - shift, 0), kept)
        out[4] = kept
        carry = jnp.ones((1, unit), jnp.float32)
        for group in range(window // 8 - 1, -1, -1):
            block = kept[group * 8 : group * 8 + 8] * carry
            out[5, group * 8 : group * 8 + 8, :] = block
            carry = block[0:1]


def recurrence_kernel(*refs):
    terms = refs[: 4 * CHUNKS]
    partials, first = refs[4 * CHUNKS : -1], refs[-1]
    for chunk in range(CHUNKS):
        own, direct, paired, factors = terms[4 * chunk : 4 * chunk + 4]
        window, unit = own.shape
        total = (
            own[...].astype(jnp.float32)
            + direct[...].astype(jnp.float32)
            + paired[...].astype(jnp.float32)
        )
        state = factors[0] * total
        for slot, shift in ((1, 1), (2, 2), (3, 4)):
            state = state + factors[slot] * pltpu.roll(state, window - shift, 0)
        carry = jnp.zeros((1, unit), jnp.float32)
        for group in range(window // 8 - 1, -1, -1):
            rows = slice(group * 8, group * 8 + 8)
            block = state[rows] + factors[4, rows, :] * carry
            partials[chunk][rows, :] = block
            carry = block[0:1]
            if group * 8 == HALO:
                first[chunk] = jnp.broadcast_to(carry, (8, unit))


def finish_kernel(incoming, admittance, *refs):
    given, (*outs, states) = refs[: 2 * CHUNKS], refs[2 * CHUNKS :]
    drives, mine, theirs = outs[:CHUNKS], outs[CHUNKS], outs[CHUNKS + 1]
    window, unit = states.shape
    length = mine.shape[1]
    row, half = lax.axis_index("row"), lax.axis_index("tm") % 2
    first = pl.multiple_of(HALO + half * length, HALO)
    second = pl.multiple_of(HALO + (1 - half) * length, HALO)
    for chunk in range(CHUNKS):
        partial, factors = given[2 * chunk : 2 * chunk + 2]
        start = pl.multiple_of(((row * 2 + half) * CHUNKS + chunk) * unit, unit)
        state = partial[...] + factors[5] * incoming[chunk, 0:1, :]
        drives[chunk][...] = (admittance[:, pl.ds(start, unit)] * state).astype(jnp.bfloat16)
        states[...] = state
        part = slice(chunk * unit, chunk * unit + unit)
        mine[part, :] = states[pl.ds(first, length), :].T
        theirs[part, :] = states[pl.ds(second, length), :].T


def reconstruct_kernel(last, d0, d1, d2, d3, kernels, *refs):
    if last:
        before, keep, send, total, steps, lagged = refs
    else:
        total, steps, lagged = refs
    lags, width, _ = lagged.shape
    unit = d0.shape[1]
    rows = total.shape[0]
    for slot, drive in enumerate((d0, d1, d2, d3)):
        steps[:, slot * unit : slot * unit + unit] = drive[...].astype(jnp.float32)
    for lag in range(lags):
        lagged[lag] = steps[HALO - lag : HALO - lag + width, :].astype(jnp.bfloat16)
    added = before[...] if last else None
    for lag in range(lags):
        term = lax.dot_general(
            kernels[lag * rows : lag * rows + rows, :],
            lagged[lag],
            (((1,), (1,)), ((), ())),
            preferred_element_type=jnp.float32,
        )
        added = term if added is None else added + term
    total[...] = added
    if last:
        length = width // 2
        half = lax.axis_index("tm") % 2
        keep[...] = total[:, pl.ds(pl.multiple_of(half * length, length), length)]
        send[...] = total[:, pl.ds(pl.multiple_of((1 - half) * length, length), length)].astype(
            send.dtype
        )


def call(kernel, name, in_specs, out_specs, out_shape, scratch, flops, moved):
    return pl.pallas_call(
        kernel,
        in_specs=in_specs,
        out_specs=out_specs,
        out_shape=out_shape,
        scratch_shapes=scratch,
        cost_estimate=pl.CostEstimate(flops=flops, bytes_accessed=moved, transcendentals=0),
        compiler_params=pltpu.CompilerParams(vmem_limit_bytes=VMEM_BYTES),
        name=name,
    )


def paired(
    traces,
    weights,
    pattern,
    cluster,
    element_damping_rate,
    local_step_length,
    housing_keep_share,
    admittance,
):
    rows, length = traces.shape
    lags = weights.shape[0]
    window = HALO + 2 * length
    unit = rows // (2 * CHUNKS)
    half = lax.axis_index("tm") % 2
    odd = half == 1
    f32, bf16 = jnp.float32, jnp.bfloat16
    tm_count = lax.axis_size("tm")
    swap = [(i, i ^ 1) for i in range(tm_count)]
    near = [(i, i + 1 if i % 2 else i - 1) for i in range(tm_count)]
    near = [(i, j) for i, j in near if 0 <= j < tm_count]
    far = [(i, i + 2 if i % 2 else i - 2) for i in range(tm_count)]
    far = [(i, j) for i, j in far if 0 <= j < tm_count]
    vmem = pl.BlockSpec(memory_space=pltpu.VMEM)

    hbm = pl.BlockSpec(memory_space=pltpu.HBM)
    barrier = lax.optimization_barrier

    def held(array):
        return pltpu.with_memory_space_constraint(array, pltpu.HBM)

    any_where = pl.BlockSpec(memory_space=pl.ANY)
    edge, clocks, columns, bits = call(
        setup_kernel,
        "setup",
        [hbm] * 5,
        [vmem] * 4,
        [
            jax.ShapeDtypeStruct((HALO, rows + 128), f32),
            jax.ShapeDtypeStruct((8, length), f32),
            jax.ShapeDtypeStruct((rows, 8), jnp.int32),
            jax.ShapeDtypeStruct((1, cluster.shape[0]), jnp.int32),
        ],
        [
            pltpu.VMEM((rows, length), bf16),
            pltpu.VMEM((length, rows + 128), f32),
            pltpu.VMEM(pattern.shape, jnp.int32),
            pltpu.VMEM((1, cluster.shape[0]), jnp.int32),
            pltpu.SemaphoreType.DMA((5,)),
        ],
        rows * length * 4,
        rows * length * 2,
    )(
        held(traces),
        held(local_step_length[None]),
        held(housing_keep_share[None]),
        held(pattern),
        held(cluster[None]),
    )
    partner_clocks = lax.ppermute(clocks, "tm", swap)
    own_traces, _ = barrier((traces, clocks))
    partner = lax.ppermute(own_traces, "tm", swap)
    got_near = lax.ppermute(edge, "tm", near)
    got_far = lax.ppermute(edge, "tm", far)

    strip = jax.ShapeDtypeStruct((window, unit), bf16)
    share_bytes = 4 * lags * rows * unit * 2
    share_flops = 2 * 4 * lags * rows * unit * window

    def chosen(chunk, columns):
        return call(
            functools.partial(mask_kernel, chunk),
            "mask",
            [vmem] * 2 + [hbm],
            vmem,
            pltpu.VMEM((lags * rows, 4 * unit), bf16),
            [pltpu.VMEM((rows, 128), jnp.int32), pltpu.SemaphoreType.DMA((4, lags))],
            share_bytes,
            share_bytes,
        )(columns, bits, weights)

    def correlated(kernels):
        *strips, lagged = call(
            correlate_kernel,
            "correlate",
            [hbm] * 2 + [vmem] * 3,
            [vmem] * 5,
            [strip] * 4 + [pltpu.VMEM((window, lags * rows), bf16)],
            [
                pltpu.VMEM((window + HALO, rows), f32),
                pltpu.VMEM((rows, length), bf16),
                pltpu.VMEM((rows, length), bf16),
                pltpu.SemaphoreType.DMA((2,)),
            ],
            share_flops,
            share_bytes // 2,
        )(held(traces), partner, got_near, got_far, kernels)
        return strips, lagged

    def correlated_again(lagged, kernels, after):
        return call(
            correlate_again_kernel,
            "correlate",
            [vmem] * 2 + [any_where],
            [vmem] * 4,
            [strip] * 4,
            [],
            share_flops,
            share_bytes // 2,
        )(lagged, kernels, after)

    def added(mine, theirs):
        return call(
            pair_kernel, "pair", [vmem] * 2, vmem, strip, [], window * unit, window * unit * 6
        )(mine, theirs)

    def over_row(array, by):
        return lax.ppermute(array, "row", [(i, i ^ by) for i in range(4)])

    def factored(clocks):
        return call(
            factors_kernel,
            "factors",
            [vmem] * 5,
            [vmem] * CHUNKS,
            [jax.ShapeDtypeStruct((6, window, unit), f32)] * CHUNKS,
            [pltpu.VMEM((window, 8), f32)],
            CHUNKS * window * unit * 100,
            CHUNKS * window * unit * 24,
        )(clocks, partner_clocks, got_near, got_far, element_damping_rate[None])

    def recurrence(parts, factors):
        given = [x for part, factor in zip(parts, factors) for x in (*part, factor)]
        *partials, first = call(
            recurrence_kernel,
            "recurrence",
            [vmem] * len(given),
            [vmem] * (CHUNKS + 1),
            [jax.ShapeDtypeStruct((window, unit), f32)] * CHUNKS
            + [jax.ShapeDtypeStruct((CHUNKS, 8, unit), f32)],
            [],
            CHUNKS * window * unit * 20,
            CHUNKS * window * unit * 30,
        )(*given)
        return partials, first

    def finished(partials, incoming, factors):
        given = [x for pair in zip(partials, factors) for x in pair]
        piece = jax.ShapeDtypeStruct((CHUNKS * unit, length), f32)
        *drives, mine, theirs = call(
            finish_kernel,
            "finish",
            [vmem] * (2 + len(given)),
            [vmem] * (CHUNKS + 2),
            [strip] * CHUNKS + [piece] * 2,
            [pltpu.VMEM((window, unit), f32)],
            CHUNKS * window * unit * 10,
            CHUNKS * window * unit * 16,
        )(incoming, admittance[None], *given)
        return drives, mine, theirs

    def reconstructed(drives, kernels, before):
        last = before is not None
        scratch = [
            pltpu.VMEM((window, 4 * unit), f32),
            pltpu.VMEM((lags, 2 * length, 4 * unit), bf16),
        ]
        out_shape = jax.ShapeDtypeStruct((rows, 2 * length), f32)
        if last:
            out_shape = [
                jax.ShapeDtypeStruct((rows, length), f32),
                jax.ShapeDtypeStruct((rows, length), bf16),
            ]
            scratch = [pltpu.VMEM((rows, 2 * length), f32)] + scratch
        return call(
            functools.partial(reconstruct_kernel, last),
            "reconstruct",
            [vmem] * (6 if last else 5),
            [vmem] * 2 if last else vmem,
            out_shape,
            scratch,
            share_flops,
            share_bytes // 2,
        )(*drives, kernels, *([before] if last else []))

    kernels = [chosen(0, columns)]
    strips_a, lagged = correlated(kernels[0])
    s3 = over_row(strips_a[3], 1)
    direct_a = over_row(strips_a[1], 1)
    late_columns, _ = barrier((columns, strips_a[0]))
    kernels.append(chosen(1, late_columns))
    pair_a = added(strips_a[2], s3)
    paired_a = over_row(pair_a, 2)
    strips_b = correlated_again(lagged, kernels[1], pair_a)
    pair_b = added(strips_b[2], over_row(strips_b[3], 1))
    paired_b = over_row(pair_b, 2)
    o1, _ = barrier((strips_b[1], pair_b))
    direct_b = over_row(o1, 1)
    parts = [(strips_a[0], direct_a, paired_a), (strips_b[0], direct_b, paired_b)]
    factors = factored(clocks)
    partials, first = recurrence(parts, factors)
    incoming = lax.ppermute(first, "tm", [(i, i - 2) for i in range(2, tm_count)])
    owned, mine, theirs = finished(partials, incoming, factors)
    theirs = lax.ppermute(theirs, "tm", swap)
    drives = []
    for drive in owned:
        d2 = over_row(drive, 2)
        drives.append((drive, over_row(drive, 1), d2, over_row(d2, 1)))
    total = None
    for chunk in range(CHUNKS):
        total = reconstructed(drives[chunk], kernels[chunk], total)
    keep, send = total
    pressure = keep + lax.ppermute(send, "tm", swap).astype(f32)
    state = jnp.where(
        odd, jnp.concatenate([theirs, mine], 0), jnp.concatenate([mine, theirs], 0)
    )
    return (state, pressure.astype(bf16))


def local(traces, weights, pattern, *rest):
    rows, length = traces.shape
    fits = (
        lax.axis_size("row") == 4
        and lax.axis_size("tm") == 4
        and length == 128
        and rows % (256 * CHUNKS) == 0
        and weights.shape[0] <= 8
        and pattern.shape[1] <= 32
    )
    return (paired if fits else general)(traces, weights, pattern, *rest)


def solution(mesh):
    placed = (P("row", ("group", "tm")), P(None, "row", None), P(), P(), P(), P("tm"), P("tm"), P())
    return jax.shard_map(
        local,
        mesh=mesh,
        in_specs=placed,
        out_specs=(P("row", ("group", "tm")), P("row", ("group", "tm"))),
        check_vma=False,
    )
```

time: 237 us -> 76.5 us (0.32)
  local copies, waits for them, and re-layouts: 77 us -> 0.01 us
  matrix products: 64.9 us -> 0 us
  waiting for transfers between devices: 53.6 us -> 23.4 us
  Pallas kernels: 0 us -> 23.7 us
  starting transfers between devices: 3.49 us -> 26.7 us
  between operations: 14.4 us -> 0.82 us
  blocking collectives: 10.5 us -> 0 us
  other arithmetic: 10.3 us -> 1.59 us
    dot_general x12 -> x0, matrix products: 64.9 us -> none  [the longest x4 29.6 us: lag_kernels(): jnp.dot(picked.astype(jnp.bfloat16), column_onehot, preferred_element_typ...]
    slice x35 -> x0, local copies, waits for them, and re-layouts: 54.2 us -> none  [the longest x16 27.4 us: advance(): kept_now = keep_block[inner] * kept_now]
    psum x1 -> x0, waiting for transfers between devices: 53.6 us -> none  [local(): lax.psum(correlate(kernels, extended).astype(jnp.bfloat16), 'row')]
    pallas_call x0 -> x12, Pallas kernels: none -> 23.7 us  [the longest x2 8.63 us: chosen(): call(functools.partial(mask_kernel, chunk), 'mask', [vmem] * 2 + [hbm], v...]
    ppermute x2 -> x19, waiting for transfers between devices: 0.01 us -> 23.4 us  [the longest x12 15.7 us: over_row(): return lax.ppermute(array, 'row', [(i, i ^ by) for i in range(4)])]
    ppermute x2 -> x19, starting transfers between devices: 3.45 us -> 26.7 us  [the longest x12 22.7 us: over_row(): return lax.ppermute(array, 'row', [(i, i ^ by) for i in range(4)])]
    dynamic_update_slice x16 -> x0, local copies, waits for them, and re-layouts: 10.7 us -> none  [block_recurrence(): lax.scan(advance, start, (keep_rows, inflow_rows), reverse=True)]
    all_gather x2 -> x0, blocking collectives: 10.5 us -> none  [carried_in(): lax.all_gather(a.astype(kind), axis)]
  transfers between devices with their start and end apart: 3 -> 19, of which waited for: 1 -> 10; matrix products, arithmetic and copies ran while one was open for 17% -> 1% of each run, Pallas kernels for 0% -> 20%
where the time goes in v2:
time: 76.5 us; the launch traced here: 76.3 us
  starting transfers between devices  26.7 us (35%)
  Pallas kernels  23.7 us (31%)
  waiting for transfers between devices  23.4 us (31%)
  other arithmetic  1.59 us (2%)
  between operations  0.82 us (1%)
    ppermute x12, starting transfers between devices, over_row(): return lax.ppermute(array, 'row', [(i, i ^ by) for i in range(4)])  22.7 us
    ppermute x12, waiting for transfers between devices, over_row(): return lax.ppermute(array, 'row', [(i, i ^ by) for i in range(4)])  15.7 us
    pallas_call x2, Pallas kernels, chosen(): call(functools.partial(mask_kernel, chunk), 'mask', [vmem] * 2 + [hbm], v...  8.63 us
    pallas_call x2, Pallas kernels, reconstructed(): call(functools.partial(reconstruct_kernel, last), 'reconstruct', [vmem] *...  4.93 us
    ppermute x1, waiting for transfers between devices, paired(): lax.ppermute(first, 'tm', [(i, i - 2) for i in range(2, tm_count)])  4.11 us
    pallas_call x1, Pallas kernels, correlated(): call(correlate_kernel, 'correlate', [hbm] * 2 + [vmem] * 3, [vmem] * 5, [...  3.97 us
    pallas_call x1, Pallas kernels, correlated_again(): call(correlate_again_kernel, 'correlate', [vmem] * 2 + [any_where], [vmem...  2.52 us
    ppermute x1, waiting for transfers between devices, paired(): got_far = lax.ppermute(edge, 'tm', far)  1.75 us
  transfers between devices with their start and end apart: 19, of which 10 were waited for; matrix products, arithmetic and copies ran while one was open for 1% of the time, Pallas kernels for 20%

profile of v2, /device:TPU:0, one launch (start us, length us, event | category | flops | bytes accessed | tf_op | source)
XLA Modules:
  0.0 76.3 jit_solution(426480927492784889)
XLA Ops:
  0.6 1.4 %setup.1 = (f32[16,1152]{1,0:T(8,128)S(1)}, f32[8,128]{1,0:T(8,128)S(1)}, s32[1024,8]{1,0:T(8,128)S(1)}, s32[1,4096]{1,0:T(1,128)S(1)}) custom-call(bf16[1024,128]{1,0:T(8,128)(2,1)} %own.1, f32[1,128]{1,0:T(1,128)} %bitcast.8, f32[1,128]{1,0:T(1,128)} %bitcast.9, s32[4,32,32]{2,1,0:T(8,128)} %pattern_in.1, s32[1,4096]{1,0:T(1,128)} %bitcast.7), custom_call_target="tpu_custom_call" | custom-call | flops 524288 | bytes 262144 | tf_op jit(solution)/shard_map/setup/pallas_call | solution.py:433
  2.0 0.5 collective-permute-start
  2.5 0.7 collective-permute-start.1
  3.2 1.3 %collective-permute-start.2 = (f32[16,1152]{1,0:T(8,128)S(1)}, f32[16,1152]{1,0:T(8,128)S(1)}, u32[]{:S(2)}, u32[]{:S(2)}) collective-permute-start(f32[16,1152]{1,0:T(8,128)S(1)} %get-tuple-element.31), channel_id=1, source_target_pairs={{4,12},{8,0},{5,13},{9,1},{6,14},{10,2},{7,15},{11,3},{20,28},{24,... | collective-permute-start | bytes 221192 | tf_op jit(solution)/shard_map/ppermute | solution.py:464
  4.5 4.3 %mask.2.kernels = bf16[4096,1024]{1,0:T(8,128)(2,1)S(1)} custom-call(s32[1024,8]{1,0:T(8,128)S(1)} %get-tuple-element.40.columns, s32[1,4096]{1,0:T(1,128)S(1)} %get-tuple-element.33.bits, bf16[4,1024,4096]{2,1,0:T(8,128)(2,1)} %weights.3), custom_call_target="tpu_custom_call" | custom-call | flops 8388608 | bytes 8388608 | tf_op jit(solution)/shard_map/mask/pallas_call | solution.py:471
  8.8 0.0 collective-permute-done.1.near
  8.8 1.8 %collective-permute-done.2.far = f32[16,1152]{1,0:T(8,128)S(1)} collective-permute-done((f32[16,1152]{1,0:T(8,128)S(1)}, f32[16,1152]{1,0:T(8,128)S(1)}, u32[]{:S(2)}, u32[]{:S(2)}) %collective-permute-start.2) | collective-permute-done | bytes 73760 | tf_op jit(solution)/shard_map/ppermute | solution.py:464
  10.6 0.0 collective-permute-done.partner_in
  10.6 4.0 %correlate.2 = (bf16[272,256]{1,0:T(8,128)(2,1)S(1)}, bf16[272,256]{1,0:T(8,128)(2,1)S(1)}, bf16[272,256]{1,0:T(8,128)(2,1)S(1)}, bf16[272,256]{1,0:T(8,128)(2,1)S(1)}, bf16[272,4096]{1,0:T(8,128)(2,1)S(1)}) custom-call(bf16[1024,128]{1,0:T(8,128)(2,1)} %own.1, bf16[1024,128]{1,0:T(8,128)(2,1)S(1)} %collective-permute-done.partner_in, ...), custom_call_target="tpu_custom_call" | custom-call | flops 2281701376 | bytes 4194304 | tf_op jit(solution)/shard_map/correlate/pallas_call | solution.py:483
  14.5 2.3 %collective-permute-start.4 = (bf16[272,256]{1,0:T(8,128)(2,1)S(1)}, bf16[272,256]{1,0:T(8,128)(2,1)S(1)}, u32[]{:S(2)}, u32[]{:S(2)}) collective-permute-start(bf16[272,256]{1,0:T(8,128)(2,1)S(1)} %get-tuple-element.37), channel_id=1, source_target_pairs={{0,1},{1,0},{2,3},{3,2},{4,5},{5,4},{6,7},{7,6},{8,9},{9,8},{10,11... | collective-permute-start | bytes 417800 | tf_op jit(solution)/shard_map/ppermute | solution.py:518
  16.8 4.3 %mask.3.kernels = bf16[4096,1024]{1,0:T(8,128)(2,1)S(1)} custom-call(s32[1024,8]{1,0:T(8,128)S(1)} %get-tuple-element.40.columns, s32[1,4096]{1,0:T(1,128)S(1)} %get-tuple-element.33.bits, bf16[4,1024,4096]{2,1,0:T(8,128)(2,1)} %weights.3), custom_call_target="tpu_custom_call" | custom-call | flops 8388608 | bytes 8388608 | tf_op jit(solution)/shard_map/mask/pallas_call | solution.py:471
  21.1 0.0 copy-start.1
  21.1 0.0 copy-start
  21.2 0.0 collective-permute-done.4.theirs
  21.2 2.5 %correlate.3 = (bf16[272,256]{1,0:T(8,128)(2,1)S(1)}, bf16[272,256]{1,0:T(8,128)(2,1)S(1)}, bf16[272,256]{1,0:T(8,128)(2,1)S(1)}, bf16[272,256]{1,0:T(8,128)(2,1)S(1)}) custom-call(bf16[272,4096]{1,0:T(8,128)(2,1)S(1)} %get-tuple-element.39.lagged, bf16[4096,1024]{1,0:T(8,128)(2,1)S(1)} %mask.3.kernels, bf16[272,256]{1,0:T(8,128)(2,1)S(1)} %pair.2.after), custom_call_target="tpu_custom_call" | custom-call | flops 2281701376 | bytes 4194304 | tf_op jit(solution)/shard_map/correlate/pallas_call | solution.py:501
  23.7 1.7 %collective-permute-start.7 = (bf16[272,256]{1,0:T(8,128)(2,1)S(1)}, bf16[272,256]{1,0:T(8,128)(2,1)S(1)}, u32[]{:S(2)}, u32[]{:S(2)}) collective-permute-start(bf16[272,256]{1,0:T(8,128)(2,1)S(1)} %get-tuple-element.44), channel_id=1, source_target_pairs={{0,1},{1,0},{2,3},{3,2},{4,5},{5,4},{6,7},{7,6},{8,9},{9,8},{10,11... | collective-permute-start | bytes 417800 | tf_op jit(solution)/shard_map/ppermute | solution.py:518
  25.5 0.4 collective-permute-start.3
  25.8 2.7 %collective-permute-start.5 = (bf16[272,256]{1,0:T(8,128)(2,1)S(1)}, bf16[272,256]{1,0:T(8,128)(2,1)S(1)}, u32[]{:S(2)}, u32[]{:S(2)}) collective-permute-start(bf16[272,256]{1,0:T(8,128)(2,1)S(1)} %pair.2.after), channel_id=1, source_target_pairs={{0,2},{1,3},{2,0},{3,1},{4,6},{5,7},{6,4},{7,5},{8,10},{9,11},{10,... | collective-permute-start | bytes 417800 | tf_op jit(solution)/shard_map/ppermute | solution.py:518
  28.5 1.6 %collective-permute-done.7.theirs = bf16[272,256]{1,0:T(8,128)(2,1)S(1)} collective-permute-done((bf16[272,256]{1,0:T(8,128)(2,1)S(1)}, bf16[272,256]{1,0:T(8,128)(2,1)S(1)}, u32[]{:S(2)}, u32[]{:S(2)}) %collective-permute-start.7) | collective-permute-done | bytes 139296 | tf_op jit(solution)/shard_map/ppermute | solution.py:518
  30.1 2.0 %collective-permute-start.8 = (bf16[272,256]{1,0:T(8,128)(2,1)S(1)}, bf16[272,256]{1,0:T(8,128)(2,1)S(1)}, u32[]{:S(2)}, u32[]{:S(2)}) collective-permute-start(bf16[272,256]{1,0:T(8,128)(2,1)S(1)} %get-tuple-element.45), channel_id=1, source_target_pairs={{0,1},{1,0},{2,3},{3,2},{4,5},{5,4},{6,7},{7,6},{8,9},{9,8},{10,11... | collective-permute-start | bytes 417800 | tf_op jit(solution)/shard_map/ppermute | solution.py:518
  32.1 5.6 %collective-permute-start.9 = (bf16[272,256]{1,0:T(8,128)(2,1)S(1)}, bf16[272,256]{1,0:T(8,128)(2,1)S(1)}, u32[]{:S(2)}, u32[]{:S(2)}) collective-permute-start(bf16[272,256]{1,0:T(8,128)(2,1)S(1)} %pair.3), channel_id=1, source_target_pairs={{0,2},{1,3},{2,0},{3,1},{4,6},{5,7},{6,4},{7,5},{8,10},{9,11},{10,... | collective-permute-start | bytes 417800 | tf_op jit(solution)/shard_map/ppermute | solution.py:518
  37.7 0.0 collective-permute-start.6
  37.7 1.2 %collective-permute-done.6.partner_clocks = f32[8,128]{1,0:T(8,128)S(1)} collective-permute-done((f32[8,128]{1,0:T(8,128)S(1)}, f32[8,128]{1,0:T(8,128)S(1)}, u32[]{:S(2)}, u32[]{:S(2)}) %collective-permute-start.6) | collective-permute-done | bytes 4128 | tf_op jit(solution)/shard_map/ppermute | solution.py:460
  38.8 0.0 copy-done.1
  38.8 1.5 %factors.1 = (f32[6,272,256]{2,1,0:T(8,128)S(1)}, f32[6,272,256]{2,1,0:T(8,128)S(1)}) custom-call(f32[8,128]{1,0:T(8,128)S(1)} %get-tuple-element.29.clocks, f32[8,128]{1,0:T(8,128)S(1)} %collective-permute-done.6.partner_clocks, f32[16,1152]{1,0:T(8,128)S(1)} %collective-permute-done.1.near, f32[16,1152]{1,0:T(8,128)S(1)} %collective-permute-done.2.far, ...), custom_call_target="tpu_custom_call" | custom-call | flops 13926400 | bytes 3342336 | tf_op jit(solution)/shard_map/factors/pallas_call | solution.py:521
  40.3 0.0 collective-permute-done.3.refs_1_
  40.3 0.0 collective-permute-done.5.refs_2_
  40.3 1.7 %collective-permute-done.8.refs_5_ = bf16[272,256]{1,0:T(8,128)(2,1)S(1)} collective-permute-done((bf16[272,256]{1,0:T(8,128)(2,1)S(1)}, bf16[272,256]{1,0:T(8,128)(2,1)S(1)}, u32[]{:S(2)}, u32[]{:S(2)}) %collective-permute-start.8) | collective-permute-done | bytes 139296 | tf_op jit(solution)/shard_map/ppermute | solution.py:518
  42.0 0.0 collective-permute-done.9.refs_6_
  42.0 0.4 recurrence.1
  42.4 1.5 %collective-permute-start.10 = (f32[2,8,256]{2,1,0:T(8,128)S(1)}, f32[2,8,256]{2,1,0:T(8,128)S(1)}, u32[]{:S(2)}, u32[]{:S(2)}) collective-permute-start(f32[2,8,256]{2,1,0:T(8,128)S(1)} %get-tuple-element.47), channel_id=1, source_target_pairs={{8,0},{12,4},{9,1},{13,5},{10,2},{14,6},{11,3},{15,7},{24,16},{28,... | collective-permute-start | bytes 49160 | tf_op jit(solution)/shard_map/ppermute | solution.py:602
  43.9 4.1 %collective-permute-done.10.incoming = f32[2,8,256]{2,1,0:T(8,128)S(1)} collective-permute-done((f32[2,8,256]{2,1,0:T(8,128)S(1)}, f32[2,8,256]{2,1,0:T(8,128)S(1)}, u32[]{:S(2)}, u32[]{:S(2)}) %collective-permute-start.10) | collective-permute-done | bytes 16416 | tf_op jit(solution)/shard_map/ppermute | solution.py:602
  48.0 0.0 copy-done
  48.1 0.3 finish.1
  48.4 2.4 %collective-permute-start.16 = (bf16[272,256]{1,0:T(8,128)(2,1)S(1)}, bf16[272,256]{1,0:T(8,128)(2,1)S(1)}, u32[]{:S(2)}, u32[]{:S(2)}) collective-permute-start(bf16[272,256]{1,0:T(8,128)(2,1)S(1)} %get-tuple-element.53.d0), channel_id=1, source_target_pairs={{0,2},{1,3},{2,0},{3,1},{4,6},{5,7},{6,4},{7,5},{8,10},{9,11},{10,... | collective-permute-start | bytes 417800 | tf_op jit(solution)/shard_map/ppermute | solution.py:518
  50.7 0.6 collective-permute-start.13
  51.4 3.0 %collective-permute-start.15 = (bf16[272,256]{1,0:T(8,128)(2,1)S(1)}, bf16[272,256]{1,0:T(8,128)(2,1)S(1)}, u32[]{:S(2)}, u32[]{:S(2)}) collective-permute-start(bf16[272,256]{1,0:T(8,128)(2,1)S(1)} %get-tuple-element.53.d0), channel_id=1, source_target_pairs={{0,1},{1,0},{2,3},{3,2},{4,5},{5,4},{6,7},{7,6},{8,9},{9,8},{10,11... | collective-permute-start | bytes 417800 | tf_op jit(solution)/shard_map/ppermute | solution.py:518
  54.4 7.1 %collective-permute-done.16.d2 = bf16[272,256]{1,0:T(8,128)(2,1)S(1)} collective-permute-done((bf16[272,256]{1,0:T(8,128)(2,1)S(1)}, bf16[272,256]{1,0:T(8,128)(2,1)S(1)}, u32[]{:S(2)}, u32[]{:S(2)}) %collective-permute-start.16) | collective-permute-done | bytes 139296 | tf_op jit(solution)/shard_map/ppermute | solution.py:518
  61.4 0.0 collective-permute-start.17
  61.4 2.0 %collective-permute-start.12 = (bf16[272,256]{1,0:T(8,128)(2,1)S(1)}, bf16[272,256]{1,0:T(8,128)(2,1)S(1)}, u32[]{:S(2)}, u32[]{:S(2)}) collective-permute-start(bf16[272,256]{1,0:T(8,128)(2,1)S(1)} %get-tuple-element.52.d0), channel_id=1, source_target_pairs={{0,1},{1,0},{2,3},{3,2},{4,5},{5,4},{6,7},{7,6},{8,9},{9,8},{10,11... | collective-permute-start | bytes 417800 | tf_op jit(solution)/shard_map/ppermute | solution.py:518
  63.5 0.0 collective-permute-start.11
  63.5 0.0 collective-permute-done.13.d2
  63.5 0.1 collective-permute-start.14
  63.6 0.0 collective-permute-done.15.d1
  63.6 3.6 %collective-permute-done.17.d3 = bf16[272,256]{1,0:T(8,128)(2,1)S(1)} collective-permute-done((bf16[272,256]{1,0:T(8,128)(2,1)S(1)}, bf16[272,256]{1,0:T(8,128)(2,1)S(1)}, u32[]{:S(2)}, u32[]{:S(2)}) %collective-permute-start.17) | collective-permute-done | bytes 139296 | tf_op jit(solution)/shard_map/ppermute | solution.py:518
  67.1 2.4 %reconstruct.2.refs_0_ = f32[1024,256]{1,0:T(8,128)S(1)} custom-call(bf16[272,256]{1,0:T(8,128)(2,1)S(1)} %get-tuple-element.53.d0, bf16[272,256]{1,0:T(8,128)(2,1)S(1)} %collective-permute-done.15.d1, bf16[272,256]{1,0:T(8,128)(2,1)S(1)} %collective-permute-done.16.d2, bf16[272,256]{1,0:T(8,128)(2,1)S(1)} %collective-permute-done.17.d3, ...), custom_call_target="tpu_custom_call" | custom-call | flops 2281701376 | bytes 4194304 | tf_op jit(solution)/shard_map/reconstruct/pallas_call | solution.py:575
  69.5 0.3 collective-permute-done.12.d1
  69.9 1.5 %collective-permute-done.14.d3 = bf16[272,256]{1,0:T(8,128)(2,1)S(1)} collective-permute-done((bf16[272,256]{1,0:T(8,128)(2,1)S(1)}, bf16[272,256]{1,0:T(8,128)(2,1)S(1)}, u32[]{:S(2)}, u32[]{:S(2)}) %collective-permute-start.14) | collective-permute-done | bytes 139296 | tf_op jit(solution)/shard_map/ppermute | solution.py:518
  71.4 2.5 %reconstruct.3 = (f32[1024,128]{1,0:T(8,128)S(1)}, bf16[1024,128]{1,0:T(8,128)(2,1)S(1)}) custom-call(bf16[272,256]{1,0:T(8,128)(2,1)S(1)} %get-tuple-element.52.d0, bf16[272,256]{1,0:T(8,128)(2,1)S(1)} %collective-permute-done.12.d1, bf16[272,256]{1,0:T(8,128)(2,1)S(1)} %collective-permute-done.13.d2, bf16[272,256]{1,0:T(8,128)(2,1)S(1)} %collective-permute-done.14.d3, ...), custom_call_target="tpu_custom_call" | custom-call | flops 2281701376 | bytes 4194304 | tf_op jit(solution)/shard_map/reconstruct/pallas_call | solution.py:575
  73.9 0.1 collective-permute-start.18
  74.0 0.0 collective-permute-done.11
  74.0 0.8 %maximum_select_fusion = f32[1024,128]{1,0:T(8,128)} fusion(f32[512,128]{1,0:T(8,128)S(1)} %get-tuple-element.51, f32[512,128]{1,0:T(8,128)S(1)} %collective-permute-done.11, pred[]{:T(512)S(6)} %eq.5), kind=kLoop, calls=%fused_computation | loop fusion | flops 393216 | bytes 1048577 | tf_op jit(solution)/shard_map/jit(_where)/select_n | solution.py:614
  74.8 0.7 collective-permute-done.18
  75.5 0.8 add_convert_fusion
  (2 shorter events, 0.1 us)
Async XLA Ops:
  2.0 8.6 %collective-permute-start = (bf16[1024,128]{1,0:T(8,128)(2,1)}, bf16[1024,128]{1,0:T(8,128)(2,1)S(1)}, u32[]{:S(2)}, u32[]{:S(2)}) collective-permute-start(bf16[1024,128]{1,0:T(8,128)(2,1)} %own.1), channel_id=1, source_target_pairs={{0,4},{4,0},{8,12},{12,8},{1,5},{5,1},{9,13},{13,9},{2,6},{6,2},{1... | collective-permute-start | bytes 786440 | tf_op jit(solution)/shard_map/ppermute | solution.py:462
  2.5 6.3 %collective-permute-start.1 = (f32[16,1152]{1,0:T(8,128)S(1)}, f32[16,1152]{1,0:T(8,128)S(1)}, u32[]{:S(2)}, u32[]{:S(2)}) collective-permute-start(f32[16,1152]{1,0:T(8,128)S(1)} %get-tuple-element.31), channel_id=1, source_target_pairs={{4,8},{8,4},{5,9},{9,5},{6,10},{10,6},{7,11},{11,7},{20,24},{24,20... | collective-permute-start | bytes 221192 | tf_op jit(solution)/shard_map/ppermute | solution.py:463
  3.2 7.4 %collective-permute-start.2 = (f32[16,1152]{1,0:T(8,128)S(1)}, f32[16,1152]{1,0:T(8,128)S(1)}, u32[]{:S(2)}, u32[]{:S(2)}) collective-permute-start(f32[16,1152]{1,0:T(8,128)S(1)} %get-tuple-element.31), channel_id=1, source_target_pairs={{4,12},{8,0},{5,13},{9,1},{6,14},{10,2},{7,15},{11,3},{20,28},{24,... | collective-permute-start | bytes 221192 | tf_op jit(solution)/shard_map/ppermute | solution.py:464
  14.5 6.6 %collective-permute-start.4 = (bf16[272,256]{1,0:T(8,128)(2,1)S(1)}, bf16[272,256]{1,0:T(8,128)(2,1)S(1)}, u32[]{:S(2)}, u32[]{:S(2)}) collective-permute-start(bf16[272,256]{1,0:T(8,128)(2,1)S(1)} %get-tuple-element.37), channel_id=1, source_target_pairs={{0,1},{1,0},{2,3},{3,2},{4,5},{5,4},{6,7},{7,6},{8,9},{9,8},{10,11... | collective-permute-start | bytes 417800 | tf_op jit(solution)/shard_map/ppermute | solution.py:518
  21.1 17.7 %copy-start.1 = (f32[4096]{0:T(1024)S(1)}, f32[4096]{0:T(1024)}, u32[]{:S(2)}) copy-start(f32[4096]{0:T(1024)} %param.12) | copy-start | bytes 49156
  21.1 26.9 %copy-start = (f32[4096]{0:T(1024)S(1)}, f32[4096]{0:T(1024)}, u32[]{:S(2)}) copy-start(f32[4096]{0:T(1024)} %param.15) | copy-start | bytes 49156
  23.7 6.3 %collective-permute-start.7 = (bf16[272,256]{1,0:T(8,128)(2,1)S(1)}, bf16[272,256]{1,0:T(8,128)(2,1)S(1)}, u32[]{:S(2)}, u32[]{:S(2)}) collective-permute-start(bf16[272,256]{1,0:T(8,128)(2,1)S(1)} %get-tuple-element.44), channel_id=1, source_target_pairs={{0,1},{1,0},{2,3},{3,2},{4,5},{5,4},{6,7},{7,6},{8,9},{9,8},{10,11... | collective-permute-start | bytes 417800 | tf_op jit(solution)/shard_map/ppermute | solution.py:518
  25.5 14.8 %collective-permute-start.3 = (bf16[272,256]{1,0:T(8,128)(2,1)S(1)}, bf16[272,256]{1,0:T(8,128)(2,1)S(1)}, u32[]{:S(2)}, u32[]{:S(2)}) collective-permute-start(bf16[272,256]{1,0:T(8,128)(2,1)S(1)} %get-tuple-element.35), channel_id=1, source_target_pairs={{0,1},{1,0},{2,3},{3,2},{4,5},{5,4},{6,7},{7,6},{8,9},{9,8},{10,11... | collective-permute-start | bytes 417800 | tf_op jit(solution)/shard_map/ppermute | solution.py:518
  25.8 14.5 %collective-permute-start.5 = (bf16[272,256]{1,0:T(8,128)(2,1)S(1)}, bf16[272,256]{1,0:T(8,128)(2,1)S(1)}, u32[]{:S(2)}, u32[]{:S(2)}) collective-permute-start(bf16[272,256]{1,0:T(8,128)(2,1)S(1)} %pair.2.after), channel_id=1, source_target_pairs={{0,2},{1,3},{2,0},{3,1},{4,6},{5,7},{6,4},{7,5},{8,10},{9,11},{10,... | collective-permute-start | bytes 417800 | tf_op jit(solution)/shard_map/ppermute | solution.py:518
  30.1 11.9 %collective-permute-start.8 = (bf16[272,256]{1,0:T(8,128)(2,1)S(1)}, bf16[272,256]{1,0:T(8,128)(2,1)S(1)}, u32[]{:S(2)}, u32[]{:S(2)}) collective-permute-start(bf16[272,256]{1,0:T(8,128)(2,1)S(1)} %get-tuple-element.45), channel_id=1, source_target_pairs={{0,1},{1,0},{2,3},{3,2},{4,5},{5,4},{6,7},{7,6},{8,9},{9,8},{10,11... | collective-permute-start | bytes 417800 | tf_op jit(solution)/shard_map/ppermute | solution.py:518
  32.1 9.9 %collective-permute-start.9 = (bf16[272,256]{1,0:T(8,128)(2,1)S(1)}, bf16[272,256]{1,0:T(8,128)(2,1)S(1)}, u32[]{:S(2)}, u32[]{:S(2)}) collective-permute-start(bf16[272,256]{1,0:T(8,128)(2,1)S(1)} %pair.3), channel_id=1, source_target_pairs={{0,2},{1,3},{2,0},{3,1},{4,6},{5,7},{6,4},{7,5},{8,10},{9,11},{10,... | collective-permute-start | bytes 417800 | tf_op jit(solution)/shard_map/ppermute | solution.py:518
  37.7 1.2 %collective-permute-start.6 = (f32[8,128]{1,0:T(8,128)S(1)}, f32[8,128]{1,0:T(8,128)S(1)}, u32[]{:S(2)}, u32[]{:S(2)}) collective-permute-start(f32[8,128]{1,0:T(8,128)S(1)} %get-tuple-element.29.clocks), channel_id=1, source_target_pairs={{0,4},{4,0},{8,12},{12,8},{1,5},{5,1},{9,13},{13,9},{2,6},{6,2},{1... | collective-permute-start | bytes 12296 | tf_op jit(solution)/shard_map/ppermute | solution.py:460
  42.4 5.6 %collective-permute-start.10 = (f32[2,8,256]{2,1,0:T(8,128)S(1)}, f32[2,8,256]{2,1,0:T(8,128)S(1)}, u32[]{:S(2)}, u32[]{:S(2)}) collective-permute-start(f32[2,8,256]{2,1,0:T(8,128)S(1)} %get-tuple-element.47), channel_id=1, source_target_pairs={{8,0},{12,4},{9,1},{13,5},{10,2},{14,6},{11,3},{15,7},{24,16},{28,... | collective-permute-start | bytes 49160 | tf_op jit(solution)/shard_map/ppermute | solution.py:602
  48.4 13.1 %collective-permute-start.16 = (bf16[272,256]{1,0:T(8,128)(2,1)S(1)}, bf16[272,256]{1,0:T(8,128)(2,1)S(1)}, u32[]{:S(2)}, u32[]{:S(2)}) collective-permute-start(bf16[272,256]{1,0:T(8,128)(2,1)S(1)} %get-tuple-element.53.d0), channel_id=1, source_target_pairs={{0,2},{1,3},{2,0},{3,1},{4,6},{5,7},{6,4},{7,5},{8,10},{9,11},{10,... | collective-permute-start | bytes 417800 | tf_op jit(solution)/shard_map/ppermute | solution.py:518
  50.7 12.7 %collective-permute-start.13 = (bf16[272,256]{1,0:T(8,128)(2,1)S(1)}, bf16[272,256]{1,0:T(8,128)(2,1)S(1)}, u32[]{:S(2)}, u32[]{:S(2)}) collective-permute-start(bf16[272,256]{1,0:T(8,128)(2,1)S(1)} %get-tuple-element.52.d0), channel_id=1, source_target_pairs={{0,2},{1,3},{2,0},{3,1},{4,6},{5,7},{6,4},{7,5},{8,10},{9,11},{10,... | collective-permute-start | bytes 417800 | tf_op jit(solution)/shard_map/ppermute | solution.py:518
  51.4 12.2 %collective-permute-start.15 = (bf16[272,256]{1,0:T(8,128)(2,1)S(1)}, bf16[272,256]{1,0:T(8,128)(2,1)S(1)}, u32[]{:S(2)}, u32[]{:S(2)}) collective-permute-start(bf16[272,256]{1,0:T(8,128)(2,1)S(1)} %get-tuple-element.53.d0), channel_id=1, source_target_pairs={{0,1},{1,0},{2,3},{3,2},{4,5},{5,4},{6,7},{7,6},{8,9},{9,8},{10,11... | collective-permute-start | bytes 417800 | tf_op jit(solution)/shard_map/ppermute | solution.py:518
  61.4 5.7 %collective-permute-start.17 = (bf16[272,256]{1,0:T(8,128)(2,1)S(1)}, bf16[272,256]{1,0:T(8,128)(2,1)S(1)}, u32[]{:S(2)}, u32[]{:S(2)}) collective-permute-start(bf16[272,256]{1,0:T(8,128)(2,1)S(1)} %collective-permute-done.16.d2), channel_id=1, source_target_pairs={{0,1},{1,0},{2,3},{3,2},{4,5},{5,4},{6,7},{7,6},{8,9},{9,8},{10,11... | collective-permute-start | bytes 417800 | tf_op jit(solution)/shard_map/ppermute | solution.py:518
  61.4 8.4 %collective-permute-start.12 = (bf16[272,256]{1,0:T(8,128)(2,1)S(1)}, bf16[272,256]{1,0:T(8,128)(2,1)S(1)}, u32[]{:S(2)}, u32[]{:S(2)}) collective-permute-start(bf16[272,256]{1,0:T(8,128)(2,1)S(1)} %get-tuple-element.52.d0), channel_id=1, source_target_pairs={{0,1},{1,0},{2,3},{3,2},{4,5},{5,4},{6,7},{7,6},{8,9},{9,8},{10,11... | collective-permute-start | bytes 417800 | tf_op jit(solution)/shard_map/ppermute | solution.py:518
  63.5 10.5 %collective-permute-start.11 = (f32[512,128]{1,0:T(8,128)S(1)}, f32[512,128]{1,0:T(8,128)S(1)}, u32[]{:S(2)}, u32[]{:S(2)}) collective-permute-start(f32[512,128]{1,0:T(8,128)S(1)} %get-tuple-element.50), channel_id=1, source_target_pairs={{0,4},{4,0},{8,12},{12,8},{1,5},{5,1},{9,13},{13,9},{2,6},{6,2},{1... | collective-permute-start | bytes 786440 | tf_op jit(solution)/shard_map/ppermute | solution.py:604
  63.5 7.9 %collective-permute-start.14 = (bf16[272,256]{1,0:T(8,128)(2,1)S(1)}, bf16[272,256]{1,0:T(8,128)(2,1)S(1)}, u32[]{:S(2)}, u32[]{:S(2)}) collective-permute-start(bf16[272,256]{1,0:T(8,128)(2,1)S(1)} %collective-permute-done.13.d2), channel_id=1, source_target_pairs={{0,1},{1,0},{2,3},{3,2},{4,5},{5,4},{6,7},{7,6},{8,9},{9,8},{10,11... | collective-permute-start | bytes 417800 | tf_op jit(solution)/shard_map/ppermute | solution.py:518
  73.9 1.6 %collective-permute-start.18 = (bf16[1024,128]{1,0:T(8,128)(2,1)S(1)}, bf16[1024,128]{1,0:T(8,128)(2,1)S(1)}, u32[]{:S(2)}, u32[]{:S(2)}) collective-permute-start(bf16[1024,128]{1,0:T(8,128)(2,1)S(1)} %get-tuple-element.55), channel_id=1, source_target_pairs={{0,4},{4,0},{8,12},{12,8},{1,5},{5,1},{9,13},{13,9},{2,6},{6,2},{1... | collective-permute-start | bytes 786440 | tf_op jit(solution)/shard_map/ppermute | solution.py:613

commit v3 on v2

v3 whole, which is shorter than its diff:
```python
import functools

import jax
import jax.numpy as jnp
from jax import lax
from jax.experimental import pallas as pl
from jax.experimental.pallas import tpu as pltpu
from jax.sharding import PartitionSpec as P

HALO = 16
VMEM_BYTES = 20 << 20


def carried_in(array, axis, join, neutral):
    count = lax.axis_size(axis)
    place = lax.axis_index(axis)
    ahead = count - 1 - place
    gathered = jax.tree.map(
        lambda a, kind: lax.all_gather(a.astype(kind), axis),
        array,
        jax.tree.map(lambda a: jnp.bfloat16 if a.dtype == jnp.float32 else a.dtype, array),
    )
    state = jax.tree.map(lambda a, e: jnp.zeros_like(a) + jnp.asarray(e, a.dtype), array, neutral)

    def one(hop, state):
        source = count - 1 - hop
        return join(
            state,
            jax.tree.map(
                lambda a, own: lax.dynamic_index_in_dim(a, source, 0, False).astype(own.dtype),
                gathered,
                array,
            ),
        )

    return lax.fori_loop(0, ahead, one, state)


def from_behind(array, axis, by):
    count = lax.axis_size(axis)
    pairs = [(i, i + by) for i in range(count) if 0 <= i + by < count]
    return lax.ppermute(array, axis, pairs)


def lag_kernels(weights, pattern, cluster, first_row):
    local_rows = weights.shape[1]
    own_labels = lax.dynamic_slice_in_dim(cluster, first_row, local_rows, 0)
    labels = jnp.arange(pattern.shape[1], dtype=jnp.int32)
    row_onehot = (own_labels[:, None] == labels[None, :]).astype(jnp.bfloat16)
    column_onehot = (labels[:, None] == cluster[None, :]).astype(jnp.bfloat16)
    kernels = []
    for lag_index in range(weights.shape[0]):
        picked = jnp.dot(
            row_onehot, pattern[lag_index].astype(jnp.bfloat16), preferred_element_type=jnp.float32
        )
        table = jnp.dot(
            picked.astype(jnp.bfloat16), column_onehot, preferred_element_type=jnp.float32
        )
        kernels.append(weights[lag_index] * table.astype(jnp.bfloat16))
    return kernels


def correlate(kernels, extended):
    length = extended.shape[1] - len(kernels) + 1
    running = None
    for lag_index in range(len(kernels)):
        product_term = lax.dot_general(
            kernels[lag_index],
            extended[:, lag_index : lag_index + length],
            (((0,), (0,)), ((), ())),
            preferred_element_type=jnp.float32,
        )
        running = product_term if running is None else running + product_term
    return running


def reconstruct(kernels, extended):
    number_of_lags = len(kernels)
    length = extended.shape[1] - number_of_lags + 1
    running = None
    for lag_index in range(number_of_lags):
        offset = number_of_lags - 1 - lag_index
        product_term = jnp.dot(
            kernels[lag_index],
            extended[:, offset : offset + length],
            preferred_element_type=jnp.float32,
        )
        running = product_term if running is None else running + product_term
    return running


def chain_step(earlier, later):
    return (later[0] * earlier[0], later[1] + later[0] * earlier[1])


def block_recurrence(keep_fraction, inflow):
    def advance(carry, pieces):
        kept_now, state_now = carry
        keep, more = pieces
        state_now = keep * state_now + more
        kept_now = keep * kept_now
        return ((kept_now, state_now), (kept_now, state_now))

    elements = keep_fraction.shape[0]
    start = (jnp.ones((elements,), jnp.float32), jnp.zeros((elements,), jnp.float32))
    _, outputs = lax.scan(advance, start, (keep_fraction.T, inflow.T), reverse=True)
    return (outputs[0].T, outputs[1].T)


def general(
    traces,
    weights,
    pattern,
    cluster,
    element_damping_rate,
    local_step_length,
    housing_keep_share,
    admittance,
):
    local_rows = traces.shape[0]
    length = traces.shape[1]
    number_of_lags = weights.shape[0]
    first_row = lax.axis_index("row") * local_rows
    kernels = lag_kernels(weights, pattern, cluster, first_row)
    trailing = from_behind(traces[:, : number_of_lags - 1], "tm", -1)
    extended = jnp.concatenate([traces, trailing], 1)
    adjoint_sum = lax.psum(correlate(kernels, extended).astype(jnp.bfloat16), "row").astype(
        jnp.float32
    )
    spent = element_damping_rate[:, None] * local_step_length[None, :]
    keep_fraction = jnp.exp(-spent) * housing_keep_share[None, :]
    inflow = jnp.sqrt(-jnp.expm1(-2.0 * spent)) * adjoint_sum
    retained, partial_state = block_recurrence(keep_fraction, inflow)
    neutral = (jnp.ones_like(retained[:, 0]), jnp.zeros_like(partial_state[:, 0]))
    incoming = carried_in((retained[:, 0], partial_state[:, 0]), "tm", chain_step, neutral)
    state = partial_state + retained * incoming[1][:, None]
    driving = (admittance[:, None] * state).astype(jnp.bfloat16)
    leading = from_behind(driving[:, length - number_of_lags + 1 :], "tm", 1)
    pressure = reconstruct(kernels, jnp.concatenate([leading, driving], 1))
    state = lax.dynamic_slice_in_dim(state, first_row, local_rows, 0)
    return (state, pressure.astype(jnp.bfloat16))


def setup_kernel(
    traces_in,
    length_in,
    share_in,
    pattern_in,
    cluster_in,
    edge,
    clocks,
    columns,
    bits,
    own,
    traces,
    turned,
    pattern,
    cluster,
    ready,
):
    rows, length = traces.shape
    lags, kinds, _ = pattern.shape
    row, odd = lax.axis_index("row"), lax.axis_index("tm") % 2
    moves = (
        (traces_in, traces),
        (length_in, clocks.at[0:1, :]),
        (share_in, clocks.at[1:2, :]),
        (pattern_in, pattern),
        (cluster_in, cluster),
    )
    clocks[...] = jnp.zeros_like(clocks)
    copies = [
        pltpu.make_async_copy(source, target, ready.at[index])
        for index, (source, target) in enumerate(moves)
    ]
    for copy in copies:
        copy.start()
    for copy in copies:
        copy.wait()
    turned[:, 0:rows] = traces[...].astype(jnp.float32).T
    turned[:, rows:] = jnp.zeros((length, 128), jnp.float32)
    turned[:, rows : rows + 8] = clocks[...].T
    edge[...] = turned[pl.ds(pl.multiple_of(odd * (length - HALO), HALO), HALO), :]
    own[...] = turned[:, 0:rows].astype(jnp.bfloat16)

    bits[...] = jnp.int32(1) << cluster[...]
    labels = cluster[:, pl.ds(pl.multiple_of(row * rows, rows), rows)]
    hit = lax.broadcasted_iota(jnp.int32, (kinds, rows), 0) == labels
    places = lax.broadcasted_iota(jnp.int32, (kinds, pattern.shape[2]), 1)
    found = []
    for lag in range(lags):
        word = (pattern[lag] << places).sum(1, keepdims=True)
        found.append(jnp.where(hit, word, 0).sum(0, keepdims=True))
    found = jnp.concatenate(found + [jnp.zeros((8 - lags, rows), jnp.int32)], 0)
    columns[...] = found.T


def mask_kernel(slots, columns, bits, weights, kernels, spread, arrived):
    lags, rows, _ = weights.shape
    unit = kernels.shape[1] // len(slots)
    row, half = lax.axis_index("row"), lax.axis_index("tm") % 2

    def start_of(slot):
        return pl.multiple_of((jnp.bitwise_xor(row, slot) * 2 + half) * unit, unit)

    def fetch(lag, index):
        return pltpu.make_async_copy(
            weights.at[lag, :, pl.ds(start_of(slots[index]), unit)],
            kernels.at[pl.ds(lag * rows, rows), pl.ds(index * unit, unit)],
            arrived.at[index, lag],
        )

    blocks = [(lag, index) for lag in range(lags) for index in range(len(slots))]
    for block in blocks:
        fetch(*block).start()
    picked = [bits[:, pl.ds(start_of(slot), unit)] for slot in slots]
    for lag, index in blocks:
        if index == 0:
            spread[...] = jnp.broadcast_to(columns[:, lag : lag + 1], (rows, 128))
        fetch(lag, index).wait()
        for at in range(0, unit, 128):
            place = slice(lag * rows, lag * rows + rows)
            part = slice(index * unit + at, index * unit + at + 128)
            weight = kernels[place, part]
            keep = (spread[...] & picked[index][:, at : at + 128]) != 0
            kernels[place, part] = jnp.where(keep, weight, jnp.zeros_like(weight))


def correlate_kernel(own, partner, near, far, kernels, *refs):
    *outs, lagged, steps = refs
    length, rows = own.shape
    window = lagged.shape[0]
    lags = lagged.shape[1] // rows
    half = lax.axis_index("tm") % 2
    odd = half == 1
    first = pl.multiple_of(HALO + half * length, HALO)
    second = pl.multiple_of(HALO + (1 - half) * length, HALO)
    steps[0:HALO, :] = jnp.where(odd, far[:, 0:rows], near[:, 0:rows])
    steps[window : window + HALO, :] = jnp.where(odd, near[:, 0:rows], far[:, 0:rows])
    steps[pl.ds(first, length), :] = own[...].astype(jnp.float32)
    steps[pl.ds(second, length), :] = partner[...].astype(jnp.float32)
    for lag in range(lags):
        part = slice(lag * rows, lag * rows + rows)
        lagged[:, part] = steps[lag : lag + window, :].astype(jnp.bfloat16)
    multiply(lagged, kernels, outs)


def correlate_again_kernel(lagged, kernels, *outs):
    multiply(lagged, kernels, outs)


def multiply(lagged, kernels, outs):
    unit = outs[0].shape[1]
    for index, out in enumerate(outs):
        out[...] = jnp.dot(
            lagged[...],
            kernels[:, index * unit : index * unit + unit],
            preferred_element_type=jnp.float32,
        ).astype(out.dtype)


def pair_kernel(mine, theirs, out):
    out[...] = (mine[...].astype(jnp.float32) + theirs[...].astype(jnp.float32)).astype(out.dtype)


def one_less_exp(y):
    series = jnp.ones_like(y)
    for k in range(9, 1, -1):
        series = 1.0 - series * y * (1.0 / k)
    return jnp.where(y < 0.5, y * series, 1.0 - jnp.exp(-y))


def factors_kernel(clocks, partner_clocks, near, far, rate, out, columns):
    _, window, unit = out.shape
    length = clocks.shape[1]
    rows = near.shape[1] - 128
    row, half = lax.axis_index("row"), lax.axis_index("tm") % 2
    first = pl.multiple_of(HALO + half * length, HALO)
    second = pl.multiple_of(HALO + (1 - half) * length, HALO)
    columns[0:HALO, :] = jnp.where(half == 1, far[:, rows : rows + 8], near[:, rows : rows + 8])
    columns[pl.ds(first, length), :] = clocks[...].T
    columns[pl.ds(second, length), :] = partner_clocks[...].T
    index = lax.broadcasted_iota(jnp.int32, (window, unit), 0) & 7
    start = pl.multiple_of((row * 2 + half) * unit, unit)
    spent = columns[:, 0:1] * rate[:, pl.ds(start, unit)]
    out[0] = jnp.sqrt(one_less_exp(2.0 * spent))
    kept = jnp.exp(-spent) * columns[:, 1:2]
    for slot, shift in ((1, 1), (2, 2), (3, 4)):
        inside = index < 8 - shift
        out[slot] = jnp.where(inside, kept, 0.0)
        kept = jnp.where(inside, kept * pltpu.roll(kept, window - shift, 0), kept)
    out[4] = kept
    carry = jnp.ones((1, unit), jnp.float32)
    for group in range(window // 8 - 1, -1, -1):
        block = kept[group * 8 : group * 8 + 8] * carry
        out[5, group * 8 : group * 8 + 8, :] = block
        carry = block[0:1]


def recurrence_kernel(own, direct, paired, factors, partial, first):
    window, unit = own.shape
    total = (
        own[...].astype(jnp.float32)
        + direct[...].astype(jnp.float32)
        + paired[...].astype(jnp.float32)
    )
    state = factors[0] * total
    for slot, shift in ((1, 1), (2, 2), (3, 4)):
        state = state + factors[slot] * pltpu.roll(state, window - shift, 0)
    carry = jnp.zeros((1, unit), jnp.float32)
    for group in range(window // 8 - 1, -1, -1):
        rows = slice(group * 8, group * 8 + 8)
        block = state[rows] + factors[4, rows, :] * carry
        partial[rows, :] = block
        carry = block[0:1]
        if group * 8 == HALO:
            first[...] = jnp.broadcast_to(carry, first.shape)


def finish_kernel(incoming, admittance, partial, factors, drive, mine, theirs, states):
    window, unit = states.shape
    length = mine.shape[1]
    row, half = lax.axis_index("row"), lax.axis_index("tm") % 2
    first = pl.multiple_of(HALO + half * length, HALO)
    second = pl.multiple_of(HALO + (1 - half) * length, HALO)
    start = pl.multiple_of((row * 2 + half) * unit, unit)
    state = partial[...] + factors[5] * incoming[0:1, :]
    drive[...] = (admittance[:, pl.ds(start, unit)] * state).astype(jnp.bfloat16)
    states[...] = state
    mine[...] = states[pl.ds(first, length), :].T
    theirs[...] = states[pl.ds(second, length), :].T


def reconstruct_kernel(count, at, stage, *refs):
    drives, (kernels, *refs) = refs[:count], refs[count:]
    if stage == "last":
        before, keep, send, steps, lagged = refs
    elif stage == "next":
        before, total, steps, lagged = refs
    else:
        total, steps, lagged = refs
    lags, width, _ = lagged.shape
    unit = drives[0].shape[1]
    rows = kernels.shape[0] // lags
    for slot, drive in enumerate(drives):
        steps[:, slot * unit : slot * unit + unit] = drive[...].astype(jnp.float32)
    for lag in range(lags):
        lagged[lag] = steps[HALO - lag : HALO - lag + width, :].astype(jnp.bfloat16)
    added = None if stage == "first" else before[...]
    for lag in range(lags):
        term = lax.dot_general(
            kernels[lag * rows : lag * rows + rows, at * unit : (at + count) * unit],
            lagged[lag],
            (((1,), (1,)), ((), ())),
            preferred_element_type=jnp.float32,
        )
        added = term if added is None else added + term
    if stage == "last":
        length = width // 2
        odd = lax.axis_index("tm") % 2 == 1
        keep[...] = jnp.where(odd, added[:, length:], added[:, :length])
        send[...] = jnp.where(odd, added[:, :length], added[:, length:]).astype(send.dtype)
    else:
        total[...] = added


def call(kernel, name, in_specs, out_specs, out_shape, scratch, flops, moved):
    return pl.pallas_call(
        kernel,
        in_specs=in_specs,
        out_specs=out_specs,
        out_shape=out_shape,
        scratch_shapes=scratch,
        cost_estimate=pl.CostEstimate(flops=flops, bytes_accessed=moved, transcendentals=0),
        compiler_params=pltpu.CompilerParams(vmem_limit_bytes=VMEM_BYTES),
        name=name,
    )


def paired(
    traces,
    weights,
    pattern,
    cluster,
    element_damping_rate,
    local_step_length,
    housing_keep_share,
    admittance,
):
    rows, length = traces.shape
    lags = weights.shape[0]
    window = HALO + 2 * length
    unit = rows // 2
    half = lax.axis_index("tm") % 2
    odd = half == 1
    f32, bf16 = jnp.float32, jnp.bfloat16
    tm_count = lax.axis_size("tm")
    swap = [(i, i ^ 1) for i in range(tm_count)]
    near = [(i, i + 1 if i % 2 else i - 1) for i in range(tm_count)]
    near = [(i, j) for i, j in near if 0 <= j < tm_count]
    far = [(i, i + 2 if i % 2 else i - 2) for i in range(tm_count)]
    far = [(i, j) for i, j in far if 0 <= j < tm_count]
    vmem = pl.BlockSpec(memory_space=pltpu.VMEM)

    hbm = pl.BlockSpec(memory_space=pltpu.HBM)
    barrier = lax.optimization_barrier

    def held(array):
        return pltpu.with_memory_space_constraint(array, pltpu.HBM)

    edge, clocks, columns, bits, own = call(
        setup_kernel,
        "setup",
        [hbm] * 5,
        [vmem] * 5,
        [
            jax.ShapeDtypeStruct((HALO, rows + 128), f32),
            jax.ShapeDtypeStruct((8, length), f32),
            jax.ShapeDtypeStruct((rows, 8), jnp.int32),
            jax.ShapeDtypeStruct((1, cluster.shape[0]), jnp.int32),
            jax.ShapeDtypeStruct((length, rows), bf16),
        ],
        [
            pltpu.VMEM((rows, length), bf16),
            pltpu.VMEM((length, rows + 128), f32),
            pltpu.VMEM(pattern.shape, jnp.int32),
            pltpu.VMEM((1, cluster.shape[0]), jnp.int32),
            pltpu.SemaphoreType.DMA((5,)),
        ],
        rows * length * 4,
        rows * length * 2,
    )(
        held(traces),
        held(local_step_length[None]),
        held(housing_keep_share[None]),
        held(pattern),
        held(cluster[None]),
    )
    partner_clocks = lax.ppermute(clocks, "tm", swap)
    partner = lax.ppermute(own, "tm", swap)
    got_near = lax.ppermute(edge, "tm", near)
    got_far = lax.ppermute(edge, "tm", far)

    strip = jax.ShapeDtypeStruct((window, unit), bf16)
    share_bytes = 2 * lags * rows * unit * 2
    share_flops = 2 * 2 * lags * rows * unit * window

    def chosen(slots, columns):
        return call(
            functools.partial(mask_kernel, slots),
            "mask",
            [vmem] * 2 + [hbm],
            vmem,
            pltpu.VMEM((lags * rows, len(slots) * unit), bf16),
            [pltpu.VMEM((rows, 128), jnp.int32), pltpu.SemaphoreType.DMA((len(slots), lags))],
            share_bytes,
            share_bytes,
        )(columns, bits, weights)

    def correlated(kernels):
        return call(
            correlate_kernel,
            "correlate",
            [vmem] * 5,
            [vmem] * 3,
            [strip] * 2 + [pltpu.VMEM((window, lags * rows), bf16)],
            [pltpu.VMEM((window + HALO, rows), f32)],
            share_flops,
            share_bytes // 2,
        )(own, partner, got_near, got_far, kernels)

    def correlated_again(lagged, kernels):
        return call(
            correlate_again_kernel,
            "correlate",
            [vmem] * 2,
            [vmem] * 2,
            [strip] * 2,
            [],
            share_flops,
            share_bytes // 2,
        )(lagged, kernels)

    def added(mine, theirs):
        return call(
            pair_kernel, "pair", [vmem] * 2, vmem, strip, [], window * unit, window * unit * 6
        )(mine, theirs)

    def over_row(array, by):
        return lax.ppermute(array, "row", [(i, i ^ by) for i in range(4)])

    def factored(clocks):
        return call(
            factors_kernel,
            "factors",
            [vmem] * 5,
            vmem,
            jax.ShapeDtypeStruct((6, window, unit), f32),
            [pltpu.VMEM((window, 8), f32)],
            window * unit * 100,
            window * unit * 24,
        )(clocks, partner_clocks, got_near, got_far, element_damping_rate[None])

    def recurrence(terms, factors):
        return call(
            recurrence_kernel,
            "recurrence",
            [vmem] * 4,
            [vmem] * 2,
            [jax.ShapeDtypeStruct((window, unit), f32), jax.ShapeDtypeStruct((8, unit), f32)],
            [],
            window * unit * 20,
            window * unit * 30,
        )(*terms, factors)

    def finished(partial, incoming, factors):
        piece = jax.ShapeDtypeStruct((unit, length), f32)
        return call(
            finish_kernel,
            "finish",
            [vmem] * 4,
            [vmem] * 3,
            [strip, piece, piece],
            [pltpu.VMEM((window, unit), f32)],
            window * unit * 10,
            window * unit * 16,
        )(incoming, admittance[None], partial, factors)

    def reconstructed(stage, at, drives, kernels, *before):
        count = len(drives)
        out_shape = jax.ShapeDtypeStruct((rows, 2 * length), f32)
        if stage == "last":
            out_shape = [
                jax.ShapeDtypeStruct((rows, length), f32),
                jax.ShapeDtypeStruct((rows, length), bf16),
            ]
        return call(
            functools.partial(reconstruct_kernel, count, at, stage),
            "reconstruct",
            [vmem] * (count + 1 + len(before)),
            [vmem] * 2 if stage == "last" else vmem,
            out_shape,
            [
                pltpu.VMEM((window, count * unit), f32),
                pltpu.VMEM((lags, 2 * length, count * unit), bf16),
            ],
            share_flops * count // 2,
            share_bytes * count // 4,
        )(*drives, kernels, *before)

    far_kernels = chosen((2, 3), columns)
    o2, o3, lagged = correlated(far_kernels)
    s3 = over_row(o3, 1)
    late_columns, _ = barrier((columns, o2))
    near_kernels = chosen((0, 1), late_columns)
    o0, o1 = correlated_again(lagged, near_kernels)
    paired = over_row(added(o2, s3), 2)
    direct = over_row(o1, 1)
    factors = factored(clocks)
    partial, first = recurrence((o0, direct, paired), factors)
    incoming = lax.ppermute(first, "tm", [(i, i - 2) for i in range(2, tm_count)])
    drive, mine, theirs = finished(partial, incoming, factors)
    d2 = over_row(drive, 2)
    d1 = over_row(drive, 1)
    d3 = over_row(d2, 1)
    theirs = lax.ppermute(theirs, "tm", swap)
    total = reconstructed("first", 0, (drive, d1), near_kernels)
    total = reconstructed("next", 0, (d2,), far_kernels, total)
    keep, send = reconstructed("last", 1, (d3,), far_kernels, total)
    pressure = keep + lax.ppermute(send, "tm", swap).astype(f32)
    state = jnp.where(
        odd, jnp.concatenate([theirs, mine], 0), jnp.concatenate([mine, theirs], 0)
    )
    return (state, pressure.astype(bf16))


def local(traces, weights, pattern, *rest):
    rows, length = traces.shape
    fits = (
        lax.axis_size("row") == 4
        and lax.axis_size("tm") == 4
        and length == 128
        and rows % 256 == 0
        and weights.shape[0] <= 8
        and pattern.shape[1] <= 32
    )
    return (paired if fits else general)(traces, weights, pattern, *rest)


def solution(mesh):
    placed = (P("row", ("group", "tm")), P(None, "row", None), P(), P(), P(), P("tm"), P("tm"), P())
    return jax.shard_map(
        local,
        mesh=mesh,
        in_specs=placed,
        out_specs=(P("row", ("group", "tm")), P("row", ("group", "tm"))),
        check_vma=False,
    )
```

time: 76.5 us -> 68.7 us (0.90)
  starting transfers between devices: 26.7 us -> 15.6 us
  waiting for transfers between devices: 23.4 us -> 28.7 us
  Pallas kernels: 23.7 us -> 21.8 us
    ppermute x12 -> x6, starting transfers between devices: 22.7 us -> 11.5 us  [over_row(): return lax.ppermute(array, 'row', [(i, i ^ by) for i in range(4)])]
    ppermute x12 -> x6, waiting for transfers between devices: 15.7 us -> 20.8 us  [over_row(): return lax.ppermute(array, 'row', [(i, i ^ by) for i in range(4)])]
    pallas_call x10 -> x11, Pallas kernels: 23.6 us -> 21.7 us  [the longest x2 8.23 us: chosen(): call(functools.partial(mask_kernel, slots), 'mask', [vmem] * 2 + [hbm], v...]
  transfers between devices with their start and end apart: 19 -> 13, of which waited for: 10 -> 8; matrix products, arithmetic and copies ran while one was open for 1% -> 1% of each run, Pallas kernels for 20% -> 25%
where the time goes in v3:
time: 68.7 us; the launch traced here: 68.5 us
  waiting for transfers between devices  28.7 us (42%)
  Pallas kernels  21.8 us (32%)
  starting transfers between devices  15.6 us (23%)
  other arithmetic  1.59 us (2%)
  between operations  0.8 us (1%)
    ppermute x6, waiting for transfers between devices, over_row(): return lax.ppermute(array, 'row', [(i, i ^ by) for i in range(4)])  20.8 us
    ppermute x6, starting transfers between devices, over_row(): return lax.ppermute(array, 'row', [(i, i ^ by) for i in range(4)])  11.5 us
    pallas_call x2, Pallas kernels, chosen(): call(functools.partial(mask_kernel, slots), 'mask', [vmem] * 2 + [hbm], v...  8.23 us
    pallas_call x3, Pallas kernels, reconstructed(): call(functools.partial(reconstruct_kernel, count, at, stage), 'reconstruc...  4.97 us
    ppermute x1, waiting for transfers between devices, paired(): lax.ppermute(first, 'tm', [(i, i - 2) for i in range(2, tm_count)])  4.15 us
    pallas_call x1, Pallas kernels, correlated(): call(correlate_kernel, 'correlate', [vmem] * 5, [vmem] * 3, [strip] * 2 +...  2.53 us
    pallas_call x1, Pallas kernels, correlated_again(): call(correlate_again_kernel, 'correlate', [vmem] * 2, [vmem] * 2, [strip]...  2.46 us
    ppermute x1, waiting for transfers between devices, paired(): got_far = lax.ppermute(edge, 'tm', far)  1.94 us
  transfers between devices with their start and end apart: 13, of which 8 were waited for; matrix products, arithmetic and copies ran while one was open for 1% of the time, Pallas kernels for 25%

profile of v3, /device:TPU:0, one launch (start us, length us, event | category | flops | bytes accessed | tf_op | source)
XLA Modules:
  0.0 68.5 jit_solution(13750777694869014028)
XLA Ops:
  0.6 1.4 %setup.1 = (f32[16,1152]{1,0:T(8,128)S(1)}, f32[8,128]{1,0:T(8,128)S(1)}, s32[1024,8]{1,0:T(8,128)S(1)}, s32[1,4096]{1,0:T(1,128)S(1)}, bf16[128,1024]{1,0:T(8,128)(2,1)S(1)}) custom-call(bf16[1024,128]{1,0:T(8,128)(2,1)} %traces_in.1, f32[1,128]{1,0:T(1,128)} %bitcast.8, f32[1,128]{1,0:T(1,128)} %bitcast.9, s32[4,32,32]{2,1,0:T(8,128)} %pattern_in.1, ...), custom_call_target="tpu_custom_call" | custom-call | flops 524288 | bytes 262144 | tf_op jit(solution)/shard_map/setup/pallas_call | solution.py:411
  2.0 0.5 collective-permute-start
  2.5 0.7 collective-permute-start.1
  3.2 1.3 %collective-permute-start.2 = (f32[16,1152]{1,0:T(8,128)S(1)}, f32[16,1152]{1,0:T(8,128)S(1)}, u32[]{:S(2)}, u32[]{:S(2)}) collective-permute-start(f32[16,1152]{1,0:T(8,128)S(1)} %get-tuple-element.21), channel_id=1, source_target_pairs={{4,12},{8,0},{5,13},{9,1},{6,14},{10,2},{7,15},{11,3},{20,28},{24,... | collective-permute-start | bytes 221192 | tf_op jit(solution)/shard_map/ppermute | solution.py:442
  4.5 4.1 %mask.2.kernels.refs_1_ = bf16[4096,1024]{1,0:T(8,128)(2,1)S(1)} custom-call(s32[1024,8]{1,0:T(8,128)S(1)} %get-tuple-element.26.columns, s32[1,4096]{1,0:T(1,128)S(1)} %get-tuple-element.23.bits, bf16[4,1024,4096]{2,1,0:T(8,128)(2,1)} %weights.3), custom_call_target="tpu_custom_call" | custom-call | flops 8388608 | bytes 8388608 | tf_op jit(solution)/shard_map/mask/pallas_call | solution.py:449
  8.6 0.0 collective-permute-done.1.near
  8.6 1.9 %collective-permute-done.2.far = f32[16,1152]{1,0:T(8,128)S(1)} collective-permute-done((f32[16,1152]{1,0:T(8,128)S(1)}, f32[16,1152]{1,0:T(8,128)S(1)}, u32[]{:S(2)}, u32[]{:S(2)}) %collective-permute-start.2) | collective-permute-done | bytes 73760 | tf_op jit(solution)/shard_map/ppermute | solution.py:442
  10.6 0.0 collective-permute-done.partner
  10.6 2.5 %correlate.2 = (bf16[272,512]{1,0:T(8,128)(2,1)S(1)}, bf16[272,512]{1,0:T(8,128)(2,1)S(1)}, bf16[272,4096]{1,0:T(8,128)(2,1)S(1)}) custom-call(bf16[128,1024]{1,0:T(8,128)(2,1)S(1)} %get-tuple-element.20.own, bf16[128,1024]{1,0:T(8,128)(2,1)S(1)} %collective-permute-done.partner, f32[16,1152]{1,0:T(8,128)S(1)} %collective-permute-done.1.near, ...), custom_call_target="tpu_custom_call" | custom-call | flops 2281701376 | bytes 4194304 | tf_op jit(solution)/shard_map/correlate/pallas_call | solution.py:461
  13.1 2.3 %collective-permute-start.4 = (bf16[272,512]{1,0:T(8,128)(2,1)S(1)}, bf16[272,512]{1,0:T(8,128)(2,1)S(1)}, u32[]{:S(2)}, u32[]{:S(2)}) collective-permute-start(bf16[272,512]{1,0:T(8,128)(2,1)S(1)} %get-tuple-element.29), channel_id=1, source_target_pairs={{0,1},{1,0},{2,3},{3,2},{4,5},{5,4},{6,7},{7,6},{8,9},{9,8},{10,11... | collective-permute-start | bytes 835592 | tf_op jit(solution)/shard_map/ppermute | solution.py:490
  15.4 4.1 %mask.3.kernels.refs_2_ = bf16[4096,1024]{1,0:T(8,128)(2,1)S(1)} custom-call(s32[1024,8]{1,0:T(8,128)S(1)} %get-tuple-element.26.columns, s32[1,4096]{1,0:T(1,128)S(1)} %get-tuple-element.23.bits, bf16[4,1024,4096]{2,1,0:T(8,128)(2,1)} %weights.3), custom_call_target="tpu_custom_call" | custom-call | flops 8388608 | bytes 8388608 | tf_op jit(solution)/shard_map/mask/pallas_call | solution.py:449
  19.5 0.0 copy-start
  19.5 0.0 copy-start.1
  19.5 2.5 %correlate.3 = (bf16[272,512]{1,0:T(8,128)(2,1)S(1)}, bf16[272,512]{1,0:T(8,128)(2,1)S(1)}) custom-call(bf16[272,4096]{1,0:T(8,128)(2,1)S(1)} %get-tuple-element.24.lagged, bf16[4096,1024]{1,0:T(8,128)(2,1)S(1)} %mask.3.kernels.refs_2_), custom_call_target="tpu_custom_call" | custom-call | flops 2281701376 | bytes 4194304 | tf_op jit(solution)/shard_map/correlate/pallas_call | solution.py:473
  22.0 0.1 collective-permute-start.3
  22.0 0.1 collective-permute-done.4.theirs
  22.1 0.1 pair.1
  22.2 3.6 %collective-permute-start.5 = (bf16[272,512]{1,0:T(8,128)(2,1)S(1)}, bf16[272,512]{1,0:T(8,128)(2,1)S(1)}, u32[]{:S(2)}, u32[]{:S(2)}) collective-permute-start(bf16[272,512]{1,0:T(8,128)(2,1)S(1)} %pair.1), channel_id=1, source_target_pairs={{0,2},{1,3},{2,0},{3,1},{4,6},{5,7},{6,4},{7,5},{8,10},{9,11},{10,... | collective-permute-start | bytes 835592 | tf_op jit(solution)/shard_map/ppermute | solution.py:490
  25.8 0.0 collective-permute-start.6
  25.8 1.2 %collective-permute-done.6.partner_clocks = f32[8,128]{1,0:T(8,128)S(1)} collective-permute-done((f32[8,128]{1,0:T(8,128)S(1)}, f32[8,128]{1,0:T(8,128)S(1)}, u32[]{:S(2)}, u32[]{:S(2)}) %collective-permute-start.6) | collective-permute-done | bytes 4128 | tf_op jit(solution)/shard_map/ppermute | solution.py:439
  26.9 0.0 copy-done
  26.9 1.5 %factors.1 = f32[6,272,512]{2,1,0:T(8,128)S(1)} custom-call(f32[8,128]{1,0:T(8,128)S(1)} %get-tuple-element.30.clocks, f32[8,128]{1,0:T(8,128)S(1)} %collective-permute-done.6.partner_clocks, f32[16,1152]{1,0:T(8,128)S(1)} %collective-permute-done.1.near, f32[16,1152]{1,0:T(8,128)S(1)} %collective-permute-done.2.far, f32[1,4096]{1,0:T(1,128)S(1)} %bitcast.5), custom_call_target="tpu_custom_call" | custom-call | flops 13926400 | bytes 3342336 | tf_op jit(solution)/shard_map/factors/pallas_call | solution.py:493
  28.4 9.1 %collective-permute-done.3.direct = bf16[272,512]{1,0:T(8,128)(2,1)S(1)} collective-permute-done((bf16[272,512]{1,0:T(8,128)(2,1)S(1)}, bf16[272,512]{1,0:T(8,128)(2,1)S(1)}, u32[]{:S(2)}, u32[]{:S(2)}) %collective-permute-start.3) | collective-permute-done | bytes 278560 | tf_op jit(solution)/shard_map/ppermute | solution.py:490
  37.4 0.0 collective-permute-done.5.paired
  37.5 0.4 recurrence.1
  37.8 1.5 %collective-permute-start.7 = (f32[8,512]{1,0:T(8,128)S(1)}, f32[8,512]{1,0:T(8,128)S(1)}, u32[]{:S(2)}, u32[]{:S(2)}) collective-permute-start(f32[8,512]{1,0:T(8,128)S(1)} %get-tuple-element.31), channel_id=1, source_target_pairs={{8,0},{12,4},{9,1},{13,5},{10,2},{14,6},{11,3},{15,7},{24,16},{28,... | collective-permute-start | bytes 49160 | tf_op jit(solution)/shard_map/ppermute | solution.py:561
  39.3 4.2 %collective-permute-done.7.incoming = f32[8,512]{1,0:T(8,128)S(1)} collective-permute-done((f32[8,512]{1,0:T(8,128)S(1)}, f32[8,512]{1,0:T(8,128)S(1)}, u32[]{:S(2)}, u32[]{:S(2)}) %collective-permute-start.7) | collective-permute-done | bytes 16416 | tf_op jit(solution)/shard_map/ppermute | solution.py:561
  43.5 0.0 copy-done.1
  43.5 0.3 finish.1
  43.8 0.7 %collective-permute-start.9 = (bf16[272,512]{1,0:T(8,128)(2,1)S(1)}, bf16[272,512]{1,0:T(8,128)(2,1)S(1)}, u32[]{:S(2)}, u32[]{:S(2)}) collective-permute-start(bf16[272,512]{1,0:T(8,128)(2,1)S(1)} %get-tuple-element.35.refs_0_), channel_id=1, source_target_pairs={{0,2},{1,3},{2,0},{3,1},{4,6},{5,7},{6,4},{7,5},{8,10},{9,11},{10,... | collective-permute-start | bytes 835592 | tf_op jit(solution)/shard_map/ppermute | solution.py:490
  44.5 4.9 %collective-permute-start.11 = (bf16[272,512]{1,0:T(8,128)(2,1)S(1)}, bf16[272,512]{1,0:T(8,128)(2,1)S(1)}, u32[]{:S(2)}, u32[]{:S(2)}) collective-permute-start(bf16[272,512]{1,0:T(8,128)(2,1)S(1)} %get-tuple-element.35.refs_0_), channel_id=1, source_target_pairs={{0,1},{1,0},{2,3},{3,2},{4,5},{5,4},{6,7},{7,6},{8,9},{9,8},{10,11... | collective-permute-start | bytes 835592 | tf_op jit(solution)/shard_map/ppermute | solution.py:490
  49.4 0.0 collective-permute-start.8
  49.4 8.8 %collective-permute-done.9.refs_0_ = bf16[272,512]{1,0:T(8,128)(2,1)S(1)} collective-permute-done((bf16[272,512]{1,0:T(8,128)(2,1)S(1)}, bf16[272,512]{1,0:T(8,128)(2,1)S(1)}, u32[]{:S(2)}, u32[]{:S(2)}) %collective-permute-start.9) | collective-permute-done | bytes 278560 | tf_op jit(solution)/shard_map/ppermute | solution.py:490
  58.2 0.0 collective-permute-start.10
  58.2 0.0 collective-permute-done.11.refs_1_
  58.3 2.4 %reconstruct.3.refs_2_ = f32[1024,256]{1,0:T(8,128)S(1)} custom-call(bf16[272,512]{1,0:T(8,128)(2,1)S(1)} %get-tuple-element.35.refs_0_, bf16[272,512]{1,0:T(8,128)(2,1)S(1)} %collective-permute-done.11.refs_1_, bf16[4096,1024]{1,0:T(8,128)(2,1)S(1)} %mask.3.kernels.refs_2_), custom_call_target="tpu_custom_call" | custom-call | flops 2281701376 | bytes 4194304 | tf_op jit(solution)/shard_map/reconstruct/pallas_call | solution.py:537
  60.6 1.3 %reconstruct.4.refs_2_ = f32[1024,256]{1,0:T(8,128)S(1)} custom-call(bf16[272,512]{1,0:T(8,128)(2,1)S(1)} %collective-permute-done.9.refs_0_, bf16[4096,1024]{1,0:T(8,128)(2,1)S(1)} %mask.2.kernels.refs_1_, f32[1024,256]{1,0:T(8,128)S(1)} %reconstruct.3.refs_2_), custom_call_target="tpu_custom_call" | custom-call | flops 1140850688 | bytes 2097152 | tf_op jit(solution)/shard_map/reconstruct/pallas_call | solution.py:537
  61.9 2.8 %collective-permute-done.10.refs_0_ = bf16[272,512]{1,0:T(8,128)(2,1)S(1)} collective-permute-done((bf16[272,512]{1,0:T(8,128)(2,1)S(1)}, bf16[272,512]{1,0:T(8,128)(2,1)S(1)}, u32[]{:S(2)}, u32[]{:S(2)}) %collective-permute-start.10) | collective-permute-done | bytes 278560 | tf_op jit(solution)/shard_map/ppermute | solution.py:490
  64.8 1.3 %reconstruct.5 = (f32[1024,128]{1,0:T(8,128)S(1)}, bf16[1024,128]{1,0:T(8,128)(2,1)S(1)}) custom-call(bf16[272,512]{1,0:T(8,128)(2,1)S(1)} %collective-permute-done.10.refs_0_, bf16[4096,1024]{1,0:T(8,128)(2,1)S(1)} %mask.2.kernels.refs_1_, f32[1024,256]{1,0:T(8,128)S(1)} %reconstruct.4.refs_2_), custom_call_target="tpu_custom_call" | custom-call | flops 1140850688 | bytes 2097152 | tf_op jit(solution)/shard_map/reconstruct/pallas_call | solution.py:537
  66.1 0.1 collective-permute-start.12
  66.2 0.0 collective-permute-done.8
  66.2 0.8 %maximum_select_fusion = f32[1024,128]{1,0:T(8,128)} fusion(f32[512,128]{1,0:T(8,128)S(1)} %get-tuple-element.34, f32[512,128]{1,0:T(8,128)S(1)} %collective-permute-done.8, pred[]{:T(512)S(6)} %eq.5), kind=kLoop, calls=%fused_computation | loop fusion | flops 393216 | bytes 1048577 | tf_op jit(solution)/shard_map/jit(_where)/select_n | solution.py:571
  67.0 0.7 collective-permute-done.12
  67.7 0.8 %add_convert_fusion = bf16[1024,128]{1,0:T(8,128)(2,1)} fusion(f32[1024,128]{1,0:T(8,128)S(1)} %get-tuple-element.36, bf16[1024,128]{1,0:T(8,128)(2,1)S(1)} %collective-permute-done.12), kind=kLoop, calls=%fused_computation.1 | loop fusion | flops 393216 | bytes 1048576 | tf_op jit(solution)/shard_map/convert_element_type | solution.py:574
Async XLA Ops:
  2.0 8.6 %collective-permute-start = (bf16[128,1024]{1,0:T(8,128)(2,1)S(1)}, bf16[128,1024]{1,0:T(8,128)(2,1)S(1)}, u32[]{:S(2)}, u32[]{:S(2)}) collective-permute-start(bf16[128,1024]{1,0:T(8,128)(2,1)S(1)} %get-tuple-element.20.own), channel_id=1, source_target_pairs={{0,4},{4,0},{8,12},{12,8},{1,5},{5,1},{9,13},{13,9},{2,6},{6,2},{1... | collective-permute-start | bytes 786440 | tf_op jit(solution)/shard_map/ppermute | solution.py:440
  2.5 6.1 %collective-permute-start.1 = (f32[16,1152]{1,0:T(8,128)S(1)}, f32[16,1152]{1,0:T(8,128)S(1)}, u32[]{:S(2)}, u32[]{:S(2)}) collective-permute-start(f32[16,1152]{1,0:T(8,128)S(1)} %get-tuple-element.21), channel_id=1, source_target_pairs={{4,8},{8,4},{5,9},{9,5},{6,10},{10,6},{7,11},{11,7},{20,24},{24,20... | collective-permute-start | bytes 221192 | tf_op jit(solution)/shard_map/ppermute | solution.py:441
  3.2 7.4 %collective-permute-start.2 = (f32[16,1152]{1,0:T(8,128)S(1)}, f32[16,1152]{1,0:T(8,128)S(1)}, u32[]{:S(2)}, u32[]{:S(2)}) collective-permute-start(f32[16,1152]{1,0:T(8,128)S(1)} %get-tuple-element.21), channel_id=1, source_target_pairs={{4,12},{8,0},{5,13},{9,1},{6,14},{10,2},{7,15},{11,3},{20,28},{24,... | collective-permute-start | bytes 221192 | tf_op jit(solution)/shard_map/ppermute | solution.py:442
  13.1 9.0 %collective-permute-start.4 = (bf16[272,512]{1,0:T(8,128)(2,1)S(1)}, bf16[272,512]{1,0:T(8,128)(2,1)S(1)}, u32[]{:S(2)}, u32[]{:S(2)}) collective-permute-start(bf16[272,512]{1,0:T(8,128)(2,1)S(1)} %get-tuple-element.29), channel_id=1, source_target_pairs={{0,1},{1,0},{2,3},{3,2},{4,5},{5,4},{6,7},{7,6},{8,9},{9,8},{10,11... | collective-permute-start | bytes 835592 | tf_op jit(solution)/shard_map/ppermute | solution.py:490
  19.5 7.5 %copy-start = (f32[4096]{0:T(1024)S(1)}, f32[4096]{0:T(1024)}, u32[]{:S(2)}) copy-start(f32[4096]{0:T(1024)} %param.12) | copy-start | bytes 49156
  19.5 24.0 %copy-start.1 = (f32[4096]{0:T(1024)S(1)}, f32[4096]{0:T(1024)}, u32[]{:S(2)}) copy-start(f32[4096]{0:T(1024)} %param.15) | copy-start | bytes 49156
  22.0 15.5 %collective-permute-start.3 = (bf16[272,512]{1,0:T(8,128)(2,1)S(1)}, bf16[272,512]{1,0:T(8,128)(2,1)S(1)}, u32[]{:S(2)}, u32[]{:S(2)}) collective-permute-start(bf16[272,512]{1,0:T(8,128)(2,1)S(1)} %get-tuple-element.28), channel_id=1, source_target_pairs={{0,1},{1,0},{2,3},{3,2},{4,5},{5,4},{6,7},{7,6},{8,9},{9,8},{10,11... | collective-permute-start | bytes 835592 | tf_op jit(solution)/shard_map/ppermute | solution.py:490
  22.2 15.3 %collective-permute-start.5 = (bf16[272,512]{1,0:T(8,128)(2,1)S(1)}, bf16[272,512]{1,0:T(8,128)(2,1)S(1)}, u32[]{:S(2)}, u32[]{:S(2)}) collective-permute-start(bf16[272,512]{1,0:T(8,128)(2,1)S(1)} %pair.1), channel_id=1, source_target_pairs={{0,2},{1,3},{2,0},{3,1},{4,6},{5,7},{6,4},{7,5},{8,10},{9,11},{10,... | collective-permute-start | bytes 835592 | tf_op jit(solution)/shard_map/ppermute | solution.py:490
  25.8 1.2 %collective-permute-start.6 = (f32[8,128]{1,0:T(8,128)S(1)}, f32[8,128]{1,0:T(8,128)S(1)}, u32[]{:S(2)}, u32[]{:S(2)}) collective-permute-start(f32[8,128]{1,0:T(8,128)S(1)} %get-tuple-element.30.clocks), channel_id=1, source_target_pairs={{0,4},{4,0},{8,12},{12,8},{1,5},{5,1},{9,13},{13,9},{2,6},{6,2},{1... | collective-permute-start | bytes 12296 | tf_op jit(solution)/shard_map/ppermute | solution.py:439
  37.8 5.6 %collective-permute-start.7 = (f32[8,512]{1,0:T(8,128)S(1)}, f32[8,512]{1,0:T(8,128)S(1)}, u32[]{:S(2)}, u32[]{:S(2)}) collective-permute-start(f32[8,512]{1,0:T(8,128)S(1)} %get-tuple-element.31), channel_id=1, source_target_pairs={{8,0},{12,4},{9,1},{13,5},{10,2},{14,6},{11,3},{15,7},{24,16},{28,... | collective-permute-start | bytes 49160 | tf_op jit(solution)/shard_map/ppermute | solution.py:561
  43.8 14.5 %collective-permute-start.9 = (bf16[272,512]{1,0:T(8,128)(2,1)S(1)}, bf16[272,512]{1,0:T(8,128)(2,1)S(1)}, u32[]{:S(2)}, u32[]{:S(2)}) collective-permute-start(bf16[272,512]{1,0:T(8,128)(2,1)S(1)} %get-tuple-element.35.refs_0_), channel_id=1, source_target_pairs={{0,2},{1,3},{2,0},{3,1},{4,6},{5,7},{6,4},{7,5},{8,10},{9,11},{10,... | collective-permute-start | bytes 835592 | tf_op jit(solution)/shard_map/ppermute | solution.py:490
  44.5 13.8 %collective-permute-start.11 = (bf16[272,512]{1,0:T(8,128)(2,1)S(1)}, bf16[272,512]{1,0:T(8,128)(2,1)S(1)}, u32[]{:S(2)}, u32[]{:S(2)}) collective-permute-start(bf16[272,512]{1,0:T(8,128)(2,1)S(1)} %get-tuple-element.35.refs_0_), channel_id=1, source_target_pairs={{0,1},{1,0},{2,3},{3,2},{4,5},{5,4},{6,7},{7,6},{8,9},{9,8},{10,11... | collective-permute-start | bytes 835592 | tf_op jit(solution)/shard_map/ppermute | solution.py:490
  49.4 16.8 %collective-permute-start.8 = (f32[512,128]{1,0:T(8,128)S(1)}, f32[512,128]{1,0:T(8,128)S(1)}, u32[]{:S(2)}, u32[]{:S(2)}) collective-permute-start(f32[512,128]{1,0:T(8,128)S(1)} %get-tuple-element.33), channel_id=1, source_target_pairs={{0,4},{4,0},{8,12},{12,8},{1,5},{5,1},{9,13},{13,9},{2,6},{6,2},{1... | collective-permute-start | bytes 786440 | tf_op jit(solution)/shard_map/ppermute | solution.py:566
  58.2 6.5 %collective-permute-start.10 = (bf16[272,512]{1,0:T(8,128)(2,1)S(1)}, bf16[272,512]{1,0:T(8,128)(2,1)S(1)}, u32[]{:S(2)}, u32[]{:S(2)}) collective-permute-start(bf16[272,512]{1,0:T(8,128)(2,1)S(1)} %collective-permute-done.9.refs_0_), channel_id=1, source_target_pairs={{0,1},{1,0},{2,3},{3,2},{4,5},{5,4},{6,7},{7,6},{8,9},{9,8},{10,11... | collective-permute-start | bytes 835592 | tf_op jit(solution)/shard_map/ppermute | solution.py:490
  66.1 1.6 %collective-permute-start.12 = (bf16[1024,128]{1,0:T(8,128)(2,1)S(1)}, bf16[1024,128]{1,0:T(8,128)(2,1)S(1)}, u32[]{:S(2)}, u32[]{:S(2)}) collective-permute-start(bf16[1024,128]{1,0:T(8,128)(2,1)S(1)} %get-tuple-element.37), channel_id=1, source_target_pairs={{0,4},{4,0},{8,12},{12,8},{1,5},{5,1},{9,13},{13,9},{2,6},{6,2},{1... | collective-permute-start | bytes 786440 | tf_op jit(solution)/shard_map/ppermute | solution.py:570

commit v4 on v3

--- a/solution.py
+++ b/solution.py
@@ -7,7 +7,7 @@
 from jax.experimental.pallas import tpu as pltpu
 from jax.sharding import PartitionSpec as P
 
-HALO = 16
+HALO = 8
 VMEM_BYTES = 20 << 20
 
 
@@ -270,7 +270,9 @@
     return jnp.where(y < 0.5, y * series, 1.0 - jnp.exp(-y))
 
 
-def factors_kernel(clocks, partner_clocks, near, far, rate, out, columns):
+def factors_kernel(
+    clocks, partner_clocks, near, far, rate, admittance, out, reach, driven, columns
+):
     _, window, unit = out.shape
     length = clocks.shape[1]
     rows = near.shape[1] - 128
@@ -280,9 +282,13 @@
     columns[0:HALO, :] = jnp.where(half == 1, far[:, rows : rows + 8], near[:, rows : rows + 8])
     columns[pl.ds(first, length), :] = clocks[...].T
     columns[pl.ds(second, length), :] = partner_clocks[...].T
+
+    def part_of(array, slot):
+        start = pl.multiple_of((jnp.bitwise_xor(row, slot) * 2 + half) * unit, unit)
+        return array[:, pl.ds(start, unit)]
+
     index = lax.broadcasted_iota(jnp.int32, (window, unit), 0) & 7
-    start = pl.multiple_of((row * 2 + half) * unit, unit)
-    spent = columns[:, 0:1] * rate[:, pl.ds(start, unit)]
+    spent = columns[:, 0:1] * part_of(rate, 0)
     out[0] = jnp.sqrt(one_less_exp(2.0 * spent))
     kept = jnp.exp(-spent) * columns[:, 1:2]
     for slot, shift in ((1, 1), (2, 2), (3, 4)):
@@ -290,15 +296,34 @@
         out[slot] = jnp.where(inside, kept, 0.0)
         kept = jnp.where(inside, kept * pltpu.roll(kept, window - shift, 0), kept)
     out[4] = kept
-    carry = jnp.ones((1, unit), jnp.float32)
+
+    spans = jnp.broadcast_to(columns[:, 0:1], (window, 128))
+    shares = jnp.broadcast_to(columns[:, 1:2], (window, 128))
+    inside = index[:, 0:128]
+    for shift in (1, 2, 4):
+        later = pltpu.roll(spans, window - shift, 0)
+        spans = jnp.where(inside < 8 - shift, spans + later, spans)
+        later = pltpu.roll(shares, window - shift, 0)
+        shares = jnp.where(inside < 8 - shift, shares * later, shares)
+    span, share = jnp.zeros((1, 128), jnp.float32), jnp.ones((1, 128), jnp.float32)
+    all_spans, all_shares = [], []
     for group in range(window // 8 - 1, -1, -1):
-        block = kept[group * 8 : group * 8 + 8] * carry
-        out[5, group * 8 : group * 8 + 8, :] = block
-        carry = block[0:1]
-
-
-def recurrence_kernel(own, direct, paired, factors, partial, first):
+        all_spans.insert(0, spans[group * 8 : group * 8 + 8] + span)
+        all_shares.insert(0, shares[group * 8 : group * 8 + 8] * share)
+        span, share = all_spans[0][0:1], all_shares[0][0:1]
+    spans = jnp.concatenate(all_spans, 0)[:, 0:1]
+    shares = jnp.concatenate(all_shares, 0)[:, 0:1]
+    for slot in range(4):
+        left = jnp.exp(-(spans * part_of(rate, slot))) * shares
+        if slot == 0:
+            reach[...] = left
+        driven[slot] = left * part_of(admittance, slot)
+
+
+def recurrence_kernel(own, direct, paired, factors, admittance, partial, first, drive):
     window, unit = own.shape
+    row, half = lax.axis_index("row"), lax.axis_index("tm") % 2
+    gain = admittance[:, pl.ds(pl.multiple_of((row * 2 + half) * unit, unit), unit)]
     total = (
         own[...].astype(jnp.float32)
         + direct[...].astype(jnp.float32)
@@ -315,24 +340,25 @@
         carry = block[0:1]
         if group * 8 == HALO:
             first[...] = jnp.broadcast_to(carry, first.shape)
-
-
-def finish_kernel(incoming, admittance, partial, factors, drive, mine, theirs, states):
+    drive[...] = (gain * partial[...]).astype(drive.dtype)
+
+
+def finish_kernel(incoming, partial, reach, mine, theirs, states):
     window, unit = states.shape
     length = mine.shape[1]
-    row, half = lax.axis_index("row"), lax.axis_index("tm") % 2
+    half = lax.axis_index("tm") % 2
     first = pl.multiple_of(HALO + half * length, HALO)
     second = pl.multiple_of(HALO + (1 - half) * length, HALO)
-    start = pl.multiple_of((row * 2 + half) * unit, unit)
-    state = partial[...] + factors[5] * incoming[0:1, :]
-    drive[...] = (admittance[:, pl.ds(start, unit)] * state).astype(jnp.bfloat16)
-    states[...] = state
+    states[...] = partial[...] + reach[...] * incoming[0:1, :]
     mine[...] = states[pl.ds(first, length), :].T
     theirs[...] = states[pl.ds(second, length), :].T
 
 
-def reconstruct_kernel(count, at, stage, *refs):
-    drives, (kernels, *refs) = refs[:count], refs[count:]
+def reconstruct_kernel(slots, places, stage, *refs):
+    count = len(slots)
+    drives, incoming, kernels = (refs[i * count : (i + 1) * count] for i in range(3))
+    kernels = list(zip(kernels, places))
+    driven, *refs = refs[3 * count :]
     if stage == "last":
         before, keep, send, steps, lagged = refs
     elif stage == "next":
@@ -341,20 +367,23 @@
         total, steps, lagged = refs
     lags, width, _ = lagged.shape
     unit = drives[0].shape[1]
-    rows = kernels.shape[0] // lags
-    for slot, drive in enumerate(drives):
-        steps[:, slot * unit : slot * unit + unit] = drive[...].astype(jnp.float32)
+    for index, slot in enumerate(slots):
+        steps[:, index * unit : index * unit + unit] = (
+            drives[index][...].astype(jnp.float32) + driven[slot] * incoming[index][0:1, :]
+        )
     for lag in range(lags):
         lagged[lag] = steps[HALO - lag : HALO - lag + width, :].astype(jnp.bfloat16)
     added = None if stage == "first" else before[...]
-    for lag in range(lags):
-        term = lax.dot_general(
-            kernels[lag * rows : lag * rows + rows, at * unit : (at + count) * unit],
-            lagged[lag],
-            (((1,), (1,)), ((), ())),
-            preferred_element_type=jnp.float32,
-        )
-        added = term if added is None else added + term
+    for index, (kernel, at) in enumerate(kernels):
+        rows = kernel.shape[0] // lags
+        for lag in range(lags):
+            term = lax.dot_general(
+                kernel[lag * rows : lag * rows + rows, at * unit : at * unit + unit],
+                lagged[lag, :, index * unit : index * unit + unit],
+                (((1,), (1,)), ((), ())),
+                preferred_element_type=jnp.float32,
+            )
+            added = term if added is None else added + term
     if stage == "last":
         length = width // 2
         odd = lax.axis_index("tm") % 2 == 1
@@ -442,8 +471,8 @@
     got_far = lax.ppermute(edge, "tm", far)
 
     strip = jax.ShapeDtypeStruct((window, unit), bf16)
-    share_bytes = 2 * lags * rows * unit * 2
-    share_flops = 2 * 2 * lags * rows * unit * window
+    share_bytes = lags * rows * unit * 2
+    share_flops = 2 * lags * rows * unit * window
 
     def chosen(slots, columns):
         return call(
@@ -462,23 +491,24 @@
             correlate_kernel,
             "correlate",
             [vmem] * 5,
-            [vmem] * 3,
-            [strip] * 2 + [pltpu.VMEM((window, lags * rows), bf16)],
+            [vmem] * 2,
+            [strip, pltpu.VMEM((window, lags * rows), bf16)],
             [pltpu.VMEM((window + HALO, rows), f32)],
             share_flops,
             share_bytes // 2,
         )(own, partner, got_near, got_far, kernels)
 
     def correlated_again(lagged, kernels):
+        count = kernels.shape[1] // unit
         return call(
             correlate_again_kernel,
             "correlate",
             [vmem] * 2,
-            [vmem] * 2,
-            [strip] * 2,
+            [vmem] * count,
+            [strip] * count,
             [],
-            share_flops,
-            share_bytes // 2,
+            share_flops * count,
+            share_bytes * count // 2,
         )(lagged, kernels)
 
     def added(mine, theirs):
@@ -490,44 +520,60 @@
         return lax.ppermute(array, "row", [(i, i ^ by) for i in range(4)])
 
     def factored(clocks):
+        full = jax.ShapeDtypeStruct((window, unit), f32)
         return call(
             factors_kernel,
             "factors",
-            [vmem] * 5,
-            vmem,
-            jax.ShapeDtypeStruct((6, window, unit), f32),
+            [vmem] * 6,
+            [vmem] * 3,
+            [
+                jax.ShapeDtypeStruct((5, window, unit), f32),
+                full,
+                jax.ShapeDtypeStruct((4, window, unit), f32),
+            ],
             [pltpu.VMEM((window, 8), f32)],
             window * unit * 100,
-            window * unit * 24,
-        )(clocks, partner_clocks, got_near, got_far, element_damping_rate[None])
+            window * unit * 40,
+        )(
+            clocks,
+            partner_clocks,
+            got_near,
+            got_far,
+            element_damping_rate[None],
+            admittance[None],
+        )
 
     def recurrence(terms, factors):
         return call(
             recurrence_kernel,
             "recurrence",
-            [vmem] * 4,
-            [vmem] * 2,
-            [jax.ShapeDtypeStruct((window, unit), f32), jax.ShapeDtypeStruct((8, unit), f32)],
+            [vmem] * 5,
+            [vmem] * 3,
+            [
+                jax.ShapeDtypeStruct((window, unit), f32),
+                jax.ShapeDtypeStruct((8, unit), f32),
+                strip,
+            ],
             [],
             window * unit * 20,
             window * unit * 30,
-        )(*terms, factors)
-
-    def finished(partial, incoming, factors):
-        piece = jax.ShapeDtypeStruct((unit, length), f32)
+        )(*terms, factors, admittance[None])
+
+    def finished(partial, incoming, reach):
         return call(
             finish_kernel,
             "finish",
-            [vmem] * 4,
             [vmem] * 3,
-            [strip, piece, piece],
+            [vmem] * 2,
+            [jax.ShapeDtypeStruct((unit, length), f32)] * 2,
             [pltpu.VMEM((window, unit), f32)],
             window * unit * 10,
             window * unit * 16,
-        )(incoming, admittance[None], partial, factors)
-
-    def reconstructed(stage, at, drives, kernels, *before):
-        count = len(drives)
+        )(incoming, partial, reach)
+
+    def reconstructed(stage, slots, units, driven, *before):
+        count = len(slots)
+        drives, incoming, kernels, places = zip(*units)
         out_shape = jax.ShapeDtypeStruct((rows, 2 * length), f32)
         if stage == "last":
             out_shape = [
@@ -535,38 +581,47 @@
                 jax.ShapeDtypeStruct((rows, length), bf16),
             ]
         return call(
-            functools.partial(reconstruct_kernel, count, at, stage),
+            functools.partial(reconstruct_kernel, slots, places, stage),
             "reconstruct",
-            [vmem] * (count + 1 + len(before)),
+            [vmem] * (3 * count + 1 + len(before)),
             [vmem] * 2 if stage == "last" else vmem,
             out_shape,
             [
                 pltpu.VMEM((window, count * unit), f32),
                 pltpu.VMEM((lags, 2 * length, count * unit), bf16),
             ],
-            share_flops * count // 2,
-            share_bytes * count // 4,
-        )(*drives, kernels, *before)
-
-    far_kernels = chosen((2, 3), columns)
-    o2, o3, lagged = correlated(far_kernels)
+            share_flops * count,
+            share_bytes * count // 2,
+        )(*drives, *incoming, *kernels, driven, *before)
+
+    first_kernels = chosen((3,), columns)
+    o3, lagged = correlated(first_kernels)
     s3 = over_row(o3, 1)
-    late_columns, _ = barrier((columns, o2))
-    near_kernels = chosen((0, 1), late_columns)
-    o0, o1 = correlated_again(lagged, near_kernels)
-    paired = over_row(added(o2, s3), 2)
+    later, _ = barrier((columns, o3))
+    middle_kernels = chosen((2, 1), later)
+    o2, o1 = correlated_again(lagged, middle_kernels)
+    pair = added(o2, s3)
+    paired = over_row(pair, 2)
+    later, _ = barrier((columns, pair))
+    last_kernels = chosen((0,), later)
+    (o0,) = correlated_again(lagged, last_kernels)
     direct = over_row(o1, 1)
-    factors = factored(clocks)
-    partial, first = recurrence((o0, direct, paired), factors)
-    incoming = lax.ppermute(first, "tm", [(i, i - 2) for i in range(2, tm_count)])
-    drive, mine, theirs = finished(partial, incoming, factors)
-    d2 = over_row(drive, 2)
-    d1 = over_row(drive, 1)
+    factors, reach, driven = factored(clocks)
+    partial, first, d0 = recurrence((o0, direct, paired), factors)
+    d2 = over_row(d0, 2)
+    d1 = over_row(d0, 1)
     d3 = over_row(d2, 1)
+    i0 = lax.ppermute(first, "tm", [(i, i - 2) for i in range(2, tm_count)])
+    i2 = over_row(i0, 2)
+    i1 = over_row(i0, 1)
+    mine, theirs = finished(partial, i0, reach)
     theirs = lax.ppermute(theirs, "tm", swap)
-    total = reconstructed("first", 0, (drive, d1), near_kernels)
-    total = reconstructed("next", 0, (d2,), far_kernels, total)
-    keep, send = reconstructed("last", 1, (d3,), far_kernels, total)
+    near_units = [(d0, i0, last_kernels, 0), (d1, i1, middle_kernels, 1)]
+    total = reconstructed("first", (0, 1), near_units, driven)
+    late, _ = barrier((i2, total))
+    i3 = over_row(late, 1)
+    total = reconstructed("next", (2,), [(d2, i2, middle_kernels, 0)], driven, total)
+    keep, send = reconstructed("last", (3,), [(d3, i3, first_kernels, 0)], driven, total)
     pressure = keep + lax.ppermute(send, "tm", swap).astype(f32)
     state = jnp.where(
         odd, jnp.concatenate([theirs, mine], 0), jnp.concatenate([mine, theirs], 0)

time: 68.7 us -> 60.8 us (0.89)
  waiting for transfers between devices: 28.7 us -> 17.4 us
  Pallas kernels: 21.8 us -> 24.4 us
  starting transfers between devices: 15.6 us -> 16.4 us
    ppermute x6 -> x9, waiting for transfers between devices: 20.8 us -> 8.24 us  [over_row(): return lax.ppermute(array, 'row', [(i, i ^ by) for i in range(4)])]
    pallas_call x2 -> x3, Pallas kernels: 8.23 us -> 9.68 us  [chosen(): call(functools.partial(mask_kernel, slots), 'mask', [vmem] * 2 + [hbm], v...]
    pallas_call x8 -> x9, Pallas kernels: 12.1 us -> 13.3 us  [the longest x3 5.02 us: reconstructed(): call(functools.partial(reconstruct_kernel, slots, places, stage), 'recons...]
    ppermute x1, waiting for transfers between devices: 1.94 us -> 2.99 us  [paired(): got_far = lax.ppermute(edge, 'tm', far)]
    ppermute x6 -> x9, starting transfers between devices: 11.5 us -> 12.5 us  [over_row(): return lax.ppermute(array, 'row', [(i, i ^ by) for i in range(4)])]
  transfers between devices with their start and end apart: 13 -> 16, of which waited for: 8 -> 9; matrix products, arithmetic and copies ran while one was open for 1% -> 1% of each run, Pallas kernels for 25% -> 35%
where the time goes in v4:
time: 60.8 us; the launch traced here: 60.6 us
  Pallas kernels  24.4 us (40%)
  waiting for transfers between devices  17.4 us (29%)
  starting transfers between devices  16.4 us (27%)
  other arithmetic  1.59 us (3%)
  between operations  0.84 us (1%)
    ppermute x9, starting transfers between devices, over_row(): return lax.ppermute(array, 'row', [(i, i ^ by) for i in range(4)])  12.5 us
    pallas_call x3, Pallas kernels, chosen(): call(functools.partial(mask_kernel, slots), 'mask', [vmem] * 2 + [hbm], v...  9.68 us
    ppermute x9, waiting for transfers between devices, over_row(): return lax.ppermute(array, 'row', [(i, i ^ by) for i in range(4)])  8.24 us
    pallas_call x3, Pallas kernels, reconstructed(): call(functools.partial(reconstruct_kernel, slots, places, stage), 'recons...  5.02 us
    ppermute x1, waiting for transfers between devices, paired(): i0 = lax.ppermute(first, 'tm', [(i, i - 2) for i in range(2, tm_count)])  4.33 us
    pallas_call x2, Pallas kernels, correlated_again(): call(correlate_again_kernel, 'correlate', [vmem] * 2, [vmem] * count, [st...  3.94 us
    ppermute x1, waiting for transfers between devices, paired(): got_far = lax.ppermute(edge, 'tm', far)  2.99 us
    pallas_call x1, Pallas kernels, factored(): call(factors_kernel, 'factors', [vmem] * 6, [vmem] * 3, [jax.ShapeDtypeSt...  2.04 us
  transfers between devices with their start and end apart: 16, of which 9 were waited for; matrix products, arithmetic and copies ran while one was open for 1% of the time, Pallas kernels for 35%

profile of v4, /device:TPU:0, one launch (start us, length us, event | category | flops | bytes accessed | tf_op | source)
XLA Modules:
  0.0 60.6 jit_solution(6669430660248964813)
XLA Ops:
  0.6 1.4 %setup.1 = (f32[8,1152]{1,0:T(8,128)S(1)}, f32[8,128]{1,0:T(8,128)S(1)}, s32[1024,8]{1,0:T(8,128)S(1)}, s32[1,4096]{1,0:T(1,128)S(1)}, bf16[128,1024]{1,0:T(8,128)(2,1)S(1)}) custom-call(bf16[1024,128]{1,0:T(8,128)(2,1)} %traces_in.1, f32[1,128]{1,0:T(1,128)} %bitcast.9, f32[1,128]{1,0:T(1,128)} %bitcast.10, s32[4,32,32]{2,1,0:T(8,128)} %pattern_in.1, ...), custom_call_target="tpu_custom_call" | custom-call | flops 524288 | bytes 262144 | tf_op jit(solution)/shard_map/setup/pallas_call | solution.py:440
  2.0 0.5 collective-permute-start
  2.5 0.7 %collective-permute-start.1 = (f32[8,1152]{1,0:T(8,128)S(1)}, f32[8,1152]{1,0:T(8,128)S(1)}, u32[]{:S(2)}, u32[]{:S(2)}) collective-permute-start(f32[8,1152]{1,0:T(8,128)S(1)} %get-tuple-element.25), channel_id=1, source_target_pairs={{4,8},{8,4},{5,9},{9,5},{6,10},{10,6},{7,11},{11,7},{20,24},{24,20... | collective-permute-start | bytes 110600 | tf_op jit(solution)/shard_map/ppermute | solution.py:470
  3.2 1.3 %collective-permute-start.2 = (f32[8,1152]{1,0:T(8,128)S(1)}, f32[8,1152]{1,0:T(8,128)S(1)}, u32[]{:S(2)}, u32[]{:S(2)}) collective-permute-start(f32[8,1152]{1,0:T(8,128)S(1)} %get-tuple-element.25), channel_id=1, source_target_pairs={{4,12},{8,0},{5,13},{9,1},{6,14},{10,2},{7,15},{11,3},{20,28},{24,... | collective-permute-start | bytes 110600 | tf_op jit(solution)/shard_map/ppermute | solution.py:471
  4.5 2.7 %mask.3.kernels.refs_2_ = bf16[4096,512]{1,0:T(8,128)(2,1)S(1)} custom-call(s32[1024,8]{1,0:T(8,128)S(1)} %get-tuple-element.32.columns, s32[1,4096]{1,0:T(1,128)S(1)} %get-tuple-element.27.bits, bf16[4,1024,4096]{2,1,0:T(8,128)(2,1)} %weights.5), custom_call_target="tpu_custom_call" | custom-call | flops 4194304 | bytes 4194304 | tf_op jit(solution)/shard_map/mask/pallas_call | solution.py:478
  7.2 0.0 collective-permute-done.1.near
  7.2 3.0 %collective-permute-done.2.far = f32[8,1152]{1,0:T(8,128)S(1)} collective-permute-done((f32[8,1152]{1,0:T(8,128)S(1)}, f32[8,1152]{1,0:T(8,128)S(1)}, u32[]{:S(2)}, u32[]{:S(2)}) %collective-permute-start.2) | collective-permute-done | bytes 36896 | tf_op jit(solution)/shard_map/ppermute | solution.py:471
  10.2 0.0 collective-permute-done.partner
  10.2 1.4 %correlate.3 = (bf16[264,512]{1,0:T(8,128)(2,1)S(1)}, bf16[264,4096]{1,0:T(8,128)(2,1)S(1)}) custom-call(bf16[128,1024]{1,0:T(8,128)(2,1)S(1)} %get-tuple-element.24.own, bf16[128,1024]{1,0:T(8,128)(2,1)S(1)} %collective-permute-done.partner, f32[8,1152]{1,0:T(8,128)S(1)} %collective-permute-done.1.near, f32[8,1152]{1,0:T(8,128)S(1)} %collective-permute-done.2.far, ...), custom_call_target="tpu_custom_call" | custom-call | flops 1107296256 | bytes 2097152 | tf_op jit(solution)/shard_map/correlate/pallas_call | solution.py:490
  11.6 2.3 %collective-permute-start.3 = (bf16[264,512]{1,0:T(8,128)(2,1)S(1)}, bf16[264,512]{1,0:T(8,128)(2,1)S(1)}, u32[]{:S(2)}, u32[]{:S(2)}) collective-permute-start(bf16[264,512]{1,0:T(8,128)(2,1)S(1)} %get-tuple-element.29), channel_id=1, source_target_pairs={{0,1},{1,0},{2,3},{3,2},{4,5},{5,4},{6,7},{7,6},{8,9},{9,8},{10,11... | collective-permute-start | bytes 811016 | tf_op jit(solution)/shard_map/ppermute | solution.py:520
  13.8 4.1 %mask.4.kernels.refs_5_.refs_2_ = bf16[4096,1024]{1,0:T(8,128)(2,1)S(1)} custom-call(s32[1024,8]{1,0:T(8,128)S(1)} %get-tuple-element.32.columns, s32[1,4096]{1,0:T(1,128)S(1)} %get-tuple-element.27.bits, bf16[4,1024,4096]{2,1,0:T(8,128)(2,1)} %weights.5), custom_call_target="tpu_custom_call" | custom-call | flops 4194304 | bytes 4194304 | tf_op jit(solution)/shard_map/mask/pallas_call | solution.py:478
  18.0 0.0 copy-start
  18.0 0.0 copy-start.1
  18.0 2.5 %correlate.4 = (bf16[264,512]{1,0:T(8,128)(2,1)S(1)}, bf16[264,512]{1,0:T(8,128)(2,1)S(1)}) custom-call(bf16[264,4096]{1,0:T(8,128)(2,1)S(1)} %get-tuple-element.28.lagged, bf16[4096,1024]{1,0:T(8,128)(2,1)S(1)} %mask.4.kernels.refs_5_.refs_2_), custom_call_target="tpu_custom_call" | custom-call | flops 2214592512 | bytes 4194304 | tf_op jit(solution)/shard_map/correlate/pallas_call | solution.py:503
  20.4 0.1 collective-permute-start.4
  20.5 0.4 collective-permute-done.3.theirs
  20.9 0.1 pair.1
  21.0 2.7 %collective-permute-start.5 = (bf16[264,512]{1,0:T(8,128)(2,1)S(1)}, bf16[264,512]{1,0:T(8,128)(2,1)S(1)}, u32[]{:S(2)}, u32[]{:S(2)}) collective-permute-start(bf16[264,512]{1,0:T(8,128)(2,1)S(1)} %pair.1), channel_id=1, source_target_pairs={{0,2},{1,3},{2,0},{3,1},{4,6},{5,7},{6,4},{7,5},{8,10},{9,11},{10,... | collective-permute-start | bytes 811016 | tf_op jit(solution)/shard_map/ppermute | solution.py:520
  23.7 0.0 collective-permute-start.6
  23.7 1.2 %collective-permute-done.6.partner_clocks = f32[8,128]{1,0:T(8,128)S(1)} collective-permute-done((f32[8,128]{1,0:T(8,128)S(1)}, f32[8,128]{1,0:T(8,128)S(1)}, u32[]{:S(2)}, u32[]{:S(2)}) %collective-permute-start.6) | collective-permute-done | bytes 4128 | tf_op jit(solution)/shard_map/ppermute | solution.py:468
  24.8 0.0 copy-done
  24.8 0.0 copy-done.1
  24.8 2.0 %factors.1 = (f32[5,264,512]{2,1,0:T(8,128)S(1)}, f32[264,512]{1,0:T(8,128)S(1)}, f32[4,264,512]{2,1,0:T(8,128)S(1)}) custom-call(f32[8,128]{1,0:T(8,128)S(1)} %get-tuple-element.34.clocks, f32[8,128]{1,0:T(8,128)S(1)} %collective-permute-done.6.partner_clocks, f32[8,1152]{1,0:T(8,128)S(1)} %collective-permute-done.1.near, ...), custom_call_target="tpu_custom_call" | custom-call | flops 13516800 | bytes 5406720 | tf_op jit(solution)/shard_map/factors/pallas_call | solution.py:524
  26.9 2.9 %mask.5.kernels.refs_4_ = bf16[4096,512]{1,0:T(8,128)(2,1)S(1)} custom-call(s32[1024,8]{1,0:T(8,128)S(1)} %get-tuple-element.32.columns, s32[1,4096]{1,0:T(1,128)S(1)} %get-tuple-element.27.bits, bf16[4,1024,4096]{2,1,0:T(8,128)(2,1)} %weights.5), custom_call_target="tpu_custom_call" | custom-call | flops 4194304 | bytes 4194304 | tf_op jit(solution)/shard_map/mask/pallas_call | solution.py:478
  29.8 1.5 %correlate.5.own = bf16[264,512]{1,0:T(8,128)(2,1)S(1)} custom-call(bf16[264,4096]{1,0:T(8,128)(2,1)S(1)} %get-tuple-element.28.lagged, bf16[4096,512]{1,0:T(8,128)(2,1)S(1)} %mask.5.kernels.refs_4_), custom_call_target="tpu_custom_call" | custom-call | flops 1107296256 | bytes 2097152 | tf_op jit(solution)/shard_map/correlate/pallas_call | solution.py:503
  31.3 3.4 %collective-permute-done.4.direct = bf16[264,512]{1,0:T(8,128)(2,1)S(1)} collective-permute-done((bf16[264,512]{1,0:T(8,128)(2,1)S(1)}, bf16[264,512]{1,0:T(8,128)(2,1)S(1)}, u32[]{:S(2)}, u32[]{:S(2)}) %collective-permute-start.4) | collective-permute-done | bytes 270368 | tf_op jit(solution)/shard_map/ppermute | solution.py:520
  34.7 0.0 collective-permute-done.5.paired
  34.7 0.7 %recurrence.1 = (f32[264,512]{1,0:T(8,128)S(1)}, f32[8,512]{1,0:T(8,128)S(1)}, bf16[264,512]{1,0:T(8,128)(2,1)S(1)}) custom-call(bf16[264,512]{1,0:T(8,128)(2,1)S(1)} %correlate.5.own, bf16[264,512]{1,0:T(8,128)(2,1)S(1)} %collective-permute-done.4.direct, bf16[264,512]{1,0:T(8,128)(2,1)S(1)} %collective-permute-done.5.paired, ...), custom_call_target="tpu_custom_call" | custom-call | flops 2703360 | bytes 4055040 | tf_op jit(solution)/shard_map/recurrence/pallas_call | solution.py:547
  35.4 1.5 %collective-permute-start.9 = (bf16[264,512]{1,0:T(8,128)(2,1)S(1)}, bf16[264,512]{1,0:T(8,128)(2,1)S(1)}, u32[]{:S(2)}, u32[]{:S(2)}) collective-permute-start(bf16[264,512]{1,0:T(8,128)(2,1)S(1)} %get-tuple-element.41.refs_0_), channel_id=1, source_target_pairs={{0,2},{1,3},{2,0},{3,1},{4,6},{5,7},{6,4},{7,5},{8,10},{9,11},{10,... | collective-permute-start | bytes 811016 | tf_op jit(solution)/shard_map/ppermute | solution.py:520
  36.9 4.0 %collective-permute-start.12 = (bf16[264,512]{1,0:T(8,128)(2,1)S(1)}, bf16[264,512]{1,0:T(8,128)(2,1)S(1)}, u32[]{:S(2)}, u32[]{:S(2)}) collective-permute-start(bf16[264,512]{1,0:T(8,128)(2,1)S(1)} %get-tuple-element.41.refs_0_), channel_id=1, source_target_pairs={{0,1},{1,0},{2,3},{3,2},{4,5},{5,4},{6,7},{7,6},{8,9},{9,8},{10,11... | collective-permute-start | bytes 811016 | tf_op jit(solution)/shard_map/ppermute | solution.py:520
  40.8 1.3 %collective-permute-start.7 = (f32[8,512]{1,0:T(8,128)S(1)}, f32[8,512]{1,0:T(8,128)S(1)}, u32[]{:S(2)}, u32[]{:S(2)}) collective-permute-start(f32[8,512]{1,0:T(8,128)S(1)} %get-tuple-element.36), channel_id=1, source_target_pairs={{8,0},{12,4},{9,1},{13,5},{10,2},{14,6},{11,3},{15,7},{24,16},{28,... | collective-permute-start | bytes 49160 | tf_op jit(solution)/shard_map/ppermute | solution.py:614
  42.1 4.3 %collective-permute-done.7.incoming.refs_2_ = f32[8,512]{1,0:T(8,128)S(1)} collective-permute-done((f32[8,512]{1,0:T(8,128)S(1)}, f32[8,512]{1,0:T(8,128)S(1)}, u32[]{:S(2)}, u32[]{:S(2)}) %collective-permute-start.7) | collective-permute-done | bytes 16416 | tf_op jit(solution)/shard_map/ppermute | solution.py:614
  46.5 0.0 collective-permute-start.13
  46.5 0.3 finish.1
  46.7 0.1 collective-permute-start.8
  46.8 0.2 collective-permute-start.11
  47.0 2.8 %collective-permute-done.9.refs_0_ = bf16[264,512]{1,0:T(8,128)(2,1)S(1)} collective-permute-done((bf16[264,512]{1,0:T(8,128)(2,1)S(1)}, bf16[264,512]{1,0:T(8,128)(2,1)S(1)}, u32[]{:S(2)}, u32[]{:S(2)}) %collective-permute-start.9) | collective-permute-done | bytes 270368 | tf_op jit(solution)/shard_map/ppermute | solution.py:520
  49.8 0.1 collective-permute-start.10
  49.9 0.3 collective-permute-done.13.refs_3_
  50.2 0.0 collective-permute-done.12.refs_1_
  50.2 2.4 %reconstruct.3.refs_4_ = f32[1024,256]{1,0:T(8,128)S(1)} custom-call(bf16[264,512]{1,0:T(8,128)(2,1)S(1)} %get-tuple-element.41.refs_0_, bf16[264,512]{1,0:T(8,128)(2,1)S(1)} %collective-permute-done.12.refs_1_, f32[8,512]{1,0:T(8,128)S(1)} %collective-permute-done.7.incoming.refs_2_, f32[8,512]{1,0:T(8,128)S(1)} %collective-permute-done.13.refs_3_, ...), custom_call_target="tpu_custom_call" | custom-call | flops 2214592512 | bytes 4194304 | tf_op jit(solution)/shard_map/reconstruct/pallas_call | solution.py:583
  52.6 0.0 collective-permute-done.11.refs_1_
  52.6 1.6 %collective-permute-start.14 = (f32[8,512]{1,0:T(8,128)S(1)}, f32[8,512]{1,0:T(8,128)S(1)}, u32[]{:S(2)}, u32[]{:S(2)}) collective-permute-start(f32[8,512]{1,0:T(8,128)S(1)} %collective-permute-done.11.refs_1_), channel_id=1, source_target_pairs={{0,1},{1,0},{2,3},{3,2},{4,5},{5,4},{6,7},{7,6},{8,9},{9,8},{10,11... | collective-permute-start | bytes 49160 | tf_op jit(solution)/shard_map/ppermute | solution.py:520
  54.3 1.3 %reconstruct.4.refs_4_ = f32[1024,256]{1,0:T(8,128)S(1)} custom-call(bf16[264,512]{1,0:T(8,128)(2,1)S(1)} %collective-permute-done.9.refs_0_, f32[8,512]{1,0:T(8,128)S(1)} %collective-permute-done.11.refs_1_, bf16[4096,1024]{1,0:T(8,128)(2,1)S(1)} %mask.4.kernels.refs_5_.refs_2_, f32[4,264,512]{2,1,0:T(8,128)S(1)} %get-tuple-element.42.refs_6_.refs_3_, ...), custom_call_target="tpu_custom_call" | custom-call | flops 1107296256 | bytes 2097152 | tf_op jit(solution)/shard_map/reconstruct/pallas_call | solution.py:583
  55.6 1.4 %collective-permute-done.14.refs_1_ = f32[8,512]{1,0:T(8,128)S(1)} collective-permute-done((f32[8,512]{1,0:T(8,128)S(1)}, f32[8,512]{1,0:T(8,128)S(1)}, u32[]{:S(2)}, u32[]{:S(2)}) %collective-permute-start.14) | collective-permute-done | bytes 16416 | tf_op jit(solution)/shard_map/ppermute | solution.py:520
  57.0 0.0 collective-permute-done.10.refs_0_
  57.0 1.3 %reconstruct.5 = (f32[1024,128]{1,0:T(8,128)S(1)}, bf16[1024,128]{1,0:T(8,128)(2,1)S(1)}) custom-call(bf16[264,512]{1,0:T(8,128)(2,1)S(1)} %collective-permute-done.10.refs_0_, f32[8,512]{1,0:T(8,128)S(1)} %collective-permute-done.14.refs_1_, bf16[4096,512]{1,0:T(8,128)(2,1)S(1)} %mask.3.kernels.refs_2_, ...), custom_call_target="tpu_custom_call" | custom-call | flops 1107296256 | bytes 2097152 | tf_op jit(solution)/shard_map/reconstruct/pallas_call | solution.py:583
  58.3 0.1 collective-permute-start.15
  58.4 0.0 collective-permute-done.8
  58.4 0.8 %maximum_select_fusion = f32[1024,128]{1,0:T(8,128)} fusion(f32[512,128]{1,0:T(8,128)S(1)} %get-tuple-element.40, f32[512,128]{1,0:T(8,128)S(1)} %collective-permute-done.8, pred[]{:T(512)S(6)} %eq.5), kind=kLoop, calls=%fused_computation | loop fusion | flops 393216 | bytes 1048577 | tf_op jit(solution)/shard_map/jit(_where)/select_n | solution.py:626
  59.2 0.7 %collective-permute-done.15 = bf16[1024,128]{1,0:T(8,128)(2,1)S(1)} collective-permute-done((bf16[1024,128]{1,0:T(8,128)(2,1)S(1)}, bf16[1024,128]{1,0:T(8,128)(2,1)S(1)}, u32[]{:S(2)}, u32[]{:S(2)}) %collective-permute-start.15) | collective-permute-done | bytes 262176 | tf_op jit(solution)/shard_map/ppermute | solution.py:625
  59.9 0.8 %add_convert_fusion = bf16[1024,128]{1,0:T(8,128)(2,1)} fusion(f32[1024,128]{1,0:T(8,128)S(1)} %get-tuple-element.44, bf16[1024,128]{1,0:T(8,128)(2,1)S(1)} %collective-permute-done.15), kind=kLoop, calls=%fused_computation.1 | loop fusion | flops 393216 | bytes 1048576 | tf_op jit(solution)/shard_map/convert_element_type | solution.py:629
Async XLA Ops:
  2.0 8.2 %collective-permute-start = (bf16[128,1024]{1,0:T(8,128)(2,1)S(1)}, bf16[128,1024]{1,0:T(8,128)(2,1)S(1)}, u32[]{:S(2)}, u32[]{:S(2)}) collective-permute-start(bf16[128,1024]{1,0:T(8,128)(2,1)S(1)} %get-tuple-element.24.own), channel_id=1, source_target_pairs={{0,4},{4,0},{8,12},{12,8},{1,5},{5,1},{9,13},{13,9},{2,6},{6,2},{1... | collective-permute-start | bytes 786440 | tf_op jit(solution)/shard_map/ppermute | solution.py:469
  2.5 4.6 %collective-permute-start.1 = (f32[8,1152]{1,0:T(8,128)S(1)}, f32[8,1152]{1,0:T(8,128)S(1)}, u32[]{:S(2)}, u32[]{:S(2)}) collective-permute-start(f32[8,1152]{1,0:T(8,128)S(1)} %get-tuple-element.25), channel_id=1, source_target_pairs={{4,8},{8,4},{5,9},{9,5},{6,10},{10,6},{7,11},{11,7},{20,24},{24,20... | collective-permute-start | bytes 110600 | tf_op jit(solution)/shard_map/ppermute | solution.py:470
  3.2 7.0 %collective-permute-start.2 = (f32[8,1152]{1,0:T(8,128)S(1)}, f32[8,1152]{1,0:T(8,128)S(1)}, u32[]{:S(2)}, u32[]{:S(2)}) collective-permute-start(f32[8,1152]{1,0:T(8,128)S(1)} %get-tuple-element.25), channel_id=1, source_target_pairs={{4,12},{8,0},{5,13},{9,1},{6,14},{10,2},{7,15},{11,3},{20,28},{24,... | collective-permute-start | bytes 110600 | tf_op jit(solution)/shard_map/ppermute | solution.py:471
  11.6 9.3 %collective-permute-start.3 = (bf16[264,512]{1,0:T(8,128)(2,1)S(1)}, bf16[264,512]{1,0:T(8,128)(2,1)S(1)}, u32[]{:S(2)}, u32[]{:S(2)}) collective-permute-start(bf16[264,512]{1,0:T(8,128)(2,1)S(1)} %get-tuple-element.29), channel_id=1, source_target_pairs={{0,1},{1,0},{2,3},{3,2},{4,5},{5,4},{6,7},{7,6},{8,9},{9,8},{10,11... | collective-permute-start | bytes 811016 | tf_op jit(solution)/shard_map/ppermute | solution.py:520
  18.0 6.9 %copy-start = (f32[4096]{0:T(1024)S(1)}, f32[4096]{0:T(1024)}, u32[]{:S(2)}) copy-start(f32[4096]{0:T(1024)} %param.15) | copy-start | bytes 49156
  18.0 6.9 %copy-start.1 = (f32[4096]{0:T(1024)S(1)}, f32[4096]{0:T(1024)}, u32[]{:S(2)}) copy-start(f32[4096]{0:T(1024)} %param.12) | copy-start | bytes 49156
  20.4 14.2 %collective-permute-start.4 = (bf16[264,512]{1,0:T(8,128)(2,1)S(1)}, bf16[264,512]{1,0:T(8,128)(2,1)S(1)}, u32[]{:S(2)}, u32[]{:S(2)}) collective-permute-start(bf16[264,512]{1,0:T(8,128)(2,1)S(1)} %get-tuple-element.33), channel_id=1, source_target_pairs={{0,1},{1,0},{2,3},{3,2},{4,5},{5,4},{6,7},{7,6},{8,9},{9,8},{10,11... | collective-permute-start | bytes 811016 | tf_op jit(solution)/shard_map/ppermute | solution.py:520
  21.0 13.7 %collective-permute-start.5 = (bf16[264,512]{1,0:T(8,128)(2,1)S(1)}, bf16[264,512]{1,0:T(8,128)(2,1)S(1)}, u32[]{:S(2)}, u32[]{:S(2)}) collective-permute-start(bf16[264,512]{1,0:T(8,128)(2,1)S(1)} %pair.1), channel_id=1, source_target_pairs={{0,2},{1,3},{2,0},{3,1},{4,6},{5,7},{6,4},{7,5},{8,10},{9,11},{10,... | collective-permute-start | bytes 811016 | tf_op jit(solution)/shard_map/ppermute | solution.py:520
  23.7 1.2 %collective-permute-start.6 = (f32[8,128]{1,0:T(8,128)S(1)}, f32[8,128]{1,0:T(8,128)S(1)}, u32[]{:S(2)}, u32[]{:S(2)}) collective-permute-start(f32[8,128]{1,0:T(8,128)S(1)} %get-tuple-element.34.clocks), channel_id=1, source_target_pairs={{0,4},{4,0},{8,12},{12,8},{1,5},{5,1},{9,13},{13,9},{2,6},{6,2},{1... | collective-permute-start | bytes 12296 | tf_op jit(solution)/shard_map/ppermute | solution.py:468
  35.4 14.4 %collective-permute-start.9 = (bf16[264,512]{1,0:T(8,128)(2,1)S(1)}, bf16[264,512]{1,0:T(8,128)(2,1)S(1)}, u32[]{:S(2)}, u32[]{:S(2)}) collective-permute-start(bf16[264,512]{1,0:T(8,128)(2,1)S(1)} %get-tuple-element.41.refs_0_), channel_id=1, source_target_pairs={{0,2},{1,3},{2,0},{3,1},{4,6},{5,7},{6,4},{7,5},{8,10},{9,11},{10,... | collective-permute-start | bytes 811016 | tf_op jit(solution)/shard_map/ppermute | solution.py:520
  36.9 13.3 %collective-permute-start.12 = (bf16[264,512]{1,0:T(8,128)(2,1)S(1)}, bf16[264,512]{1,0:T(8,128)(2,1)S(1)}, u32[]{:S(2)}, u32[]{:S(2)}) collective-permute-start(bf16[264,512]{1,0:T(8,128)(2,1)S(1)} %get-tuple-element.41.refs_0_), channel_id=1, source_target_pairs={{0,1},{1,0},{2,3},{3,2},{4,5},{5,4},{6,7},{7,6},{8,9},{9,8},{10,11... | collective-permute-start | bytes 811016 | tf_op jit(solution)/shard_map/ppermute | solution.py:520
  40.8 5.6 %collective-permute-start.7 = (f32[8,512]{1,0:T(8,128)S(1)}, f32[8,512]{1,0:T(8,128)S(1)}, u32[]{:S(2)}, u32[]{:S(2)}) collective-permute-start(f32[8,512]{1,0:T(8,128)S(1)} %get-tuple-element.36), channel_id=1, source_target_pairs={{8,0},{12,4},{9,1},{13,5},{10,2},{14,6},{11,3},{15,7},{24,16},{28,... | collective-permute-start | bytes 49160 | tf_op jit(solution)/shard_map/ppermute | solution.py:614
  46.5 3.7 %collective-permute-start.13 = (f32[8,512]{1,0:T(8,128)S(1)}, f32[8,512]{1,0:T(8,128)S(1)}, u32[]{:S(2)}, u32[]{:S(2)}) collective-permute-start(f32[8,512]{1,0:T(8,128)S(1)} %collective-permute-done.7.incoming.refs_2_), channel_id=1, source_target_pairs={{0,1},{1,0},{2,3},{3,2},{4,5},{5,4},{6,7},{7,6},{8,9},{9,8},{10,11... | collective-permute-start | bytes 49160 | tf_op jit(solution)/shard_map/ppermute | solution.py:520
  46.7 11.6 %collective-permute-start.8 = (f32[512,128]{1,0:T(8,128)S(1)}, f32[512,128]{1,0:T(8,128)S(1)}, u32[]{:S(2)}, u32[]{:S(2)}) collective-permute-start(f32[512,128]{1,0:T(8,128)S(1)} %get-tuple-element.39), channel_id=1, source_target_pairs={{0,4},{4,0},{8,12},{12,8},{1,5},{5,1},{9,13},{13,9},{2,6},{6,2},{1... | collective-permute-start | bytes 786440 | tf_op jit(solution)/shard_map/ppermute | solution.py:618
  46.8 5.8 %collective-permute-start.11 = (f32[8,512]{1,0:T(8,128)S(1)}, f32[8,512]{1,0:T(8,128)S(1)}, u32[]{:S(2)}, u32[]{:S(2)}) collective-permute-start(f32[8,512]{1,0:T(8,128)S(1)} %collective-permute-done.7.incoming.refs_2_), channel_id=1, source_target_pairs={{0,2},{1,3},{2,0},{3,1},{4,6},{5,7},{6,4},{7,5},{8,10},{9,11},{10,... | collective-permute-start | bytes 49160 | tf_op jit(solution)/shard_map/ppermute | solution.py:520
  49.8 7.2 %collective-permute-start.10 = (bf16[264,512]{1,0:T(8,128)(2,1)S(1)}, bf16[264,512]{1,0:T(8,128)(2,1)S(1)}, u32[]{:S(2)}, u32[]{:S(2)}) collective-permute-start(bf16[264,512]{1,0:T(8,128)(2,1)S(1)} %collective-permute-done.9.refs_0_), channel_id=1, source_target_pairs={{0,1},{1,0},{2,3},{3,2},{4,5},{5,4},{6,7},{7,6},{8,9},{9,8},{10,11... | collective-permute-start | bytes 811016 | tf_op jit(solution)/shard_map/ppermute | solution.py:520
  52.6 4.3 %collective-permute-start.14 = (f32[8,512]{1,0:T(8,128)S(1)}, f32[8,512]{1,0:T(8,128)S(1)}, u32[]{:S(2)}, u32[]{:S(2)}) collective-permute-start(f32[8,512]{1,0:T(8,128)S(1)} %collective-permute-done.11.refs_1_), channel_id=1, source_target_pairs={{0,1},{1,0},{2,3},{3,2},{4,5},{5,4},{6,7},{7,6},{8,9},{9,8},{10,11... | collective-permute-start | bytes 49160 | tf_op jit(solution)/shard_map/ppermute | solution.py:520
  58.3 1.6 %collective-permute-start.15 = (bf16[1024,128]{1,0:T(8,128)(2,1)S(1)}, bf16[1024,128]{1,0:T(8,128)(2,1)S(1)}, u32[]{:S(2)}, u32[]{:S(2)}) collective-permute-start(bf16[1024,128]{1,0:T(8,128)(2,1)S(1)} %get-tuple-element.45), channel_id=1, source_target_pairs={{0,4},{4,0},{8,12},{12,8},{1,5},{5,1},{9,13},{13,9},{2,6},{6,2},{1... | collective-permute-start | bytes 786440 | tf_op jit(solution)/shard_map/ppermute | solution.py:625

commit v5 on v4

--- a/solution.py
+++ b/solution.py
@@ -218,12 +218,14 @@
         if index == 0:
             spread[...] = jnp.broadcast_to(columns[:, lag : lag + 1], (rows, 128))
         fetch(lag, index).wait()
-        for at in range(0, unit, 128):
-            place = slice(lag * rows, lag * rows + rows)
-            part = slice(index * unit + at, index * unit + at + 128)
-            weight = kernels[place, part]
-            keep = (spread[...] & picked[index][:, at : at + 128]) != 0
-            kernels[place, part] = jnp.where(keep, weight, jnp.zeros_like(weight))
+        for top in range(0, rows, 128):
+            word = spread[top : top + 128, :]
+            place = slice(lag * rows + top, lag * rows + top + 128)
+            for at in range(0, unit, 128):
+                part = slice(index * unit + at, index * unit + at + 128)
+                weight = kernels[place, part]
+                keep = (word & picked[index][:, at : at + 128]) != 0
+                kernels[place, part] = jnp.where(keep, weight, jnp.zeros_like(weight))
 
 
 def correlate_kernel(own, partner, near, far, kernels, *refs):
@@ -245,7 +247,9 @@
     multiply(lagged, kernels, outs)
 
 
-def correlate_again_kernel(lagged, kernels, *outs):
+def mask_correlate_kernel(slots, lagged, columns, bits, weights, *refs):
+    *outs, kernels, spread, arrived = refs
+    mask_kernel(slots, columns, bits, weights, kernels, spread, arrived)
     multiply(lagged, kernels, outs)
 
 
@@ -271,7 +275,7 @@
 
 
 def factors_kernel(
-    clocks, partner_clocks, near, far, rate, admittance, out, reach, driven, columns
+    clocks, partner_clocks, near, far, rate, out, columns
 ):
     _, window, unit = out.shape
     length = clocks.shape[1]
@@ -283,12 +287,9 @@
     columns[pl.ds(first, length), :] = clocks[...].T
     columns[pl.ds(second, length), :] = partner_clocks[...].T
 
-    def part_of(array, slot):
-        start = pl.multiple_of((jnp.bitwise_xor(row, slot) * 2 + half) * unit, unit)
-        return array[:, pl.ds(start, unit)]
-
+    start = pl.multiple_of((row * 2 + half) * unit, unit)
     index = lax.broadcasted_iota(jnp.int32, (window, unit), 0) & 7
-    spent = columns[:, 0:1] * part_of(rate, 0)
+    spent = columns[:, 0:1] * rate[:, pl.ds(start, unit)]
     out[0] = jnp.sqrt(one_less_exp(2.0 * spent))
     kept = jnp.exp(-spent) * columns[:, 1:2]
     for slot, shift in ((1, 1), (2, 2), (3, 4)):
@@ -297,9 +298,18 @@
         kept = jnp.where(inside, kept * pltpu.roll(kept, window - shift, 0), kept)
     out[4] = kept
 
+
+def reach_kernel(columns, rate, admittance, reach, driven):
+    _, window, unit = driven.shape
+    row, half = lax.axis_index("row"), lax.axis_index("tm") % 2
+
+    def part_of(array, slot):
+        start = pl.multiple_of((jnp.bitwise_xor(row, slot) * 2 + half) * unit, unit)
+        return array[:, pl.ds(start, unit)]
+
     spans = jnp.broadcast_to(columns[:, 0:1], (window, 128))
     shares = jnp.broadcast_to(columns[:, 1:2], (window, 128))
-    inside = index[:, 0:128]
+    inside = lax.broadcasted_iota(jnp.int32, (window, 128), 0) & 7
     for shift in (1, 2, 4):
         later = pltpu.roll(spans, window - shift, 0)
         spans = jnp.where(inside < 8 - shift, spans + later, spans)
@@ -333,6 +343,7 @@
     for slot, shift in ((1, 1), (2, 2), (3, 4)):
         state = state + factors[slot] * pltpu.roll(state, window - shift, 0)
     carry = jnp.zeros((1, unit), jnp.float32)
+    waiting = None
     for group in range(window // 8 - 1, -1, -1):
         rows = slice(group * 8, group * 8 + 8)
         block = state[rows] + factors[4, rows, :] * carry
@@ -340,7 +351,14 @@
         carry = block[0:1]
         if group * 8 == HALO:
             first[...] = jnp.broadcast_to(carry, first.shape)
-    drive[...] = (gain * partial[...]).astype(drive.dtype)
+        if waiting is not None:
+            both = jnp.concatenate([gain * block, waiting], 0)
+            drive[group * 8 : group * 8 + 16, :] = both.astype(drive.dtype)
+            waiting = None
+        elif group % 2 == 0:
+            drive[rows, :] = (gain * block).astype(drive.dtype)
+        else:
+            waiting = gain * block
 
 
 def finish_kernel(incoming, partial, reach, mine, theirs, states):
@@ -498,18 +516,18 @@
             share_bytes // 2,
         )(own, partner, got_near, got_far, kernels)
 
-    def correlated_again(lagged, kernels):
-        count = kernels.shape[1] // unit
-        return call(
-            correlate_again_kernel,
+    def correlated_again(lagged, slots, columns):
+        count = len(slots)
+        return call(
+            functools.partial(mask_correlate_kernel, slots),
             "correlate",
-            [vmem] * 2,
-            [vmem] * count,
-            [strip] * count,
-            [],
+            [vmem] * 3 + [hbm],
+            [vmem] * (count + 1),
+            [strip] * count + [pltpu.VMEM((lags * rows, count * unit), bf16)],
+            [pltpu.VMEM((rows, 128), jnp.int32), pltpu.SemaphoreType.DMA((count, lags))],
             share_flops * count,
-            share_bytes * count // 2,
-        )(lagged, kernels)
+            share_bytes * count,
+        )(lagged, columns, bits, weights)
 
     def added(mine, theirs):
         return call(
@@ -520,28 +538,34 @@
         return lax.ppermute(array, "row", [(i, i ^ by) for i in range(4)])
 
     def factored(clocks):
-        full = jax.ShapeDtypeStruct((window, unit), f32)
         return call(
             factors_kernel,
             "factors",
-            [vmem] * 6,
-            [vmem] * 3,
+            [vmem] * 5,
+            [vmem] * 2,
             [
                 jax.ShapeDtypeStruct((5, window, unit), f32),
-                full,
+                jax.ShapeDtypeStruct((window, 8), f32),
+            ],
+            [],
+            window * unit * 80,
+            window * unit * 20,
+        )(clocks, partner_clocks, got_near, got_far, element_damping_rate[None])
+
+    def reaching(columns):
+        return call(
+            reach_kernel,
+            "reach",
+            [vmem] * 3,
+            [vmem] * 2,
+            [
+                jax.ShapeDtypeStruct((window, unit), f32),
                 jax.ShapeDtypeStruct((4, window, unit), f32),
             ],
-            [pltpu.VMEM((window, 8), f32)],
-            window * unit * 100,
+            [],
             window * unit * 40,
-        )(
-            clocks,
-            partner_clocks,
-            got_near,
-            got_far,
-            element_damping_rate[None],
-            admittance[None],
-        )
+            window * unit * 20,
+        )(columns, element_damping_rate[None], admittance[None])
 
     def recurrence(terms, factors):
         return call(
@@ -598,16 +622,16 @@
     o3, lagged = correlated(first_kernels)
     s3 = over_row(o3, 1)
     later, _ = barrier((columns, o3))
-    middle_kernels = chosen((2, 1), later)
-    o2, o1 = correlated_again(lagged, middle_kernels)
+    o2, o1, middle_kernels = correlated_again(lagged, (2, 1), later)
     pair = added(o2, s3)
     paired = over_row(pair, 2)
     later, _ = barrier((columns, pair))
-    last_kernels = chosen((0,), later)
-    (o0,) = correlated_again(lagged, last_kernels)
+    o0, last_kernels = correlated_again(lagged, (0,), later)
     direct = over_row(o1, 1)
-    factors, reach, driven = factored(clocks)
+    factors, step_columns = factored(clocks)
     partial, first, d0 = recurrence((o0, direct, paired), factors)
+    late_columns, _ = barrier((step_columns, d0))
+    reach, driven = reaching(late_columns)
     d2 = over_row(d0, 2)
     d1 = over_row(d0, 1)
     d3 = over_row(d2, 1)

time: 60.8 us -> 60.6 us (level)
  Pallas kernels: 24.4 us -> 23.1 us
  waiting for transfers between devices: 17.4 us -> 18.3 us
    pallas_call x3 -> x1, Pallas kernels: 9.68 us -> 2.63 us  [chosen(): call(functools.partial(mask_kernel, slots), 'mask', [vmem] * 2 + [hbm], v...]
    pallas_call x3 -> x4, Pallas kernels: 5.98 us -> 11.9 us  [the longest x2 9.88 us: correlated_again(): call(functools.partial(mask_correlate_kernel, slots), 'correlate', [vmem]...]
    ppermute x9, waiting for transfers between devices: 8.24 us -> 9.27 us  [over_row(): return lax.ppermute(array, 'row', [(i, i ^ by) for i in range(4)])]
  transfers between devices with their start and end apart: 16 -> 16, of which waited for: 9 -> 9; matrix products, arithmetic and copies ran while one was open for 1% -> 1% of each run, Pallas kernels for 35% -> 33%
where the time goes in v5:
time: 60.6 us; the launch traced here: 60.4 us
  Pallas kernels  23.1 us (38%)
  waiting for transfers between devices  18.3 us (30%)
  starting transfers between devices  16.7 us (28%)
  other arithmetic  1.59 us (3%)
  between operations  0.82 us (1%)
    ppermute x9, starting transfers between devices, over_row(): return lax.ppermute(array, 'row', [(i, i ^ by) for i in range(4)])  12.6 us
    pallas_call x2, Pallas kernels, correlated_again(): call(functools.partial(mask_correlate_kernel, slots), 'correlate', [vmem]...  9.88 us
    ppermute x9, waiting for transfers between devices, over_row(): return lax.ppermute(array, 'row', [(i, i ^ by) for i in range(4)])  9.27 us
    pallas_call x3, Pallas kernels, reconstructed(): call(functools.partial(reconstruct_kernel, slots, places, stage), 'recons...  5.01 us
    ppermute x1, waiting for transfers between devices, paired(): i0 = lax.ppermute(first, 'tm', [(i, i - 2) for i in range(2, tm_count)])  4.15 us
    ppermute x1, waiting for transfers between devices, paired(): got_far = lax.ppermute(edge, 'tm', far)  3.03 us
    pallas_call x1, Pallas kernels, chosen(): call(functools.partial(mask_kernel, slots), 'mask', [vmem] * 2 + [hbm], v...  2.63 us
    ppermute x1, starting transfers between devices, paired(): i0 = lax.ppermute(first, 'tm', [(i, i - 2) for i in range(2, tm_count)])  1.46 us
  transfers between devices with their start and end apart: 16, of which 9 were waited for; matrix products, arithmetic and copies ran while one was open for 1% of the time, Pallas kernels for 33%

profile of v5, /device:TPU:0, one launch (start us, length us, event | category | flops | bytes accessed | tf_op | source)
XLA Modules:
  0.0 60.4 jit_solution(4313237625915058063)
XLA Ops:
  0.6 1.4 %setup.1 = (f32[8,1152]{1,0:T(8,128)S(1)}, f32[8,128]{1,0:T(8,128)S(1)}, s32[1024,8]{1,0:T(8,128)S(1)}, s32[1,4096]{1,0:T(1,128)S(1)}, bf16[128,1024]{1,0:T(8,128)(2,1)S(1)}) custom-call(bf16[1024,128]{1,0:T(8,128)(2,1)} %traces_in.1, f32[1,128]{1,0:T(1,128)} %bitcast.10, f32[1,128]{1,0:T(1,128)} %bitcast.11, s32[4,32,32]{2,1,0:T(8,128)} %pattern_in.1, ...), custom_call_target="tpu_custom_call" | custom-call | flops 524288 | bytes 262144 | tf_op jit(solution)/shard_map/setup/pallas_call | solution.py:458
  2.0 0.5 collective-permute-start
  2.5 0.7 %collective-permute-start.1 = (f32[8,1152]{1,0:T(8,128)S(1)}, f32[8,1152]{1,0:T(8,128)S(1)}, u32[]{:S(2)}, u32[]{:S(2)}) collective-permute-start(f32[8,1152]{1,0:T(8,128)S(1)} %get-tuple-element.30), channel_id=1, source_target_pairs={{4,8},{8,4},{5,9},{9,5},{6,10},{10,6},{7,11},{11,7},{20,24},{24,20... | collective-permute-start | bytes 110600 | tf_op jit(solution)/shard_map/ppermute | solution.py:488
  3.2 1.3 %collective-permute-start.2 = (f32[8,1152]{1,0:T(8,128)S(1)}, f32[8,1152]{1,0:T(8,128)S(1)}, u32[]{:S(2)}, u32[]{:S(2)}) collective-permute-start(f32[8,1152]{1,0:T(8,128)S(1)} %get-tuple-element.30), channel_id=1, source_target_pairs={{4,12},{8,0},{5,13},{9,1},{6,14},{10,2},{7,15},{11,3},{20,28},{24,... | collective-permute-start | bytes 110600 | tf_op jit(solution)/shard_map/ppermute | solution.py:489
  4.5 2.6 %mask.1.kernels.refs_2_ = bf16[4096,512]{1,0:T(8,128)(2,1)S(1)} custom-call(s32[1024,8]{1,0:T(8,128)S(1)} %get-tuple-element.37.columns, s32[1,4096]{1,0:T(1,128)S(1)} %get-tuple-element.32.bits, bf16[4,1024,4096]{2,1,0:T(8,128)(2,1)} %weights.5), custom_call_target="tpu_custom_call" | custom-call | flops 4194304 | bytes 4194304 | tf_op jit(solution)/shard_map/mask/pallas_call | solution.py:496
  7.1 0.0 collective-permute-done.1.near
  7.1 3.0 %collective-permute-done.2.far = f32[8,1152]{1,0:T(8,128)S(1)} collective-permute-done((f32[8,1152]{1,0:T(8,128)S(1)}, f32[8,1152]{1,0:T(8,128)S(1)}, u32[]{:S(2)}, u32[]{:S(2)}) %collective-permute-start.2) | collective-permute-done | bytes 36896 | tf_op jit(solution)/shard_map/ppermute | solution.py:489
  10.2 0.0 collective-permute-done.partner
  10.2 1.4 %correlate.3 = (bf16[264,512]{1,0:T(8,128)(2,1)S(1)}, bf16[264,4096]{1,0:T(8,128)(2,1)S(1)}) custom-call(bf16[128,1024]{1,0:T(8,128)(2,1)S(1)} %get-tuple-element.29.own, bf16[128,1024]{1,0:T(8,128)(2,1)S(1)} %collective-permute-done.partner, f32[8,1152]{1,0:T(8,128)S(1)} %collective-permute-done.1.near, f32[8,1152]{1,0:T(8,128)S(1)} %collective-permute-done.2.far, ...), custom_call_target="tpu_custom_call" | custom-call | flops 1107296256 | bytes 2097152 | tf_op jit(solution)/shard_map/correlate/pallas_call | solution.py:508
  11.6 2.3 %collective-permute-start.3 = (bf16[264,512]{1,0:T(8,128)(2,1)S(1)}, bf16[264,512]{1,0:T(8,128)(2,1)S(1)}, u32[]{:S(2)}, u32[]{:S(2)}) collective-permute-start(bf16[264,512]{1,0:T(8,128)(2,1)S(1)} %get-tuple-element.34), channel_id=1, source_target_pairs={{0,1},{1,0},{2,3},{3,2},{4,5},{5,4},{6,7},{7,6},{8,9},{9,8},{10,11... | collective-permute-start | bytes 811016 | tf_op jit(solution)/shard_map/ppermute | solution.py:538
  13.8 0.0 copy-start.1
  13.8 6.2 %correlate.4 = (bf16[264,512]{1,0:T(8,128)(2,1)S(1)}, bf16[264,512]{1,0:T(8,128)(2,1)S(1)}, bf16[4096,1024]{1,0:T(8,128)(2,1)S(1)}) custom-call(bf16[264,4096]{1,0:T(8,128)(2,1)S(1)} %get-tuple-element.33.lagged, s32[1024,8]{1,0:T(8,128)S(1)} %get-tuple-element.37.columns, s32[1,4096]{1,0:T(1,128)S(1)} %get-tuple-element.32.bits, bf16[4,1024,4096]{2,1,0:T(8,128)(2,1)} %weights.5), custom_call_target="tpu_custom_call" | custom-call | flops 2214592512 | bytes 8388608 | tf_op jit(solution)/shard_map/correlate/pallas_call | solution.py:521
  20.0 0.1 collective-permute-start.4
  20.1 0.7 %collective-permute-done.3.theirs = bf16[264,512]{1,0:T(8,128)(2,1)S(1)} collective-permute-done((bf16[264,512]{1,0:T(8,128)(2,1)S(1)}, bf16[264,512]{1,0:T(8,128)(2,1)S(1)}, u32[]{:S(2)}, u32[]{:S(2)}) %collective-permute-start.3) | collective-permute-done | bytes 270368 | tf_op jit(solution)/shard_map/ppermute | solution.py:538
  20.9 0.1 pair.1
  20.9 2.7 %collective-permute-start.5 = (bf16[264,512]{1,0:T(8,128)(2,1)S(1)}, bf16[264,512]{1,0:T(8,128)(2,1)S(1)}, u32[]{:S(2)}, u32[]{:S(2)}) collective-permute-start(bf16[264,512]{1,0:T(8,128)(2,1)S(1)} %pair.1), channel_id=1, source_target_pairs={{0,2},{1,3},{2,0},{3,1},{4,6},{5,7},{6,4},{7,5},{8,10},{9,11},{10,... | collective-permute-start | bytes 811016 | tf_op jit(solution)/shard_map/ppermute | solution.py:538
  23.6 0.0 collective-permute-start.6
  23.6 1.2 %collective-permute-done.6.partner_clocks = f32[8,128]{1,0:T(8,128)S(1)} collective-permute-done((f32[8,128]{1,0:T(8,128)S(1)}, f32[8,128]{1,0:T(8,128)S(1)}, u32[]{:S(2)}, u32[]{:S(2)}) %collective-permute-start.6) | collective-permute-done | bytes 4128 | tf_op jit(solution)/shard_map/ppermute | solution.py:486
  24.8 0.0 copy-done.1
  24.8 1.4 %factors.1 = (f32[5,264,512]{2,1,0:T(8,128)S(1)}, f32[264,8]{1,0:T(8,128)S(1)}) custom-call(f32[8,128]{1,0:T(8,128)S(1)} %get-tuple-element.40.clocks, f32[8,128]{1,0:T(8,128)S(1)} %collective-permute-done.6.partner_clocks, f32[8,1152]{1,0:T(8,128)S(1)} %collective-permute-done.1.near, f32[8,1152]{1,0:T(8,128)S(1)} %collective-permute-done.2.far, ...), custom_call_target="tpu_custom_call" | custom-call | flops 10813440 | bytes 2703360 | tf_op jit(solution)/shard_map/factors/pallas_call | solution.py:541
  26.1 0.0 copy-start
  26.2 3.7 %correlate.5 = (bf16[264,512]{1,0:T(8,128)(2,1)S(1)}, bf16[4096,512]{1,0:T(8,128)(2,1)S(1)}) custom-call(bf16[264,4096]{1,0:T(8,128)(2,1)S(1)} %get-tuple-element.33.lagged, s32[1024,8]{1,0:T(8,128)S(1)} %get-tuple-element.37.columns, s32[1,4096]{1,0:T(1,128)S(1)} %get-tuple-element.32.bits, bf16[4,1024,4096]{2,1,0:T(8,128)(2,1)} %weights.5), custom_call_target="tpu_custom_call" | custom-call | flops 1107296256 | bytes 4194304 | tf_op jit(solution)/shard_map/correlate/pallas_call | solution.py:521
  29.9 4.3 %collective-permute-done.4.direct = bf16[264,512]{1,0:T(8,128)(2,1)S(1)} collective-permute-done((bf16[264,512]{1,0:T(8,128)(2,1)S(1)}, bf16[264,512]{1,0:T(8,128)(2,1)S(1)}, u32[]{:S(2)}, u32[]{:S(2)}) %collective-permute-start.4) | collective-permute-done | bytes 270368 | tf_op jit(solution)/shard_map/ppermute | solution.py:538
  34.2 0.0 collective-permute-done.5.paired
  34.2 0.0 copy-done
  34.2 0.4 recurrence.1
  34.6 1.5 %collective-permute-start.9 = (bf16[264,512]{1,0:T(8,128)(2,1)S(1)}, bf16[264,512]{1,0:T(8,128)(2,1)S(1)}, u32[]{:S(2)}, u32[]{:S(2)}) collective-permute-start(bf16[264,512]{1,0:T(8,128)(2,1)S(1)} %get-tuple-element.45.refs_0_), channel_id=1, source_target_pairs={{0,2},{1,3},{2,0},{3,1},{4,6},{5,7},{6,4},{7,5},{8,10},{9,11},{10,... | collective-permute-start | bytes 811016 | tf_op jit(solution)/shard_map/ppermute | solution.py:538
  36.2 4.1 %collective-permute-start.12 = (bf16[264,512]{1,0:T(8,128)(2,1)S(1)}, bf16[264,512]{1,0:T(8,128)(2,1)S(1)}, u32[]{:S(2)}, u32[]{:S(2)}) collective-permute-start(bf16[264,512]{1,0:T(8,128)(2,1)S(1)} %get-tuple-element.45.refs_0_), channel_id=1, source_target_pairs={{0,1},{1,0},{2,3},{3,2},{4,5},{5,4},{6,7},{7,6},{8,9},{9,8},{10,11... | collective-permute-start | bytes 811016 | tf_op jit(solution)/shard_map/ppermute | solution.py:538
  40.2 1.5 %collective-permute-start.7 = (f32[8,512]{1,0:T(8,128)S(1)}, f32[8,512]{1,0:T(8,128)S(1)}, u32[]{:S(2)}, u32[]{:S(2)}) collective-permute-start(f32[8,512]{1,0:T(8,128)S(1)} %get-tuple-element.42), channel_id=1, source_target_pairs={{8,0},{12,4},{9,1},{13,5},{10,2},{14,6},{11,3},{15,7},{24,16},{28,... | collective-permute-start | bytes 49160 | tf_op jit(solution)/shard_map/ppermute | solution.py:638
  41.7 4.2 %collective-permute-done.7.incoming.refs_2_ = f32[8,512]{1,0:T(8,128)S(1)} collective-permute-done((f32[8,512]{1,0:T(8,128)S(1)}, f32[8,512]{1,0:T(8,128)S(1)}, u32[]{:S(2)}, u32[]{:S(2)}) %collective-permute-start.7) | collective-permute-done | bytes 16416 | tf_op jit(solution)/shard_map/ppermute | solution.py:638
  45.9 0.0 collective-permute-start.13
  45.9 0.6 %reach.1 = (f32[264,512]{1,0:T(8,128)S(1)}, f32[4,264,512]{2,1,0:T(8,128)S(1)}) custom-call(f32[264,8]{1,0:T(8,128)S(1)} %get-tuple-element.46.columns, f32[1,4096]{1,0:T(1,128)S(1)} %bitcast.8, f32[1,4096]{1,0:T(1,128)S(1)} %bitcast.6), custom_call_target="tpu_custom_call" | custom-call | flops 5406720 | bytes 2703360 | tf_op jit(solution)/shard_map/reach/pallas_call | solution.py:556
  46.5 0.3 finish.1
  46.8 0.1 collective-permute-start.8
  46.9 0.2 collective-permute-start.11
  47.0 2.0 %collective-permute-done.9.refs_0_ = bf16[264,512]{1,0:T(8,128)(2,1)S(1)} collective-permute-done((bf16[264,512]{1,0:T(8,128)(2,1)S(1)}, bf16[264,512]{1,0:T(8,128)(2,1)S(1)}, u32[]{:S(2)}, u32[]{:S(2)}) %collective-permute-start.9) | collective-permute-done | bytes 270368 | tf_op jit(solution)/shard_map/ppermute | solution.py:538
  49.0 0.0 collective-permute-start.10
  49.0 0.5 collective-permute-done.13.refs_3_
  49.6 0.0 collective-permute-done.12.refs_1_
  49.6 2.4 %reconstruct.3.refs_4_ = f32[1024,256]{1,0:T(8,128)S(1)} custom-call(bf16[264,512]{1,0:T(8,128)(2,1)S(1)} %get-tuple-element.45.refs_0_, bf16[264,512]{1,0:T(8,128)(2,1)S(1)} %collective-permute-done.12.refs_1_, f32[8,512]{1,0:T(8,128)S(1)} %collective-permute-done.7.incoming.refs_2_, f32[8,512]{1,0:T(8,128)S(1)} %collective-permute-done.13.refs_3_, ...), custom_call_target="tpu_custom_call" | custom-call | flops 2214592512 | bytes 4194304 | tf_op jit(solution)/shard_map/reconstruct/pallas_call | solution.py:607
  52.0 0.0 collective-permute-done.11.refs_1_
  52.0 1.8 %collective-permute-start.14 = (f32[8,512]{1,0:T(8,128)S(1)}, f32[8,512]{1,0:T(8,128)S(1)}, u32[]{:S(2)}, u32[]{:S(2)}) collective-permute-start(f32[8,512]{1,0:T(8,128)S(1)} %collective-permute-done.11.refs_1_), channel_id=1, source_target_pairs={{0,1},{1,0},{2,3},{3,2},{4,5},{5,4},{6,7},{7,6},{8,9},{9,8},{10,11... | collective-permute-start | bytes 49160 | tf_op jit(solution)/shard_map/ppermute | solution.py:538
  53.8 1.3 %reconstruct.4.refs_4_ = f32[1024,256]{1,0:T(8,128)S(1)} custom-call(bf16[264,512]{1,0:T(8,128)(2,1)S(1)} %collective-permute-done.9.refs_0_, f32[8,512]{1,0:T(8,128)S(1)} %collective-permute-done.11.refs_1_, bf16[4096,1024]{1,0:T(8,128)(2,1)S(1)} %get-tuple-element.51.refs_5_.refs_2_, f32[4,264,512]{2,1,0:T(8,128)S(1)} %get-tuple-element.52.refs_6_.refs_3_, ...), custom_call_target="tpu_custom_call" | custom-call | flops 1107296256 | bytes 2097152 | tf_op jit(solution)/shard_map/reconstruct/pallas_call | solution.py:607
  55.1 1.7 %collective-permute-done.14.refs_1_ = f32[8,512]{1,0:T(8,128)S(1)} collective-permute-done((f32[8,512]{1,0:T(8,128)S(1)}, f32[8,512]{1,0:T(8,128)S(1)}, u32[]{:S(2)}, u32[]{:S(2)}) %collective-permute-start.14) | collective-permute-done | bytes 16416 | tf_op jit(solution)/shard_map/ppermute | solution.py:538
  56.7 0.0 collective-permute-done.10.refs_0_
  56.7 1.3 %reconstruct.5 = (f32[1024,128]{1,0:T(8,128)S(1)}, bf16[1024,128]{1,0:T(8,128)(2,1)S(1)}) custom-call(bf16[264,512]{1,0:T(8,128)(2,1)S(1)} %collective-permute-done.10.refs_0_, f32[8,512]{1,0:T(8,128)S(1)} %collective-permute-done.14.refs_1_, bf16[4096,512]{1,0:T(8,128)(2,1)S(1)} %mask.1.kernels.refs_2_, ...), custom_call_target="tpu_custom_call" | custom-call | flops 1107296256 | bytes 2097152 | tf_op jit(solution)/shard_map/reconstruct/pallas_call | solution.py:607
  58.1 0.1 collective-permute-start.15
  58.1 0.0 collective-permute-done.8
  58.2 0.8 %maximum_select_fusion = f32[1024,128]{1,0:T(8,128)} fusion(f32[512,128]{1,0:T(8,128)S(1)} %get-tuple-element.49, f32[512,128]{1,0:T(8,128)S(1)} %collective-permute-done.8, pred[]{:T(512)S(6)} %eq.5), kind=kLoop, calls=%fused_computation | loop fusion | flops 393216 | bytes 1048577 | tf_op jit(solution)/shard_map/jit(_where)/select_n | solution.py:650
  59.0 0.7 %collective-permute-done.15 = bf16[1024,128]{1,0:T(8,128)(2,1)S(1)} collective-permute-done((bf16[1024,128]{1,0:T(8,128)(2,1)S(1)}, bf16[1024,128]{1,0:T(8,128)(2,1)S(1)}, u32[]{:S(2)}, u32[]{:S(2)}) %collective-permute-start.15) | collective-permute-done | bytes 262176 | tf_op jit(solution)/shard_map/ppermute | solution.py:649
  59.7 0.8 %add_convert_fusion = bf16[1024,128]{1,0:T(8,128)(2,1)} fusion(f32[1024,128]{1,0:T(8,128)S(1)} %get-tuple-element.54, bf16[1024,128]{1,0:T(8,128)(2,1)S(1)} %collective-permute-done.15), kind=kLoop, calls=%fused_computation.1 | loop fusion | flops 393216 | bytes 1048576 | tf_op jit(solution)/shard_map/convert_element_type | solution.py:653
Async XLA Ops:
  2.0 8.2 %collective-permute-start = (bf16[128,1024]{1,0:T(8,128)(2,1)S(1)}, bf16[128,1024]{1,0:T(8,128)(2,1)S(1)}, u32[]{:S(2)}, u32[]{:S(2)}) collective-permute-start(bf16[128,1024]{1,0:T(8,128)(2,1)S(1)} %get-tuple-element.29.own), channel_id=1, source_target_pairs={{0,4},{4,0},{8,12},{12,8},{1,5},{5,1},{9,13},{13,9},{2,6},{6,2},{1... | collective-permute-start | bytes 786440 | tf_op jit(solution)/shard_map/ppermute | solution.py:487
  2.5 4.6 %collective-permute-start.1 = (f32[8,1152]{1,0:T(8,128)S(1)}, f32[8,1152]{1,0:T(8,128)S(1)}, u32[]{:S(2)}, u32[]{:S(2)}) collective-permute-start(f32[8,1152]{1,0:T(8,128)S(1)} %get-tuple-element.30), channel_id=1, source_target_pairs={{4,8},{8,4},{5,9},{9,5},{6,10},{10,6},{7,11},{11,7},{20,24},{24,20... | collective-permute-start | bytes 110600 | tf_op jit(solution)/shard_map/ppermute | solution.py:488
  3.2 7.0 %collective-permute-start.2 = (f32[8,1152]{1,0:T(8,128)S(1)}, f32[8,1152]{1,0:T(8,128)S(1)}, u32[]{:S(2)}, u32[]{:S(2)}) collective-permute-start(f32[8,1152]{1,0:T(8,128)S(1)} %get-tuple-element.30), channel_id=1, source_target_pairs={{4,12},{8,0},{5,13},{9,1},{6,14},{10,2},{7,15},{11,3},{20,28},{24,... | collective-permute-start | bytes 110600 | tf_op jit(solution)/shard_map/ppermute | solution.py:489
  11.6 9.3 %collective-permute-start.3 = (bf16[264,512]{1,0:T(8,128)(2,1)S(1)}, bf16[264,512]{1,0:T(8,128)(2,1)S(1)}, u32[]{:S(2)}, u32[]{:S(2)}) collective-permute-start(bf16[264,512]{1,0:T(8,128)(2,1)S(1)} %get-tuple-element.34), channel_id=1, source_target_pairs={{0,1},{1,0},{2,3},{3,2},{4,5},{5,4},{6,7},{7,6},{8,9},{9,8},{10,11... | collective-permute-start | bytes 811016 | tf_op jit(solution)/shard_map/ppermute | solution.py:538
  13.8 11.0 %copy-start.1 = (f32[4096]{0:T(1024)S(1)}, f32[4096]{0:T(1024)}, u32[]{:S(2)}) copy-start(f32[4096]{0:T(1024)} %param.12) | copy-start | bytes 49156
  20.0 14.2 %collective-permute-start.4 = (bf16[264,512]{1,0:T(8,128)(2,1)S(1)}, bf16[264,512]{1,0:T(8,128)(2,1)S(1)}, u32[]{:S(2)}, u32[]{:S(2)}) collective-permute-start(bf16[264,512]{1,0:T(8,128)(2,1)S(1)} %get-tuple-element.39), channel_id=1, source_target_pairs={{0,1},{1,0},{2,3},{3,2},{4,5},{5,4},{6,7},{7,6},{8,9},{9,8},{10,11... | collective-permute-start | bytes 811016 | tf_op jit(solution)/shard_map/ppermute | solution.py:538
  20.9 13.3 %collective-permute-start.5 = (bf16[264,512]{1,0:T(8,128)(2,1)S(1)}, bf16[264,512]{1,0:T(8,128)(2,1)S(1)}, u32[]{:S(2)}, u32[]{:S(2)}) collective-permute-start(bf16[264,512]{1,0:T(8,128)(2,1)S(1)} %pair.1), channel_id=1, source_target_pairs={{0,2},{1,3},{2,0},{3,1},{4,6},{5,7},{6,4},{7,5},{8,10},{9,11},{10,... | collective-permute-start | bytes 811016 | tf_op jit(solution)/shard_map/ppermute | solution.py:538
  23.6 1.2 %collective-permute-start.6 = (f32[8,128]{1,0:T(8,128)S(1)}, f32[8,128]{1,0:T(8,128)S(1)}, u32[]{:S(2)}, u32[]{:S(2)}) collective-permute-start(f32[8,128]{1,0:T(8,128)S(1)} %get-tuple-element.40.clocks), channel_id=1, source_target_pairs={{0,4},{4,0},{8,12},{12,8},{1,5},{5,1},{9,13},{13,9},{2,6},{6,2},{1... | collective-permute-start | bytes 12296 | tf_op jit(solution)/shard_map/ppermute | solution.py:486
  26.1 8.1 %copy-start = (f32[4096]{0:T(1024)S(1)}, f32[4096]{0:T(1024)}, u32[]{:S(2)}) copy-start(f32[4096]{0:T(1024)} %param.15) | copy-start | bytes 49156
  34.6 14.4 %collective-permute-start.9 = (bf16[264,512]{1,0:T(8,128)(2,1)S(1)}, bf16[264,512]{1,0:T(8,128)(2,1)S(1)}, u32[]{:S(2)}, u32[]{:S(2)}) collective-permute-start(bf16[264,512]{1,0:T(8,128)(2,1)S(1)} %get-tuple-element.45.refs_0_), channel_id=1, source_target_pairs={{0,2},{1,3},{2,0},{3,1},{4,6},{5,7},{6,4},{7,5},{8,10},{9,11},{10,... | collective-permute-start | bytes 811016 | tf_op jit(solution)/shard_map/ppermute | solution.py:538
  36.2 13.4 %collective-permute-start.12 = (bf16[264,512]{1,0:T(8,128)(2,1)S(1)}, bf16[264,512]{1,0:T(8,128)(2,1)S(1)}, u32[]{:S(2)}, u32[]{:S(2)}) collective-permute-start(bf16[264,512]{1,0:T(8,128)(2,1)S(1)} %get-tuple-element.45.refs_0_), channel_id=1, source_target_pairs={{0,1},{1,0},{2,3},{3,2},{4,5},{5,4},{6,7},{7,6},{8,9},{9,8},{10,11... | collective-permute-start | bytes 811016 | tf_op jit(solution)/shard_map/ppermute | solution.py:538
  40.2 5.6 %collective-permute-start.7 = (f32[8,512]{1,0:T(8,128)S(1)}, f32[8,512]{1,0:T(8,128)S(1)}, u32[]{:S(2)}, u32[]{:S(2)}) collective-permute-start(f32[8,512]{1,0:T(8,128)S(1)} %get-tuple-element.42), channel_id=1, source_target_pairs={{8,0},{12,4},{9,1},{13,5},{10,2},{14,6},{11,3},{15,7},{24,16},{28,... | collective-permute-start | bytes 49160 | tf_op jit(solution)/shard_map/ppermute | solution.py:638
  45.9 3.7 %collective-permute-start.13 = (f32[8,512]{1,0:T(8,128)S(1)}, f32[8,512]{1,0:T(8,128)S(1)}, u32[]{:S(2)}, u32[]{:S(2)}) collective-permute-start(f32[8,512]{1,0:T(8,128)S(1)} %collective-permute-done.7.incoming.refs_2_), channel_id=1, source_target_pairs={{0,1},{1,0},{2,3},{3,2},{4,5},{5,4},{6,7},{7,6},{8,9},{9,8},{10,11... | collective-permute-start | bytes 49160 | tf_op jit(solution)/shard_map/ppermute | solution.py:538
  46.8 11.4 %collective-permute-start.8 = (f32[512,128]{1,0:T(8,128)S(1)}, f32[512,128]{1,0:T(8,128)S(1)}, u32[]{:S(2)}, u32[]{:S(2)}) collective-permute-start(f32[512,128]{1,0:T(8,128)S(1)} %get-tuple-element.48), channel_id=1, source_target_pairs={{0,4},{4,0},{8,12},{12,8},{1,5},{5,1},{9,13},{13,9},{2,6},{6,2},{1... | collective-permute-start | bytes 786440 | tf_op jit(solution)/shard_map/ppermute | solution.py:642
  46.9 5.1 %collective-permute-start.11 = (f32[8,512]{1,0:T(8,128)S(1)}, f32[8,512]{1,0:T(8,128)S(1)}, u32[]{:S(2)}, u32[]{:S(2)}) collective-permute-start(f32[8,512]{1,0:T(8,128)S(1)} %collective-permute-done.7.incoming.refs_2_), channel_id=1, source_target_pairs={{0,2},{1,3},{2,0},{3,1},{4,6},{5,7},{6,4},{7,5},{8,10},{9,11},{10,... | collective-permute-start | bytes 49160 | tf_op jit(solution)/shard_map/ppermute | solution.py:538
  49.0 7.7 %collective-permute-start.10 = (bf16[264,512]{1,0:T(8,128)(2,1)S(1)}, bf16[264,512]{1,0:T(8,128)(2,1)S(1)}, u32[]{:S(2)}, u32[]{:S(2)}) collective-permute-start(bf16[264,512]{1,0:T(8,128)(2,1)S(1)} %collective-permute-done.9.refs_0_), channel_id=1, source_target_pairs={{0,1},{1,0},{2,3},{3,2},{4,5},{5,4},{6,7},{7,6},{8,9},{9,8},{10,11... | collective-permute-start | bytes 811016 | tf_op jit(solution)/shard_map/ppermute | solution.py:538
  52.0 4.7 %collective-permute-start.14 = (f32[8,512]{1,0:T(8,128)S(1)}, f32[8,512]{1,0:T(8,128)S(1)}, u32[]{:S(2)}, u32[]{:S(2)}) collective-permute-start(f32[8,512]{1,0:T(8,128)S(1)} %collective-permute-done.11.refs_1_), channel_id=1, source_target_pairs={{0,1},{1,0},{2,3},{3,2},{4,5},{5,4},{6,7},{7,6},{8,9},{9,8},{10,11... | collective-permute-start | bytes 49160 | tf_op jit(solution)/shard_map/ppermute | solution.py:538
  58.1 1.6 %collective-permute-start.15 = (bf16[1024,128]{1,0:T(8,128)(2,1)S(1)}, bf16[1024,128]{1,0:T(8,128)(2,1)S(1)}, u32[]{:S(2)}, u32[]{:S(2)}) collective-permute-start(bf16[1024,128]{1,0:T(8,128)(2,1)S(1)} %get-tuple-element.55), channel_id=1, source_target_pairs={{0,4},{4,0},{8,12},{12,8},{1,5},{5,1},{9,13},{13,9},{2,6},{6,2},{1... | collective-permute-start | bytes 786440 | tf_op jit(solution)/shard_map/ppermute | solution.py:649
